TPU v7x, 512 devices: a whole 4x8x8 slice. The times are simulated.
512 devices in a mesh: dp: 4 (over x), gx: 8 (over y), gy: 16 (over z, core).
Axes of the slice: x: 4, y: 8, z: 8, core: 2. Of those that a mesh axis runs over, the one named last changes fastest.
Arguments:
- fields: float32 [4, 20, 32, 32, 512], P('dp', None, 'gx', 'gy'), may hold values from -6 to 6
- cotangent: float32 [4, 20, 32, 32, 512], P('dp', None, 'gx', 'gy'), may hold values from -6 to 6
- spectral: float32 [2, 72, 16, 12, 20, 20], P(None, 'gx', 'gy'), may hold values from -6 to 6
- bypass: float32 [20, 20], replicated, may hold values from -1.25 to 1.25
Outputs:
- outputs: float32 [4, 20, 32, 32, 512], P('dp', None, 'gx', 'gy')
- field_grad: float32 [4, 20, 32, 32, 512], P('dp', None, 'gx', 'gy')
- spectral_grad: float32 [2, 72, 16, 12, 20, 20], P(None, 'gx', 'gy')
All inputs are finite; a program needn't handle non-finite values.
Results may differ from a plain program's by a relative error of at most 0.00011.
Values sent between devices are 32-bit elements; how exact they have to be, the bound alone decides.
No kernel may reach another device: no remote copies, remote signals or barrier semaphores. Data moves between devices by JAX's collectives and lax.ppermute only.
A program may use at most 64 MiB of HBM per device.

v0:
```python
import functools
import math

import jax
import jax.numpy as jnp
import numpy as np
from jax import lax
from jax.experimental import pallas as pl
from jax.experimental.pallas import tpu as pltpu
from jax.sharding import PartitionSpec as P

C = 20
NX, NY, NR = 4, 2, 512
GX, GY = 8, 16
S6 = 6
KX = 12
F32 = jnp.float32
EXACT = lax.Precision.HIGHEST
VMEM = pltpu.VMEM
INV_CELLS = 1.0 / (32 * 32 * 512)
INTERPRET = False


def freq(i, n):
    return i if i < n // 2 else i - n


def z_table():
    r = np.arange(NR)
    z, t = r // 8, r % 8
    out = np.zeros((S6, 2, GY, NR))
    for s in range(S6):
        for j in range(GY):
            m = 6 * j + s
            kz, kt = freq(m // 8, 12), freq(m % 8, 8)
            w = (kz * z * 8 + kt * t * 64) % 512
            ang = w * (2.0 * math.pi / 512)
            out[s, 0, j] = np.cos(ang)
            out[s, 1, j] = -np.sin(ang)
    return out.reshape(S6 * 2 * GY, NR).astype(np.float32)


def rot(k, n, sign):
    ang = ((k * n) % 32) * (2.0 * math.pi / 32)
    c, s = math.cos(ang), sign * math.sin(ang)
    return np.array([[c, -s], [s, c]])


def y_forward():
    out = np.zeros((2, 3, 8, NY, 2, GY))
    for t in range(3):
        for h in range(4):
            for yl in range(NY):
                for g in range(GY):
                    out[:, t, h, yl, :, g] = rot(freq(3 * h + t, 12), 2 * g + yl, -1)
    return out.reshape(48, 64).astype(np.float32)


def y_inverse():
    out = np.zeros((NY, 2, GY, 2, 3, 4))
    for t in range(3):
        for h in range(4):
            for yl in range(NY):
                for g in range(GY):
                    out[yl, :, g, :, t, h] = rot(freq(3 * h + t, 12), 2 * g + yl, 1)
    return out.reshape(64, 24).astype(np.float32)


def x_forward(scale):
    out = np.zeros((2, 16, GX, NX, 2))
    for k in range(KX):
        for g in range(GX):
            for xl in range(NX):
                out[:, k, g, xl, :] = rot(freq(k, 12), 4 * g + xl, -1)
    return (out * scale).reshape(32, 64).astype(np.float32)


def x_inverse(scale):
    out = np.zeros((GX, NX, 2, 2, 16))
    for k in range(KX):
        for g in range(GX):
            for xl in range(NX):
                out[g, xl, :, :, k] = rot(freq(k, 12), 4 * g + xl, 1)
    return (out * scale).reshape(64, 32).astype(np.float32)


def call(body, outs, *args, scratch=(), smem=(), flops=10**7, name=None):
    specs = [
        pl.BlockSpec(memory_space=pltpu.SMEM if i in smem else VMEM) for i in range(len(args))
    ]
    shapes = [jax.ShapeDtypeStruct(s, F32) for s in outs]
    nbytes = 4 * sum(math.prod(s) for s in outs) + sum(a.size * a.dtype.itemsize for a in args)
    got = pl.pallas_call(
        body,
        out_shape=shapes,
        in_specs=specs,
        out_specs=[pl.BlockSpec(memory_space=VMEM)] * len(outs),
        scratch_shapes=list(scratch),
        cost_estimate=pl.CostEstimate(flops=flops, bytes_accessed=nbytes, transcendentals=0),
        interpret=INTERPRET,
        name=name,
    )(*args)
    return got if len(outs) > 1 else got[0]


def dot(a, b):
    return jnp.dot(a, b, precision=EXACT, preferred_element_type=F32)


def lanes(rows):
    return lax.broadcasted_iota(jnp.int32, (rows, 128), 1)


def load_cells(ref, x, y):
    return jnp.concatenate(
        [ref[pl.ds(x * 8 + tile * 2 + y, C, stride=32), :] for tile in range(4)], axis=1
    )


def store_cells(ref, x, y, value):
    for tile in range(4):
        ref[pl.ds(x * 8 + tile * 2 + y, C, stride=32), :] = value[:, tile * 128 : tile * 128 + 128]


def emit_depth(table_ref, stage_ref, send_ref):
    modes = lax.dot_general(
        table_ref[...], stage_ref[...], (((1,), (1,)), ((), ())), precision=EXACT, preferred_element_type=F32
    )
    lane = lanes(GY)
    for y in range(NY):
        for x in range(NX):
            for part in range(2):
                total = jnp.zeros((GY, 128), F32)
                for s in range(S6):
                    at = (s * 2 + part) * GY
                    piece = modes[at : at + GY, y * 128 : y * 128 + 128]
                    shift = (20 * s - 32 * x) % 128
                    if shift:
                        piece = pltpu.roll(piece, shift, axis=1)
                    total = jnp.where((lane >= 20 * s) & (lane < 20 * s + 20), piece, total)
                send_ref[pl.ds(x * 4 + y * 2 + part, GY, stride=16), :] = total


def gather_depth(recv_ref, table_ref, modes_ref):
    lane = lanes(GY)
    for y in range(NY):
        for part in range(2):
            pieces = [recv_ref[pl.ds(x * 4 + y * 2 + part, GY, stride=16), :] for x in range(NX)]
            for s in range(S6):
                total = jnp.zeros((GY, 128), F32)
                for x in range(NX):
                    shift = (32 * x - 20 * s) % 128
                    piece = pltpu.roll(pieces[x], shift, axis=1) if shift else pieces[x]
                    total = jnp.where((lane >= 32 * x) & (lane < 32 * x + 20), piece, total)
                at = (s * 2 + part) * GY
                modes_ref[at : at + GY, y * 128 : y * 128 + 128] = total
    return lax.dot_general(
        modes_ref[...], table_ref[...], (((0,), (0,)), ((), ())), precision=EXACT, preferred_element_type=F32
    )


def depth_forward(fields_ref, table_ref, send_ref, stage_ref):
    stage_ref[...] = jnp.zeros_like(stage_ref)
    for y in range(NY):
        for x in range(NX):
            at = (y * NX + x) * 32
            stage_ref[at : at + C, :] = load_cells(fields_ref, x, y)
    emit_depth(table_ref, stage_ref, send_ref)


def bypass_fields(fields_ref, map_ref, out_ref):
    for y in range(NY):
        for x in range(NX):
            at = (y * NX + x) * 32
            out_ref[at : at + C, :] = dot(map_ref[...], load_cells(fields_ref, x, y))
            out_ref[at + C : at + 32, :] = jnp.zeros((32 - C, NR), F32)


def bypass_signal(signal_ref, map_ref, out_ref):
    for cell in range(8):
        at = cell * 32
        out_ref[at : at + C, :] = dot(map_ref[...], signal_ref[at : at + C, :])
        out_ref[at + C : at + 32, :] = jnp.zeros((32 - C, NR), F32)


def y_spectrum(recv_ref, table_ref, send_ref):
    columns = []
    for x in range(NX):
        columns.append(
            jnp.concatenate(
                [recv_ref[pl.ds(x * 4 + row, GY, stride=16), :] for row in range(4)], axis=0
            )
        )
    turned = dot(table_ref[...], jnp.concatenate(columns, axis=1))
    for x in range(NX):
        for part in range(2):
            row = x * 2 + part
            t0, t1, t2 = [
                turned[part * 24 + t * 8 : part * 24 + t * 8 + 8, x * 128 : x * 128 + 128] for t in range(3)
            ]
            send_ref[pl.ds(row, 4, stride=32), :] = t0[:4]
            send_ref[pl.ds(8 + row, 4, stride=32), :] = t1[:4]
            send_ref[pl.ds(16 + row, 4, stride=32), :] = t2[:4]
            send_ref[pl.ds(24 + row, 4, stride=32), :] = pltpu.roll(t1, 68, axis=1)[:4]


def y_cells(recv_ref, table_ref, send_ref, stage_ref):
    lane = lanes(4)
    for x in range(NX):
        for part in range(2):
            row = x * 2 + part
            t0, low, t2, high = [recv_ref[pl.ds(slot * 8 + row, 4, stride=32), :] for slot in range(4)]
            at = part * 12
            cut = slice(x * 128, x * 128 + 128)
            stage_ref[at : at + 4, cut] = t0
            stage_ref[at + 4 : at + 8, cut] = jnp.where(lane < 60, low, pltpu.roll(high, 60, axis=1))
            stage_ref[at + 8 : at + 12, cut] = t2
    cells = dot(table_ref[...], stage_ref[...])
    for x in range(NX):
        for row in range(4):
            send_ref[pl.ds(x * 4 + row, GY, stride=16), :] = cells[
                row * 16 : row * 16 + 16, x * 128 : x * 128 + 128
            ]


def x_spectrum(recv_ref, table_ref):
    found = []
    for tile in range(2):
        data = jnp.concatenate(
            [recv_ref[src * 16 + tile * 8 : src * 16 + tile * 8 + 8, :] for src in range(GX)], axis=0
        )
        found.append(dot(table_ref[...], data))
    return found


def slots(odd):
    for s in range(6):
        yield 0, s, s + 3 * odd
    for s in range(3):
        yield 1, s, s + 6 * (1 - odd)


def x_cells(mixed, table_ref, send_ref):
    for tile in range(2):
        cells = dot(table_ref[...], mixed[tile])
        for g in range(GX):
            send_ref[g * 16 + tile * 8 : g * 16 + tile * 8 + 8, :] = cells[g * 8 : g * 8 + 8, :]


def weight_row(pair, c):
    return pl.ds(pair * (KX * C) + c, KX, stride=C)


def x_mix(odd_ref, recv_ref, weight_ref, fwd_ref, inv_ref, send_ref, spec_ref, mixed_ref):
    odd = odd_ref[0]
    spectrum = x_spectrum(recv_ref, fwd_ref)
    for tile in range(2):
        spec_ref[tile * 32 : tile * 32 + 32, :] = spectrum[tile]
    mixed_ref[...] = jnp.zeros_like(mixed_ref)
    for tile, s, pair in slots(odd):
        real = spectrum[tile][:KX]
        imag = spectrum[tile][16 : 16 + KX]
        out_real = jnp.zeros((KX, C), F32)
        out_imag = jnp.zeros((KX, C), F32)
        for c in range(C):
            wr = weight_ref[weight_row(pair, c), :]
            wi = weight_ref[weight_row(9 + pair, c), :]
            at = 20 * s + c
            sr = real[:, at : at + 1]
            si = imag[:, at : at + 1]
            out_real = out_real + (sr * wr - si * wi)
            out_imag = out_imag + (sr * wi + si * wr)
        mixed_ref[tile * 32 : tile * 32 + KX, 20 * s : 20 * s + C] = out_real
        mixed_ref[tile * 32 + 16 : tile * 32 + 16 + KX, 20 * s : 20 * s + C] = out_imag
    x_cells([mixed_ref[:32, :], mixed_ref[32:, :]], inv_ref, send_ref)


def x_dual(recv_ref, spec_ref, fwd_ref, dual_ref, share_ref):
    spectrum = x_spectrum(recv_ref, fwd_ref)
    copies = share_ref.shape[0] // 128
    for tile in range(2):
        dual_ref[tile * 32 : tile * 32 + 32, :] = spectrum[tile]
        for n in range(copies):
            share_ref[n * 128 + tile * 32 : n * 128 + tile * 32 + 32, :] = spec_ref[
                tile * 32 : tile * 32 + 32, :
            ]
            share_ref[n * 128 + 64 + tile * 32 : n * 128 + 96 + tile * 32, :] = spectrum[tile]


def x_unmix(odd_ref, dual_ref, weight_ref, inv_ref, send_ref):
    odd = odd_ref[0]
    lane = lanes(KX)
    back = [[jnp.zeros((KX, 128), F32) for _ in range(2)] for _ in range(2)]
    for tile, s, pair in slots(odd):
        dr = dual_ref[tile * 32 : tile * 32 + KX, 20 * s : 20 * s + C]
        di = dual_ref[tile * 32 + 16 : tile * 32 + 16 + KX, 20 * s : 20 * s + C]
        for c in range(C):
            wr = weight_ref[weight_row(pair, c), :]
            wi = weight_ref[weight_row(9 + pair, c), :]
            real = jnp.sum(dr * wr + di * wi, axis=1, keepdims=True)
            imag = jnp.sum(di * wr - dr * wi, axis=1, keepdims=True)
            here = lane == 20 * s + c
            back[tile][0] = jnp.where(here, real, back[tile][0])
            back[tile][1] = jnp.where(here, imag, back[tile][1])
    gap = jnp.zeros((16 - KX, 128), F32)
    x_cells(
        [jnp.concatenate([re, gap, im, gap], axis=0) for re, im in back], inv_ref, send_ref
    )


def weight_grad(odd_ref, share_ref, grad_ref):
    odd = odd_ref[0]
    samples = share_ref.shape[0] // 128
    for tile, s, pair in slots(odd):
        spec, dual = [], []
        for n in range(samples):
            at = n * 128 + tile * 32
            spec.append([share_ref[at + p * 16 : at + p * 16 + KX, :] for p in range(2)])
            dual.append(
                [share_ref[at + 64 + p * 16 : at + 64 + p * 16 + KX, 20 * s : 20 * s + C] for p in range(2)]
            )
        for c in range(C):
            real = jnp.zeros((KX, C), F32)
            imag = jnp.zeros((KX, C), F32)
            at = 20 * s + c
            for n in range(samples):
                sr = spec[n][0][:, at : at + 1]
                si = spec[n][1][:, at : at + 1]
                dr, di = dual[n]
                real = real + (sr * dr + si * di)
                imag = imag + (sr * di - si * dr)
            grad_ref[weight_row(pair, c), :] = real
            grad_ref[weight_row(9 + pair, c), :] = imag


def activate(recv_ref, table_ref, bypass_ref, cotangent_ref, out_ref, signal_ref, send_ref, modes_ref):
    spectral = gather_depth(recv_ref, table_ref, modes_ref)
    k = math.sqrt(2.0 / math.pi)
    for y in range(NY):
        for x in range(NX):
            at = (y * NX + x) * 32
            v = spectral[at : at + C, :] + bypass_ref[at : at + C, :]
            cube = v * v * v
            th = jnp.tanh(k * (v + 0.044715 * cube))
            half = 0.5 * (1.0 + th)
            store_cells(out_ref, x, y, v * half)
            slope = half + 0.5 * v * (1.0 - th * th) * (k * (1.0 + 3 * 0.044715 * (v * v)))
            signal_ref[at : at + C, :] = slope * load_cells(cotangent_ref, x, y)
            signal_ref[at + C : at + 32, :] = jnp.zeros((32 - C, NR), F32)
    emit_depth(table_ref, signal_ref, send_ref)


def finish(recv_ref, table_ref, bypass_ref, out_ref, modes_ref):
    spectral = gather_depth(recv_ref, table_ref, modes_ref)
    for y in range(NY):
        for x in range(NX):
            at = (y * NX + x) * 32
            store_cells(out_ref, x, y, spectral[at : at + C, :] + bypass_ref[at : at + C, :])


def as_rows(a):
    return a.reshape(C * NX, NY, 4, 128).transpose(0, 2, 1, 3).reshape(640, 128)


def from_rows(a):
    return a.reshape(C * NX, 4, NY, 128).transpose(0, 2, 1, 3).reshape(1, C, NX, NY, NR)


CELLS = (256, NR)
SEND_Y = (GY * 16, 128)
SEND_X = (GX * 16, 128)


def stages(samples):
    tz, ay, by = z_table(), y_forward(), y_inverse()
    ax, bx = x_forward(1.0), x_inverse(INV_CELLS)
    ax_dual, bx_dual = x_forward(INV_CELLS), x_inverse(1.0)
    modes = [VMEM((192, 256), F32)]
    return dict(
        depth_forward=lambda f: call(depth_forward, [SEND_Y], f, tz, scratch=[VMEM(CELLS, F32)], name="depth_forward"),
        bypass_fields=lambda f, b: call(bypass_fields, [CELLS], f, b, name="bypass_fields"),
        bypass_signal=lambda f, b: call(bypass_signal, [CELLS], f, b, name="bypass_signal"),
        y_spectrum=lambda r: call(y_spectrum, [SEND_X], r, ay, name="y_spectrum"),
        y_cells=lambda r: call(y_cells, [SEND_Y], r, by, scratch=[VMEM((24, 512), F32)], name="y_cells"),
        x_mix=lambda o, r, w: call(
            x_mix, [SEND_X, (64, 128)], o, r, w, ax, bx, scratch=[VMEM((64, 128), F32)], smem=(0,), name="x_mix"
        ),
        x_dual=lambda r, s: call(x_dual, [(64, 128), (samples * 128, 128)], r, s, ax_dual, name="x_dual"),
        x_unmix=lambda o, d, w: call(x_unmix, [SEND_X], o, d, w, bx_dual, smem=(0,), name="x_unmix"),
        weight_grad=lambda o, s: call(weight_grad, [(2 * 9 * KX * C, C)], o, s, smem=(0,), name="weight_grad"),
        activate=lambda r, b, ct: call(
            activate, [(640, 128), CELLS, SEND_Y], r, tz, b, ct, scratch=modes, name="activate"
        ),
        finish=lambda r, b: call(finish, [(640, 128)], r, tz, b, scratch=modes, name="finish"),
    )


def swap(a, axis, n):
    rows = a.shape[0] // n
    return lax.all_to_all(
        a.reshape(n, rows, 128), axis, split_axis=0, concat_axis=0, tiled=True
    ).reshape(n * rows, 128)


def on_device(fields, cotangent, spectral, bypass):
    samples = lax.axis_size("dp")
    st = stages(samples)
    odd = (lax.axis_index("gx") % 2).astype(jnp.int32).reshape(1)
    rows = as_rows(fields)
    weights = spectral.reshape(2 * 9 * KX * C, C)
    to_y = functools.partial(swap, axis="gy", n=GY)
    to_x = functools.partial(swap, axis="gx", n=GX)
    direct = st["bypass_fields"](rows, bypass.T)
    arrived = to_x(st["y_spectrum"](to_y(st["depth_forward"](rows))))
    mixed, spec = st["x_mix"](odd, arrived, weights)
    arrived = to_y(st["y_cells"](to_x(mixed)))
    output, signal, sent = st["activate"](arrived, direct, as_rows(cotangent))
    direct = st["bypass_signal"](signal, bypass)
    arrived = to_x(st["y_spectrum"](to_y(sent)))
    dual, share = st["x_dual"](arrived, spec)
    shared = swap(share, "dp", samples)
    grad = st["weight_grad"](odd, shared)
    arrived = to_y(st["y_cells"](to_x(st["x_unmix"](odd, dual, weights))))
    field_grad = st["finish"](arrived, direct)
    return (from_rows(output), from_rows(field_grad), grad.reshape(spectral.shape))


def solution(mesh):
    cells = P("dp", None, "gx", "gy", None)
    modes = P(None, "gx", "gy", None, None, None)
    return jax.shard_map(
        on_device,
        mesh=mesh,
        in_specs=(cells, cells, modes, P()),
        out_specs=(cells, cells, modes),
        check_vma=False,
    )
```

profile of v0, /device:TPU:1, one launch (start us, length us, event | category | flops | bytes accessed | tf_op | source)
XLA Modules:
  0.0 188.8 jit_solution(1555783545535015102)
XLA Ops:
  0.6 0.0 copy-start.4
  0.6 2.8 %depth_forward.1 = f32[256,128]{1,0:T(8,128)} custom-call(f32[640,128]{1,0:T(8,128)} %bitcast.45, f32[192,512]{1,0:T(8,128)} %constant.33.clone.table_ref), custom_call_target="tpu_custom_call" | custom-call | flops 10000000 | bytes 851968 | tf_op jit(solution)/shard_map/depth_forward/pallas_call | solution.py:93
  3.5 20.8 %all_to_all.45 = f32[16,16,128]{2,1,0:T(8,128)} all-to-all(f32[16,16,128]{2,1,0:T(8,128)} %bitcast.52), channel_id=1, replica_groups=mesh['dp'=4,'gx'=8,'gy'=16] {'gy'}, dimensions={0} | all-to-all | bytes 262144 | tf_op jit(solution)/shard_map/all_to_all | solution.py:400
  24.3 1.9 y_spectrum.2
  26.2 6.8 %all-to-all-start.1 = ((f32[8,16,128]{2,1,0:T(8,128)}), f32[8,16,128]{2,1,0:T(8,128)S(1)}, u32[]{:S(2)}, u32[]{:S(2)}) async-start(f32[8,16,128]{2,1,0:T(8,128)} %bitcast.58), calls=%async_computation.1 | async-start | bytes 131072 | tf_op jit(solution)/shard_map/all_to_all | solution.py:400
  33.0 7.2 %all-to-all-done.1 = f32[8,16,128]{2,1,0:T(8,128)S(1)} async-done(((f32[8,16,128]{2,1,0:T(8,128)}), f32[8,16,128]{2,1,0:T(8,128)S(1)}, u32[]{:S(2)}, u32[]{:S(2)}) %all-to-all-start.1) | async-done | bytes 65568 | tf_op jit(solution)/shard_map/all_to_all | solution.py:400
  40.1 0.0 copy-start.3
  40.1 0.6 copy-done.3
  40.8 4.1 %x_mix.1 = (f32[128,128]{1,0:T(8,128)}, f32[64,128]{1,0:T(8,128)}) custom-call(s32[1]{0:T(128)} %bitcast.odd_ref, f32[128,128]{1,0:T(8,128)} %bitcast.57, f32[4320,20]{1,0:T(8,128)} %bitcast.42, f32[32,64]{1,0:T(8,128)} %constant.35.clone.fwd_ref, f32[64,32]{1,0:T(8,128)} %constant.36.clone.inv_ref), custom_call_target="tpu_custom_call" | custom-call | flops 10000000 | bytes 525828 | tf_op jit(solution)/shard_map/x_mix/pallas_call | solution.py:93
  44.9 11.2 %all_to_all.46 = f32[8,16,128]{2,1,0:T(8,128)} all-to-all(f32[8,16,128]{2,1,0:T(8,128)} %bitcast.65), channel_id=1, replica_groups=mesh['dp'=4,'gx'=8,'gy'=16] {'gx'}, dimensions={0} | all-to-all | bytes 131072 | tf_op jit(solution)/shard_map/all_to_all | solution.py:400
  56.1 1.8 y_cells.2
  57.9 5.9 %all-to-all-start.3 = ((f32[16,16,128]{2,1,0:T(8,128)}), f32[16,16,128]{2,1,0:T(8,128)S(1)}, u32[]{:S(2)}, u32[]{:S(2)}) async-start(f32[16,16,128]{2,1,0:T(8,128)} %bitcast.49), calls=%async_computation.3 | async-start | bytes 262144 | tf_op jit(solution)/shard_map/all_to_all | solution.py:400
  63.9 0.0 copy-done.4
  63.9 0.7 copy.21
  64.5 2.3 %bypass_fields.1.bypass_ref = f32[256,512]{1,0:T(8,128)} custom-call(f32[640,128]{1,0:T(8,128)} %bitcast.46, f32[20,20]{1,0:T(8,128)} %bitcast.66), custom_call_target="tpu_custom_call" | custom-call | flops 10000000 | bytes 853568 | tf_op jit(solution)/shard_map/bypass_fields/pallas_call | solution.py:93
  66.9 6.2 %all-to-all-done.3 = f32[16,16,128]{2,1,0:T(8,128)S(1)} async-done(((f32[16,16,128]{2,1,0:T(8,128)}), f32[16,16,128]{2,1,0:T(8,128)S(1)}, u32[]{:S(2)}, u32[]{:S(2)}) %all-to-all-start.3) | async-done | bytes 131104 | tf_op jit(solution)/shard_map/all_to_all | solution.py:400
  73.0 0.0 copy-start.1
  73.0 0.7 copy-done.1
  73.7 4.5 %activate.1 = (f32[640,128]{1,0:T(8,128)}, f32[256,512]{1,0:T(8,128)}, f32[256,128]{1,0:T(8,128)}) custom-call(f32[256,128]{1,0:T(8,128)} %bitcast.53, f32[192,512]{1,0:T(8,128)} %constant.33.clone.table_ref, f32[256,512]{1,0:T(8,128)} %bypass_fields.1.bypass_ref, f32[640,128]{1,0:T(8,128)} %bitcast.55), custom_call_target="tpu_custom_call" | custom-call | flops 10000000 | bytes 2359296 | tf_op jit(solution)/shard_map/activate/pallas_call | solution.py:93
  78.2 12.5 %all_to_all.47 = f32[16,16,128]{2,1,0:T(8,128)} all-to-all(f32[16,16,128]{2,1,0:T(8,128)} %bitcast.64), channel_id=1, replica_groups=mesh['dp'=4,'gx'=8,'gy'=16] {'gy'}, dimensions={0} | all-to-all | bytes 262144 | tf_op jit(solution)/shard_map/all_to_all | solution.py:400
  90.7 1.9 y_spectrum.3
  92.6 11.4 %all_to_all.48 = f32[8,16,128]{2,1,0:T(8,128)} all-to-all(f32[8,16,128]{2,1,0:T(8,128)} %bitcast.60), channel_id=1, replica_groups=mesh['dp'=4,'gx'=8,'gy'=16] {'gx'}, dimensions={0} | all-to-all | bytes 131072 | tf_op jit(solution)/shard_map/all_to_all | solution.py:400
  104.0 1.8 x_dual.1
  105.7 33.3 %x_unmix.1 = f32[128,128]{1,0:T(8,128)} custom-call(s32[1]{0:T(128)} %bitcast.odd_ref, f32[64,128]{1,0:T(8,128)} %get-tuple-element.14.dual_ref, f32[4320,20]{1,0:T(8,128)} %bitcast.43, f32[64,32]{1,0:T(8,128)} %constant.39.clone.inv_ref), custom_call_target="tpu_custom_call" | custom-call | flops 10000000 | bytes 452100 | tf_op jit(solution)/shard_map/x_unmix/pallas_call | solution.py:93
  139.1 11.2 %all_to_all.49 = f32[8,16,128]{2,1,0:T(8,128)} all-to-all(f32[8,16,128]{2,1,0:T(8,128)} %bitcast.61), channel_id=1, replica_groups=mesh['dp'=4,'gx'=8,'gy'=16] {'gx'}, dimensions={0} | all-to-all | bytes 131072 | tf_op jit(solution)/shard_map/all_to_all | solution.py:400
  150.3 4.0 %all-to-all-start.8 = ((f32[4,128,128]{2,1,0:T(8,128)}), f32[4,128,128]{2,1,0:T(8,128)S(1)}, u32[]{:S(2)}, u32[]{:S(2)}) async-start(f32[4,128,128]{2,1,0:T(8,128)} %bitcast.33), calls=%async_computation.8 | async-start | bytes 524288 | tf_op jit(solution)/shard_map/all_to_all | solution.py:400
  154.3 1.8 y_cells.3
  156.1 3.7 %all-to-all-done.8 = f32[4,128,128]{2,1,0:T(8,128)S(1)} async-done(((f32[4,128,128]{2,1,0:T(8,128)}), f32[4,128,128]{2,1,0:T(8,128)S(1)}, u32[]{:S(2)}, u32[]{:S(2)}) %all-to-all-start.8) | async-done | bytes 262176 | tf_op jit(solution)/shard_map/all_to_all | solution.py:400
  159.8 0.0 copy-start
  159.8 7.0 %all-to-all-start.7 = ((f32[16,16,128]{2,1,0:T(8,128)}), f32[16,16,128]{2,1,0:T(8,128)S(1)}, u32[]{:S(2)}, u32[]{:S(2)}) async-start(f32[16,16,128]{2,1,0:T(8,128)} %bitcast.48), calls=%async_computation.7 | async-start | bytes 262144 | tf_op jit(solution)/shard_map/all_to_all | solution.py:400
  166.8 2.4 %bypass_signal.1.bypass_ref = f32[256,512]{1,0:T(8,128)} custom-call(f32[256,512]{1,0:T(8,128)} %get-tuple-element.15.signal_ref, f32[20,20]{1,0:T(8,128)} %map_ref.1), custom_call_target="tpu_custom_call" | custom-call | flops 10000000 | bytes 1050176 | tf_op jit(solution)/shard_map/bypass_signal/pallas_call | solution.py:93
  169.2 0.0 copy-done
  169.2 16.0 %weight_grad.1 = f32[4320,20]{1,0:T(8,128)} custom-call(s32[1]{0:T(128)} %bitcast.odd_ref, f32[512,128]{1,0:T(8,128)} %bitcast.47), custom_call_target="tpu_custom_call" | custom-call | flops 10000000 | bytes 607748 | tf_op jit(solution)/shard_map/weight_grad/pallas_call | solution.py:93
  185.2 0.0 all-to-all-done.7
  185.2 0.0 copy-start.2
  185.2 0.7 copy-done.2
  185.9 2.9 %finish.1 = f32[640,128]{1,0:T(8,128)} custom-call(f32[256,128]{1,0:T(8,128)} %bitcast.54, f32[192,512]{1,0:T(8,128)} %constant.33.clone.table_ref, f32[256,512]{1,0:T(8,128)} %bypass_signal.1.bypass_ref), custom_call_target="tpu_custom_call" | custom-call | flops 10000000 | bytes 1376256 | tf_op jit(solution)/shard_map/finish/pallas_call | solution.py:93
Async XLA Ops:
  0.6 63.2 %copy-start.4 = (f32[20,20]{1,0:T(8,128)S(1)}, f32[20,20]{1,0:T(8,128)}, u32[]{:S(2)}) copy-start(f32[20,20]{1,0:T(8,128)} %map_ref.1) | copy-start | bytes 4804
  26.2 14.0 %all-to-all-start.1 = ((f32[8,16,128]{2,1,0:T(8,128)}), f32[8,16,128]{2,1,0:T(8,128)S(1)}, u32[]{:S(2)}, u32[]{:S(2)}) async-start(f32[8,16,128]{2,1,0:T(8,128)} %bitcast.58), calls=%async_computation.1 | async-start | bytes 131072 | tf_op jit(solution)/shard_map/all_to_all | solution.py:400
  40.1 0.6 copy-start.3
  57.9 15.1 %all-to-all-start.3 = ((f32[16,16,128]{2,1,0:T(8,128)}), f32[16,16,128]{2,1,0:T(8,128)S(1)}, u32[]{:S(2)}, u32[]{:S(2)}) async-start(f32[16,16,128]{2,1,0:T(8,128)} %bitcast.49), calls=%async_computation.3 | async-start | bytes 262144 | tf_op jit(solution)/shard_map/all_to_all | solution.py:400
  73.0 0.7 copy-start.1
  150.3 9.5 %all-to-all-start.8 = ((f32[4,128,128]{2,1,0:T(8,128)}), f32[4,128,128]{2,1,0:T(8,128)S(1)}, u32[]{:S(2)}, u32[]{:S(2)}) async-start(f32[4,128,128]{2,1,0:T(8,128)} %bitcast.33), calls=%async_computation.8 | async-start | bytes 524288 | tf_op jit(solution)/shard_map/all_to_all | solution.py:400
  159.8 9.4 %copy-start = (f32[4,128,128]{2,1,0:T(8,128)}, f32[4,128,128]{2,1,0:T(8,128)S(1)}, u32[]{:S(2)}) copy-start(f32[4,128,128]{2,1,0:T(8,128)S(1)} %all-to-all-done.8) | copy-start | bytes 786436
  159.8 25.4 %all-to-all-start.7 = ((f32[16,16,128]{2,1,0:T(8,128)}), f32[16,16,128]{2,1,0:T(8,128)S(1)}, u32[]{:S(2)}, u32[]{:S(2)}) async-start(f32[16,16,128]{2,1,0:T(8,128)} %bitcast.48), calls=%async_computation.7 | async-start | bytes 262144 | tf_op jit(solution)/shard_map/all_to_all | solution.py:400
  185.2 0.7 copy-start.2
where the time goes:
time: 190 us; the launch traced here: 189 us
  Pallas kernels  77.6 us (41%)
  blocking collectives  67.1 us (35%)
  starting transfers between devices  23.8 us (13%)
  waiting for transfers between devices  17 us (9%)
  local copies, waits for them, and re-layouts  2.64 us (1%)
    pallas_call x13, Pallas kernels, call(): pl.pallas_call(body, out_shape=shapes, in_specs=specs, out_specs=[pl.Bloc...  77.6 us
    all_to_all x5, blocking collectives, swap(): lax.all_to_all(a.reshape(n, rows, 128), axis, split_axis=0, concat_axis=0...  67.1 us
    all_to_all x4, starting transfers between devices, swap(): lax.all_to_all(a.reshape(n, rows, 128), axis, split_axis=0, concat_axis=0...  23.8 us
    all_to_all x4, waiting for transfers between devices, swap(): lax.all_to_all(a.reshape(n, rows, 128), axis, split_axis=0, concat_axis=0...  17 us
  transfers between devices with their start and end apart: 4, of which 3 were waited for; matrix products, arithmetic and copies ran while one was open for 0% of the time, Pallas kernels for 12%

commit v1 on v0

--- a/solution.py
+++ b/solution.py
@@ -96,6 +96,7 @@
         in_specs=specs,
         out_specs=[pl.BlockSpec(memory_space=VMEM)] * len(outs),
         scratch_shapes=list(scratch),
+        compiler_params=pltpu.CompilerParams(vmem_limit_bytes=16 << 20),
         cost_estimate=pl.CostEstimate(flops=flops, bytes_accessed=nbytes, transcendentals=0),
         interpret=INTERPRET,
         name=name,
@@ -251,86 +252,105 @@
     return pl.ds(pair * (KX * C) + c, KX, stride=C)
 
 
-def x_mix(odd_ref, recv_ref, weight_ref, fwd_ref, inv_ref, send_ref, spec_ref, mixed_ref):
+def packed_row(part, c, tile):
+    at = ((part * C + c) * 2 + tile) * 16
+    return slice(at, at + 16)
+
+
+def pack_weights(odd_ref, weight_ref, packed_ref):
     odd = odd_ref[0]
+    packed_ref[...] = jnp.zeros_like(packed_ref)
+    for tile, s, pair in slots(odd):
+        for part in range(2):
+            for c in range(C):
+                at = packed_row(part, c, tile).start
+                packed_ref[at : at + KX, 20 * s : 20 * s + C] = weight_ref[weight_row(9 * part + pair, c), :]
+
+
+def group_start():
+    lane = lanes(16)
+    return jnp.right_shift(lane * 205, 12) * 20
+
+
+def pick(a, index):
+    return jnp.take_along_axis(a, index, axis=1, mode="promise_in_bounds")
+
+
+def x_mix(recv_ref, packed_ref, fwd_ref, inv_ref, send_ref, spec_ref):
     spectrum = x_spectrum(recv_ref, fwd_ref)
+    start = group_start()
+    mixed = []
     for tile in range(2):
         spec_ref[tile * 32 : tile * 32 + 32, :] = spectrum[tile]
-    mixed_ref[...] = jnp.zeros_like(mixed_ref)
-    for tile, s, pair in slots(odd):
-        real = spectrum[tile][:KX]
-        imag = spectrum[tile][16 : 16 + KX]
-        out_real = jnp.zeros((KX, C), F32)
-        out_imag = jnp.zeros((KX, C), F32)
+        real, imag = spectrum[tile][:16], spectrum[tile][16:]
+        out_real = jnp.zeros((16, 128), F32)
+        out_imag = jnp.zeros((16, 128), F32)
         for c in range(C):
-            wr = weight_ref[weight_row(pair, c), :]
-            wi = weight_ref[weight_row(9 + pair, c), :]
-            at = 20 * s + c
-            sr = real[:, at : at + 1]
-            si = imag[:, at : at + 1]
+            index = jnp.minimum(start + c, 127)
+            sr, si = pick(real, index), pick(imag, index)
+            wr = packed_ref[packed_row(0, c, tile), :]
+            wi = packed_ref[packed_row(1, c, tile), :]
             out_real = out_real + (sr * wr - si * wi)
             out_imag = out_imag + (sr * wi + si * wr)
-        mixed_ref[tile * 32 : tile * 32 + KX, 20 * s : 20 * s + C] = out_real
-        mixed_ref[tile * 32 + 16 : tile * 32 + 16 + KX, 20 * s : 20 * s + C] = out_imag
-    x_cells([mixed_ref[:32, :], mixed_ref[32:, :]], inv_ref, send_ref)
-
-
-def x_dual(recv_ref, spec_ref, fwd_ref, dual_ref, share_ref):
+        mixed.append(jnp.concatenate([out_real, out_imag], axis=0))
+    x_cells(mixed, inv_ref, send_ref)
+
+
+def x_unmix(recv_ref, spec_ref, packed_ref, fwd_ref, inv_ref, sum_ref, share_ref, send_ref, high_ref, low_ref):
     spectrum = x_spectrum(recv_ref, fwd_ref)
     copies = share_ref.shape[0] // 128
     for tile in range(2):
-        dual_ref[tile * 32 : tile * 32 + 32, :] = spectrum[tile]
         for n in range(copies):
-            share_ref[n * 128 + tile * 32 : n * 128 + tile * 32 + 32, :] = spec_ref[
-                tile * 32 : tile * 32 + 32, :
-            ]
-            share_ref[n * 128 + 64 + tile * 32 : n * 128 + 96 + tile * 32, :] = spectrum[tile]
-
-
-def x_unmix(odd_ref, dual_ref, weight_ref, inv_ref, send_ref):
-    odd = odd_ref[0]
-    lane = lanes(KX)
-    back = [[jnp.zeros((KX, 128), F32) for _ in range(2)] for _ in range(2)]
-    for tile, s, pair in slots(odd):
-        dr = dual_ref[tile * 32 : tile * 32 + KX, 20 * s : 20 * s + C]
-        di = dual_ref[tile * 32 + 16 : tile * 32 + 16 + KX, 20 * s : 20 * s + C]
+            at = n * 128 + tile * 32
+            share_ref[at : at + 32, :] = spec_ref[tile * 32 : tile * 32 + 32, :]
+            share_ref[at + 64 : at + 96, :] = spectrum[tile]
+        dr, di = spectrum[tile][:16], spectrum[tile][16:]
         for c in range(C):
-            wr = weight_ref[weight_row(pair, c), :]
-            wi = weight_ref[weight_row(9 + pair, c), :]
-            real = jnp.sum(dr * wr + di * wi, axis=1, keepdims=True)
-            imag = jnp.sum(di * wr - dr * wi, axis=1, keepdims=True)
-            here = lane == 20 * s + c
-            back[tile][0] = jnp.where(here, real, back[tile][0])
-            back[tile][1] = jnp.where(here, imag, back[tile][1])
-    gap = jnp.zeros((16 - KX, 128), F32)
-    x_cells(
-        [jnp.concatenate([re, gap, im, gap], axis=0) for re, im in back], inv_ref, send_ref
-    )
+            wr = packed_ref[packed_row(0, c, tile), :]
+            wi = packed_ref[packed_row(1, c, tile), :]
+            for part, term in enumerate((dr * wr + di * wi, di * wr - dr * wi)):
+                high = term.astype(jnp.bfloat16)
+                at = (tile * 2 + part) * 16
+                high_ref[at : at + 16, c * 128 : c * 128 + 128] = high
+                low_ref[at : at + 16, c * 128 : c * 128 + 128] = (term - high.astype(F32)).astype(jnp.bfloat16)
+    back = jnp.dot(high_ref[...], sum_ref[...], preferred_element_type=F32) + jnp.dot(
+        low_ref[...], sum_ref[...], preferred_element_type=F32
+    )
+    x_cells([back[:32], back[32:]], inv_ref, send_ref)
+
+
+def sum_table():
+    out = np.zeros((C, 128, 128))
+    for c in range(C):
+        for s in range(6):
+            out[c, 20 * s : 20 * s + C, 20 * s + c] = 1.0
+    return out.reshape(C * 128, 128).astype(jnp.bfloat16)
 
 
 def weight_grad(odd_ref, share_ref, grad_ref):
     odd = odd_ref[0]
     samples = share_ref.shape[0] // 128
-    for tile, s, pair in slots(odd):
+    start = group_start()
+    owned = list(slots(odd))
+    for tile in range(2):
         spec, dual = [], []
         for n in range(samples):
             at = n * 128 + tile * 32
-            spec.append([share_ref[at + p * 16 : at + p * 16 + KX, :] for p in range(2)])
-            dual.append(
-                [share_ref[at + 64 + p * 16 : at + 64 + p * 16 + KX, 20 * s : 20 * s + C] for p in range(2)]
-            )
+            spec.append([share_ref[at + p * 16 : at + p * 16 + 16, :] for p in range(2)])
+            dual.append([share_ref[at + 64 + p * 16 : at + 80 + p * 16, :] for p in range(2)])
         for c in range(C):
-            real = jnp.zeros((KX, C), F32)
-            imag = jnp.zeros((KX, C), F32)
-            at = 20 * s + c
+            index = jnp.minimum(start + c, 127)
+            real = jnp.zeros((16, 128), F32)
+            imag = jnp.zeros((16, 128), F32)
             for n in range(samples):
-                sr = spec[n][0][:, at : at + 1]
-                si = spec[n][1][:, at : at + 1]
+                sr, si = pick(spec[n][0], index), pick(spec[n][1], index)
                 dr, di = dual[n]
                 real = real + (sr * dr + si * di)
                 imag = imag + (sr * di - si * dr)
-            grad_ref[weight_row(pair, c), :] = real
-            grad_ref[weight_row(9 + pair, c), :] = imag
+            for where, s, pair in owned:
+                if where == tile:
+                    grad_ref[weight_row(pair, c), :] = real[:KX, 20 * s : 20 * s + C]
+                    grad_ref[weight_row(9 + pair, c), :] = imag[:KX, 20 * s : 20 * s + C]
 
 
 def activate(recv_ref, table_ref, bypass_ref, cotangent_ref, out_ref, signal_ref, send_ref, modes_ref):
@@ -369,6 +389,7 @@
 CELLS = (256, NR)
 SEND_Y = (GY * 16, 128)
 SEND_X = (GX * 16, 128)
+PACKED = (2 * C * 2 * 16, 128)
 
 
 def stages(samples):
@@ -382,11 +403,15 @@
         bypass_signal=lambda f, b: call(bypass_signal, [CELLS], f, b, name="bypass_signal"),
         y_spectrum=lambda r: call(y_spectrum, [SEND_X], r, ay, name="y_spectrum"),
         y_cells=lambda r: call(y_cells, [SEND_Y], r, by, scratch=[VMEM((24, 512), F32)], name="y_cells"),
-        x_mix=lambda o, r, w: call(
-            x_mix, [SEND_X, (64, 128)], o, r, w, ax, bx, scratch=[VMEM((64, 128), F32)], smem=(0,), name="x_mix"
+        pack_weights=lambda o, w: call(pack_weights, [PACKED], o, w, smem=(0,), name="pack_weights"),
+        x_mix=lambda r, w: call(x_mix, [SEND_X, (64, 128)], r, w, ax, bx, name="x_mix"),
+        x_unmix=lambda r, s, w: call(
+            x_unmix,
+            [(samples * 128, 128), SEND_X],
+            *(r, s, w, ax_dual, bx_dual, sum_table()),
+            scratch=[VMEM((64, C * 128), jnp.bfloat16)] * 2,
+            name="x_unmix",
         ),
-        x_dual=lambda r, s: call(x_dual, [(64, 128), (samples * 128, 128)], r, s, ax_dual, name="x_dual"),
-        x_unmix=lambda o, d, w: call(x_unmix, [SEND_X], o, d, w, bx_dual, smem=(0,), name="x_unmix"),
         weight_grad=lambda o, s: call(weight_grad, [(2 * 9 * KX * C, C)], o, s, smem=(0,), name="weight_grad"),
         activate=lambda r, b, ct: call(
             activate, [(640, 128), CELLS, SEND_Y], r, tz, b, ct, scratch=modes, name="activate"
@@ -412,15 +437,16 @@
     to_x = functools.partial(swap, axis="gx", n=GX)
     direct = st["bypass_fields"](rows, bypass.T)
     arrived = to_x(st["y_spectrum"](to_y(st["depth_forward"](rows))))
-    mixed, spec = st["x_mix"](odd, arrived, weights)
+    packed = st["pack_weights"](odd, weights)
+    mixed, spec = st["x_mix"](arrived, packed)
     arrived = to_y(st["y_cells"](to_x(mixed)))
     output, signal, sent = st["activate"](arrived, direct, as_rows(cotangent))
     direct = st["bypass_signal"](signal, bypass)
     arrived = to_x(st["y_spectrum"](to_y(sent)))
-    dual, share = st["x_dual"](arrived, spec)
+    share, sent = st["x_unmix"](arrived, spec, packed)
     shared = swap(share, "dp", samples)
     grad = st["weight_grad"](odd, shared)
-    arrived = to_y(st["y_cells"](to_x(st["x_unmix"](odd, dual, weights))))
+    arrived = to_y(st["y_cells"](to_x(sent)))
     field_grad = st["finish"](arrived, direct)
     return (from_rows(output), from_rows(field_grad), grad.reshape(spectral.shape))
 

time: 190 us -> 134 us (0.71)
  Pallas kernels: 77.6 us -> 18.3 us
  blocking collectives: 67.1 us -> 61 us
  local copies, waits for them, and re-layouts: 2.64 us -> 7.43 us
  waiting for transfers between devices: 17 us -> 21.3 us
    pallas_call x13, Pallas kernels: 77.6 us -> 18.3 us  [call(): pl.pallas_call(body, out_shape=shapes, in_specs=specs, out_specs=[pl.Bloc...]
    all_to_all x5, blocking collectives: 67.1 us -> 61 us  [swap(): lax.all_to_all(a.reshape(n, rows, 128), axis, split_axis=0, concat_axis=0...]
    unnamed x11 -> x37, local copies, waits for them, and re-layouts: 2.64 us -> 7.43 us
    all_to_all x4, waiting for transfers between devices: 17 us -> 21.3 us  [swap(): lax.all_to_all(a.reshape(n, rows, 128), axis, split_axis=0, concat_axis=0...]
  transfers between devices with their start and end apart: 4 -> 4, of which waited for: 3 -> 4; matrix products, arithmetic and copies ran while one was open for 0% -> 0% of each run, Pallas kernels for 12% -> 6%
where the time goes in v1:
time: 134 us; the launch traced here: 132 us
  blocking collectives  61 us (46%)
  starting transfers between devices  23.7 us (18%)
  waiting for transfers between devices  21.3 us (16%)
  Pallas kernels  18.3 us (14%)
  local copies, waits for them, and re-layouts  7.43 us (6%)
    all_to_all x5, blocking collectives, swap(): lax.all_to_all(a.reshape(n, rows, 128), axis, split_axis=0, concat_axis=0...  61 us
    all_to_all x4, starting transfers between devices, swap(): lax.all_to_all(a.reshape(n, rows, 128), axis, split_axis=0, concat_axis=0...  23.7 us
    all_to_all x4, waiting for transfers between devices, swap(): lax.all_to_all(a.reshape(n, rows, 128), axis, split_axis=0, concat_axis=0...  21.3 us
    pallas_call x13, Pallas kernels, call(): pl.pallas_call(body, out_shape=shapes, in_specs=specs, out_specs=[pl.Bloc...  18.3 us
    unnamed x37, local copies, waits for them, and re-layouts  7.43 us
  transfers between devices with their start and end apart: 4, of which 4 were waited for; matrix products, arithmetic and copies ran while one was open for 0% of the time, Pallas kernels for 6%

profile of v1, /device:TPU:1, one launch (start us, length us, event | category | flops | bytes accessed | tf_op | source)
XLA Modules:
  0.0 132.5 jit_solution(7013396802194443011)
XLA Ops:
  0.6 0.0 copy-start
  0.6 1.0 copy-done
  1.6 0.0 copy-start.3
  1.6 1.0 copy-done.3
  2.6 0.0 copy-start.13
  2.6 0.0 copy-start.17
  2.6 1.1 depth_forward.1
  3.7 0.0 copy-start.7
  3.7 20.5 %all_to_all.45 = f32[16,16,128]{2,1,0:T(8,128)S(1)} all-to-all(f32[16,16,128]{2,1,0:T(8,128)S(1)} %bitcast.48), channel_id=1, replica_groups=mesh['dp'=4,'gx'=8,'gy'=16] {'gy'}, dimensions={0} | all-to-all | bytes 262144 | tf_op jit(solution)/shard_map/all_to_all | solution.py:425
  24.2 0.0 copy-start.9
  24.2 0.7 copy-done.9
  25.0 0.0 copy-start.4
  25.0 1.0 y_spectrum.2
  25.9 0.0 copy-start.11
  25.9 7.0 %all-to-all-start.1 = ((f32[8,16,128]{2,1,0:T(8,128)}), f32[8,16,128]{2,1,0:T(8,128)S(1)}, u32[]{:S(2)}, u32[]{:S(2)}) async-start(f32[8,16,128]{2,1,0:T(8,128)} %bitcast.5), calls=%async_computation.1 | async-start | bytes 131072 | tf_op jit(solution)/shard_map/all_to_all | solution.py:425
  32.9 0.0 copy-start.2
  32.9 1.6 %copy-done.2 = f32[2,9,1,12,20,20]{5,2,4,3,1,0:T(1,128)S(1)} copy-done((f32[2,9,1,12,20,20]{5,2,4,3,1,0:T(1,128)S(1)}, f32[2,9,1,12,20,20]{5,2,4,3,1,0:T(1,128)}, u32[]{:S(2)}) %copy-start.2) | copy-done | bytes 345624
  34.5 0.0 copy-start.1
  34.5 0.0 copy-start.6
  34.5 0.7 pack_weights.1.packed_ref
  35.2 0.0 copy-start.5
  35.2 4.9 %all-to-all-done.1 = f32[8,16,128]{2,1,0:T(8,128)S(1)} async-done(((f32[8,16,128]{2,1,0:T(8,128)}), f32[8,16,128]{2,1,0:T(8,128)S(1)}, u32[]{:S(2)}, u32[]{:S(2)}) %all-to-all-start.1) | async-done | bytes 65568 | tf_op jit(solution)/shard_map/all_to_all | solution.py:425
  40.0 0.0 copy-done.13
  40.0 0.0 copy-done.17
  40.0 0.8 x_mix.1
  40.9 0.0 copy-start.14
  40.9 9.6 %all_to_all.46 = f32[8,16,128]{2,1,0:T(8,128)S(1)} all-to-all(f32[8,16,128]{2,1,0:T(8,128)S(1)} %bitcast.59), channel_id=1, replica_groups=mesh['dp'=4,'gx'=8,'gy'=16] {'gx'}, dimensions={0} | all-to-all | bytes 131072 | tf_op jit(solution)/shard_map/all_to_all | solution.py:425
  50.5 0.0 copy-done.7
  50.5 1.0 y_cells.2
  51.5 0.0 copy-done.14
  51.5 5.9 %all-to-all-start.3 = ((f32[16,16,128]{2,1,0:T(8,128)}), f32[16,16,128]{2,1,0:T(8,128)S(1)}, u32[]{:S(2)}, u32[]{:S(2)}) async-start(f32[16,16,128]{2,1,0:T(8,128)} %bitcast.11), calls=%async_computation.3 | async-start | bytes 262144 | tf_op jit(solution)/shard_map/all_to_all | solution.py:425
  57.4 0.0 copy-done.11
  57.4 0.1 copy.22
  57.5 0.0 copy-done.4
  57.5 0.5 bypass_fields.1.bypass_ref
  58.0 0.0 copy-start.8
  58.0 8.6 %all-to-all-done.3 = f32[16,16,128]{2,1,0:T(8,128)S(1)} async-done(((f32[16,16,128]{2,1,0:T(8,128)}), f32[16,16,128]{2,1,0:T(8,128)S(1)}, u32[]{:S(2)}, u32[]{:S(2)}) %all-to-all-start.3) | async-done | bytes 131104 | tf_op jit(solution)/shard_map/all_to_all | solution.py:425
  66.6 0.0 copy-done.1
  66.6 0.0 copy-done.6
  66.6 3.0 %activate.1 = (f32[640,128]{1,0:T(8,128)}, f32[256,512]{1,0:T(8,128)S(1)}, f32[256,128]{1,0:T(8,128)S(1)}) custom-call(f32[256,128]{1,0:T(8,128)S(1)} %bitcast.49, f32[192,512]{1,0:T(8,128)S(1)} %copy-done.1, f32[256,512]{1,0:T(8,128)S(1)} %bypass_fields.1.bypass_ref, f32[640,128]{1,0:T(8,128)S(1)} %bitcast.51), custom_call_target="tpu_custom_call" | custom-call | flops 10000000 | bytes 2359296 | tf_op jit(solution)/shard_map/activate/pallas_call | solution.py:93
  69.6 11.3 %all_to_all.47 = f32[16,16,128]{2,1,0:T(8,128)S(1)} all-to-all(f32[16,16,128]{2,1,0:T(8,128)S(1)} %bitcast.57), channel_id=1, replica_groups=mesh['dp'=4,'gx'=8,'gy'=16] {'gy'}, dimensions={0} | all-to-all | bytes 262144 | tf_op jit(solution)/shard_map/all_to_all | solution.py:425
  80.9 0.0 copy-start.10
  80.9 0.7 copy-done.10
  81.6 0.3 y_spectrum.3
  82.0 9.9 %all_to_all.48 = f32[8,16,128]{2,1,0:T(8,128)S(1)} all-to-all(f32[8,16,128]{2,1,0:T(8,128)S(1)} %bitcast.55), channel_id=1, replica_groups=mesh['dp'=4,'gx'=8,'gy'=16] {'gx'}, dimensions={0} | all-to-all | bytes 131072 | tf_op jit(solution)/shard_map/all_to_all | solution.py:425
  91.9 0.0 copy-done.5
  91.9 0.0 copy-start.12
  91.9 0.8 copy-done.12
  92.7 0.0 copy-start.15
  92.7 0.8 copy-done.15
  93.4 0.0 copy-start.16
  93.4 0.7 copy-done.16
  94.1 1.4 %x_unmix.1 = (f32[512,128]{1,0:T(8,128)}, f32[128,128]{1,0:T(8,128)S(1)}) custom-call(f32[128,128]{1,0:T(8,128)S(1)} %bitcast.53, f32[64,128]{1,0:T(8,128)S(1)} %copy-done.15, f32[1280,128]{1,0:T(8,128)S(1)} %pack_weights.1.packed_ref, f32[32,64]{1,0:T(8,128)S(1)} %copy-done.16, f32[64,32]{1,0:T(8,128)S(1)} %copy-done.12, bf16[2560,128]{1,0:T(8,128)(2,1)S(1)} %copy-done.5), custom_call_target="tpu_custom_call" | custom-call | flops 10000000 | bytes 1753088 | tf_op jit(solution)/shard_map/x_unmix/pallas_call | solution.py:93
  95.5 9.7 %all_to_all.49 = f32[8,16,128]{2,1,0:T(8,128)S(1)} all-to-all(f32[8,16,128]{2,1,0:T(8,128)S(1)} %bitcast.58), channel_id=1, replica_groups=mesh['dp'=4,'gx'=8,'gy'=16] {'gx'}, dimensions={0} | all-to-all | bytes 131072 | tf_op jit(solution)/shard_map/all_to_all | solution.py:425
  105.2 4.0 %all-to-all-start.8 = ((f32[4,128,128]{2,1,0:T(8,128)}), f32[4,128,128]{2,1,0:T(8,128)S(1)}, u32[]{:S(2)}, u32[]{:S(2)}) async-start(f32[4,128,128]{2,1,0:T(8,128)} %bitcast.33), calls=%async_computation.8 | async-start | bytes 524288 | tf_op jit(solution)/shard_map/all_to_all | solution.py:425
  109.2 0.0 copy-done.8
  109.2 1.0 y_cells.3
  110.3 4.5 %all-to-all-done.8 = f32[4,128,128]{2,1,0:T(8,128)S(1)} async-done(((f32[4,128,128]{2,1,0:T(8,128)}), f32[4,128,128]{2,1,0:T(8,128)S(1)}, u32[]{:S(2)}, u32[]{:S(2)}) %all-to-all-start.8) | async-done | bytes 262176 | tf_op jit(solution)/shard_map/all_to_all | solution.py:425
  114.8 6.8 %all-to-all-start.7 = ((f32[16,16,128]{2,1,0:T(8,128)}), f32[16,16,128]{2,1,0:T(8,128)S(1)}, u32[]{:S(2)}, u32[]{:S(2)}) async-start(f32[16,16,128]{2,1,0:T(8,128)} %bitcast.28), calls=%async_computation.7 | async-start | bytes 262144 | tf_op jit(solution)/shard_map/all_to_all | solution.py:425
  121.6 0.5 bypass_signal.1.bypass_ref
  122.1 5.3 %weight_grad.1 = f32[4320,20]{1,0:T(8,128)} custom-call(s32[1]{0:T(128)} %bitcast.7.odd_ref, f32[512,128]{1,0:T(8,128)S(1)} %bitcast.45), custom_call_target="tpu_custom_call" | custom-call | flops 10000000 | bytes 607748 | tf_op jit(solution)/shard_map/weight_grad/pallas_call | solution.py:93
  127.4 3.3 %all-to-all-done.7 = f32[16,16,128]{2,1,0:T(8,128)S(1)} async-done(((f32[16,16,128]{2,1,0:T(8,128)}), f32[16,16,128]{2,1,0:T(8,128)S(1)}, u32[]{:S(2)}, u32[]{:S(2)}) %all-to-all-start.7) | async-done | bytes 131104 | tf_op jit(solution)/shard_map/all_to_all | solution.py:425
  130.8 1.7 %finish.1 = f32[640,128]{1,0:T(8,128)} custom-call(f32[256,128]{1,0:T(8,128)S(1)} %bitcast.50, f32[192,512]{1,0:T(8,128)S(1)} %copy-done.1, f32[256,512]{1,0:T(8,128)S(1)} %bypass_signal.1.bypass_ref), custom_call_target="tpu_custom_call" | custom-call | flops 10000000 | bytes 1376256 | tf_op jit(solution)/shard_map/finish/pallas_call | solution.py:93
Async XLA Ops:
  0.6 1.0 copy-start
  1.6 1.0 copy-start.3
  2.6 37.4 %copy-start.13 = (f32[64,32]{1,0:T(8,128)S(1)}, f32[64,32]{1,0:T(8,128)}, u32[]{:S(2)}) copy-start(f32[64,32]{1,0:T(8,128)} %constant.38.clone.inv_ref) | copy-start | bytes 24580
  2.6 37.4 %copy-start.17 = (f32[32,64]{1,0:T(8,128)S(1)}, f32[32,64]{1,0:T(8,128)}, u32[]{:S(2)}) copy-start(f32[32,64]{1,0:T(8,128)} %constant.37.clone.fwd_ref) | copy-start | bytes 24580
  3.7 46.8 %copy-start.7 = (f32[64,24]{1,0:T(8,128)S(1)}, f32[64,24]{1,0:T(8,128)}, u32[]{:S(2)}) copy-start(f32[64,24]{1,0:T(8,128)} %constant.39.clone.table_ref) | copy-start | bytes 18436
  24.2 0.7 copy-start.9
  25.0 32.5 %copy-start.4 = (f32[1,20,4,2,512]{4,3,2,1,0:T(2,128)S(1)}, f32[1,20,4,2,512]{4,3,2,1,0:T(2,128)}, u32[]{:S(2)}) copy-start(f32[1,20,4,2,512]{4,3,2,1,0:T(2,128)} %param.12) | copy-start | bytes 983044
  25.9 31.5 %copy-start.11 = (f32[20,20]{1,0:T(8,128)S(1)}, f32[20,20]{1,0:T(8,128)}, u32[]{:S(2)}) copy-start(f32[20,20]{1,0:T(8,128)} %map_ref.1) | copy-start | bytes 4804
  25.9 14.1 %all-to-all-start.1 = ((f32[8,16,128]{2,1,0:T(8,128)}), f32[8,16,128]{2,1,0:T(8,128)S(1)}, u32[]{:S(2)}, u32[]{:S(2)}) async-start(f32[8,16,128]{2,1,0:T(8,128)} %bitcast.5), calls=%async_computation.1 | async-start | bytes 131072 | tf_op jit(solution)/shard_map/all_to_all | solution.py:425
  32.9 1.6 %copy-start.2 = (f32[2,9,1,12,20,20]{5,2,4,3,1,0:T(1,128)S(1)}, f32[2,9,1,12,20,20]{5,2,4,3,1,0:T(1,128)}, u32[]{:S(2)}) copy-start(f32[2,9,1,12,20,20]{5,2,4,3,1,0:T(1,128)} %param.14) | copy-start | bytes 1036804
  34.5 32.1 %copy-start.1 = (f32[192,512]{1,0:T(8,128)S(1)}, f32[192,512]{1,0:T(8,128)}, u32[]{:S(2)}) copy-start(f32[192,512]{1,0:T(8,128)} %constant.35.clone.table_ref) | copy-start | bytes 1179652
  34.5 32.1 %copy-start.6 = (f32[1,20,4,2,512]{4,3,2,1,0:T(2,128)S(1)}, f32[1,20,4,2,512]{4,3,2,1,0:T(2,128)}, u32[]{:S(2)}) copy-start(f32[1,20,4,2,512]{4,3,2,1,0:T(2,128)} %param.13) | copy-start | bytes 983044
  35.2 56.7 %copy-start.5 = (bf16[2560,128]{1,0:T(8,128)(2,1)S(1)}, bf16[2560,128]{1,0:T(8,128)(2,1)}, u32[]{:S(2)}) copy-start(bf16[2560,128]{1,0:T(8,128)(2,1)} %constant.42.clone.sum_ref) | copy-start | bytes 1966084
  40.9 10.6 %copy-start.14 = (f32[64,128]{1,0:T(8,128)}, f32[64,128]{1,0:T(8,128)S(1)}, u32[]{:S(2)}) copy-start(f32[64,128]{1,0:T(8,128)S(1)} %get-tuple-element.13.spec_ref) | copy-start | bytes 98308
  51.5 15.1 %all-to-all-start.3 = ((f32[16,16,128]{2,1,0:T(8,128)}), f32[16,16,128]{2,1,0:T(8,128)S(1)}, u32[]{:S(2)}, u32[]{:S(2)}) async-start(f32[16,16,128]{2,1,0:T(8,128)} %bitcast.11), calls=%async_computation.3 | async-start | bytes 262144 | tf_op jit(solution)/shard_map/all_to_all | solution.py:425
  58.0 51.2 %copy-start.8 = (f32[64,24]{1,0:T(8,128)S(1)}, f32[64,24]{1,0:T(8,128)}, u32[]{:S(2)}) copy-start(f32[64,24]{1,0:T(8,128)} %constant.39.clone.table_ref) | copy-start | bytes 18436
  80.9 0.7 copy-start.10
  91.9 0.8 copy-start.12
  92.7 0.8 copy-start.15
  93.4 0.7 copy-start.16
  105.2 9.5 %all-to-all-start.8 = ((f32[4,128,128]{2,1,0:T(8,128)}), f32[4,128,128]{2,1,0:T(8,128)S(1)}, u32[]{:S(2)}, u32[]{:S(2)}) async-start(f32[4,128,128]{2,1,0:T(8,128)} %bitcast.33), calls=%async_computation.8 | async-start | bytes 524288 | tf_op jit(solution)/shard_map/all_to_all | solution.py:425
  114.8 16.0 %all-to-all-start.7 = ((f32[16,16,128]{2,1,0:T(8,128)}), f32[16,16,128]{2,1,0:T(8,128)S(1)}, u32[]{:S(2)}, u32[]{:S(2)}) async-start(f32[16,16,128]{2,1,0:T(8,128)} %bitcast.28), calls=%async_computation.7 | async-start | bytes 262144 | tf_op jit(solution)/shard_map/all_to_all | solution.py:425

commit v2 on v1

v2 whole, which is shorter than its diff:
```python
import functools
import math

import jax
import jax.numpy as jnp
import numpy as np
from jax import lax
from jax.experimental import pallas as pl
from jax.experimental.pallas import tpu as pltpu
from jax.sharding import PartitionSpec as P


C = 20
NX, NY, NR = 4, 2, 512
GX, GY = 8, 16
S6 = 6
KX = 12
F32 = jnp.float32
VMEM = pltpu.VMEM
INV_CELLS = 1.0 / (32 * 32 * 512)
INTERPRET = False


def freq(i, n):
    return i if i < n // 2 else i - n


def z_table():
    r = np.arange(NR)
    z, t = r // 8, r % 8
    out = np.zeros((S6, 2, GY, NR))
    for s in range(S6):
        for j in range(GY):
            m = 6 * j + s
            kz, kt = freq(m // 8, 12), freq(m % 8, 8)
            w = (kz * z * 8 + kt * t * 64) % 512
            ang = w * (2.0 * math.pi / 512)
            out[s, 0, j] = np.cos(ang)
            out[s, 1, j] = -np.sin(ang)
    return out.reshape(S6 * 2 * GY, NR).astype(np.float32)


def split_table(table, axis):
    high = table.astype(jnp.bfloat16)
    low = (table - high.astype(np.float32)).astype(jnp.bfloat16)
    return np.concatenate([high, low], axis=axis)


COS = [(-1) ** i * math.pi ** (2 * i) / math.factorial(2 * i) for i in range(11)]
SIN = [(-1) ** i * math.pi ** (2 * i + 1) / math.factorial(2 * i + 1) for i in range(11)]


def rotation(mode, cell, part_out, part_in, sign, scale):
    k = jnp.where(mode >= 6, mode - 12, mode)
    turns = (((k * cell + 16) & 31) - 16).astype(F32) * (1.0 / 16)
    u = turns * turns
    cos = jnp.full_like(u, COS[-1])
    sin = jnp.full_like(u, SIN[-1])
    for i in range(len(COS) - 2, -1, -1):
        cos = cos * u + COS[i]
        sin = sin * u + SIN[i]
    sin = sin * turns * sign
    value = jnp.where(part_out == part_in, cos, jnp.where(part_out == 1, sin, -sin))
    return value * scale if scale != 1.0 else value


def row_col(rows, cols):
    shape = (rows, cols)
    return lax.broadcasted_iota(jnp.int32, shape, 0), lax.broadcasted_iota(jnp.int32, shape, 1)


def y_forward():
    row, col = row_col(48, 64)
    part = (row >= 24).astype(jnp.int32)
    rest = row - 24 * part
    mode = 3 * (rest & 7) + (rest >> 3)
    return rotation(mode, 2 * (col & 15) + (col >> 5), part, (col >> 4) & 1, -1.0, 1.0)


def y_inverse():
    row, col = row_col(64, 24)
    part = (col >= 12).astype(jnp.int32)
    rest = col - 12 * part
    mode = 3 * (rest & 3) + (rest >> 2)
    return rotation(mode, 2 * (row & 15) + (row >> 5), (row >> 4) & 1, part, 1.0, 1.0)


def x_forward(scale):
    row, col = row_col(32, 64)
    return rotation(row & 15, col >> 1, row >> 4, col & 1, -1.0, scale)


def x_inverse(scale):
    row, col = row_col(64, 32)
    return rotation(col & 15, row >> 1, row & 1, col >> 4, 1.0, scale)


def call(body, outs, *args, scratch=(), smem=(), hbm=(), vmem=16 << 20, flops=10**7):
    specs = [
        pl.BlockSpec(memory_space=pltpu.SMEM if i in smem else pltpu.HBM if i in hbm else VMEM)
        for i in range(len(args))
    ]
    shapes = [jax.ShapeDtypeStruct(s, F32) for s in outs]
    nbytes = 4 * sum(math.prod(s) for s in outs) + sum(a.size * a.dtype.itemsize for a in args)
    got = pl.pallas_call(
        body,
        out_shape=shapes,
        in_specs=specs,
        out_specs=[pl.BlockSpec(memory_space=VMEM)] * len(outs),
        scratch_shapes=list(scratch),
        compiler_params=pltpu.CompilerParams(vmem_limit_bytes=vmem),
        cost_estimate=pl.CostEstimate(flops=flops, bytes_accessed=nbytes, transcendentals=0),
        interpret=INTERPRET,
    )(*args)
    return got if len(outs) > 1 else got[0]


def halves(a):
    high = a.astype(jnp.bfloat16)
    return high, (a - high.astype(F32)).astype(jnp.bfloat16)


def dot(a, b, dims=((1,), (0,))):
    ah, al = a if isinstance(a, tuple) else halves(a)
    bh, bl = b if isinstance(b, tuple) else halves(b)

    def one(x, y):
        return lax.dot_general(x, y, (dims, ((), ())), preferred_element_type=F32)

    return one(ah, bh) + (one(ah, bl) + one(al, bh))


def pair(ref):
    rows = ref.shape[0] // 2
    return ref[:rows, :], ref[rows:, :]


def lanes(rows):
    return lax.broadcasted_iota(jnp.int32, (rows, 128), 1)


def load_cells(ref, x, y):
    return jnp.concatenate(
        [ref[pl.ds(x * 8 + tile * 2 + y, C, stride=32), :] for tile in range(4)], axis=1
    )


def store_cells(ref, x, y, value):
    for tile in range(4):
        ref[pl.ds(x * 8 + tile * 2 + y, C, stride=32), :] = value[:, tile * 128 : tile * 128 + 128]


def emit_depth(modes, send_ref):
    lane = lanes(GY)
    for y in range(NY):
        for x in range(NX):
            for part in range(2):
                total = jnp.zeros((GY, 128), F32)
                for s in range(S6):
                    at = (s * 2 + part) * GY
                    piece = modes[at : at + GY, y * 128 : y * 128 + 128]
                    shift = (20 * s - 32 * x) % 128
                    if shift:
                        piece = pltpu.roll(piece, shift, axis=1)
                    total = jnp.where((lane >= 20 * s) & (lane < 20 * s + 20), piece, total)
                send_ref[pl.ds(x * 4 + y * 2 + part, GY, stride=16), :] = total


def gather_depth(recv_ref, modes_ref):
    lane = lanes(GY)
    for y in range(NY):
        for part in range(2):
            pieces = [recv_ref[pl.ds(x * 4 + y * 2 + part, GY, stride=16), :] for x in range(NX)]
            for s in range(S6):
                total = jnp.zeros((GY, 128), F32)
                for x in range(NX):
                    shift = (32 * x - 20 * s) % 128
                    piece = pltpu.roll(pieces[x], shift, axis=1) if shift else pieces[x]
                    total = jnp.where((lane >= 32 * x) & (lane < 32 * x + 20), piece, total)
                at = (s * 2 + part) * GY
                modes_ref[at : at + GY, y * 128 : y * 128 + 128] = total
    return modes_ref[...]


def cell_rows():
    for y in range(NY):
        for x in range(NX):
            yield x, y, (y * NX + x) * 32


def depth_forward(fields_hbm, table_hbm, send_ref, fields_ref, table_ref, stage_ref, sems):
    fields_copy = pltpu.make_async_copy(fields_hbm, fields_ref, sems.at[0])
    table_copy = pltpu.make_async_copy(table_hbm, table_ref, sems.at[1])
    fields_copy.start()
    table_copy.start()
    stage_ref[...] = jnp.zeros_like(stage_ref)
    fields_copy.wait()
    for x, y, at in cell_rows():
        stage_ref[at : at + C, :] = load_cells(fields_ref, x, y)
    table_copy.wait()
    emit_depth(dot(pair(table_ref), stage_ref[...], ((1,), (1,))), send_ref)


def y_spectrum(recv_ref, send_ref):
    columns = []
    for x in range(NX):
        columns.append(
            jnp.concatenate(
                [recv_ref[pl.ds(x * 4 + row, GY, stride=16), :] for row in range(4)], axis=0
            )
        )
    turned = dot(y_forward(), jnp.concatenate(columns, axis=1))
    for x in range(NX):
        for part in range(2):
            row = x * 2 + part
            t0, t1, t2 = [
                turned[part * 24 + t * 8 : part * 24 + t * 8 + 8, x * 128 : x * 128 + 128] for t in range(3)
            ]
            send_ref[pl.ds(row, 4, stride=32), :] = t0[:4]
            send_ref[pl.ds(8 + row, 4, stride=32), :] = t1[:4]
            send_ref[pl.ds(16 + row, 4, stride=32), :] = t2[:4]
            send_ref[pl.ds(24 + row, 4, stride=32), :] = pltpu.roll(t1, 68, axis=1)[:4]


def y_cells(recv_ref, send_ref, stage_ref):
    lane = lanes(4)
    for x in range(NX):
        for part in range(2):
            row = x * 2 + part
            t0, low, t2, high = [recv_ref[pl.ds(slot * 8 + row, 4, stride=32), :] for slot in range(4)]
            at = part * 12
            cut = slice(x * 128, x * 128 + 128)
            stage_ref[at : at + 4, cut] = t0
            stage_ref[at + 4 : at + 8, cut] = jnp.where(lane < 60, low, pltpu.roll(high, 60, axis=1))
            stage_ref[at + 8 : at + 12, cut] = t2
    cells = dot(y_inverse(), stage_ref[...])
    for x in range(NX):
        for row in range(4):
            send_ref[pl.ds(x * 4 + row, GY, stride=16), :] = cells[
                row * 16 : row * 16 + 16, x * 128 : x * 128 + 128
            ]


def x_spectrum(recv_ref, scale):
    found = []
    table = halves(x_forward(scale))
    for tile in range(2):
        data = jnp.concatenate(
            [recv_ref[src * 16 + tile * 8 : src * 16 + tile * 8 + 8, :] for src in range(GX)], axis=0
        )
        found.append(dot(table, data))
    return found


def slots(odd):
    for s in range(6):
        yield 0, s, s + 3 * odd
    for s in range(3):
        yield 1, s, s + 6 * (1 - odd)


def x_cells(mixed, scale, send_ref):
    table = halves(x_inverse(scale))
    for tile in range(2):
        cells = dot(table, mixed[tile])
        for g in range(GX):
            send_ref[g * 16 + tile * 8 : g * 16 + tile * 8 + 8, :] = cells[g * 8 : g * 8 + 8, :]


def weight_row(pair, c):
    return pl.ds(pair * (KX * C) + c, KX, stride=C)


def packed_row(part, c, tile):
    at = ((part * C + c) * 2 + tile) * 16
    return slice(at, at + 16)


def prepare(odd_ref, weight_ref, fields_ref, cotangent_ref, map_ref, packed_ref, direct_ref, cotangent_t_ref, stage_ref):
    pack_weights(odd_ref, weight_ref, packed_ref)
    stage_ref[...] = jnp.zeros_like(stage_ref)
    for x, y, at in cell_rows():
        stage_ref[at : at + C, :] = dot(map_ref[...], load_cells(fields_ref, x, y))
    direct_ref[...] = stage_ref[...].T
    for x, y, at in cell_rows():
        stage_ref[at : at + C, :] = load_cells(cotangent_ref, x, y)
    cotangent_t_ref[...] = stage_ref[...].T


def pack_weights(odd_ref, weight_ref, packed_ref):
    odd = odd_ref[0]
    packed_ref[...] = jnp.zeros_like(packed_ref)
    for tile, s, pair in slots(odd):
        for part in range(2):
            for c in range(C):
                at = packed_row(part, c, tile).start
                packed_ref[at : at + KX, 20 * s : 20 * s + C] = weight_ref[weight_row(9 * part + pair, c), :]


def group_start():
    lane = lanes(16)
    return jnp.right_shift(lane * 205, 12) * 20


def pick(a, index):
    return jnp.take_along_axis(a, index, axis=1, mode="promise_in_bounds")


def x_mix(recv_ref, packed_ref, send_ref, spec_ref):
    spectrum = x_spectrum(recv_ref, 1.0)
    start = group_start()
    mixed = []
    for tile in range(2):
        spec_ref[tile * 32 : tile * 32 + 32, :] = spectrum[tile]
        real, imag = spectrum[tile][:16], spectrum[tile][16:]
        out_real = jnp.zeros((16, 128), F32)
        out_imag = jnp.zeros((16, 128), F32)
        for c in range(C):
            index = jnp.minimum(start + c, 127)
            sr, si = pick(real, index), pick(imag, index)
            wr = packed_ref[packed_row(0, c, tile), :]
            wi = packed_ref[packed_row(1, c, tile), :]
            out_real = out_real + (sr * wr - si * wi)
            out_imag = out_imag + (sr * wi + si * wr)
        mixed.append(jnp.concatenate([out_real, out_imag], axis=0))
    x_cells(mixed, INV_CELLS, send_ref)


def x_unmix(recv_ref, spec_ref, packed_ref, share_ref, send_ref, high_ref, low_ref):
    share_ref[:64, :] = spec_ref[...]
    spectrum = x_spectrum(recv_ref, INV_CELLS)
    for tile in range(2):
        share_ref[64 + tile * 32 : 96 + tile * 32, :] = spectrum[tile]
        dr, di = spectrum[tile][:16], spectrum[tile][16:]
        for c in range(C):
            wr = packed_ref[packed_row(0, c, tile), :]
            wi = packed_ref[packed_row(1, c, tile), :]
            for part, term in enumerate((dr * wr + di * wi, di * wr - dr * wi)):
                high, low = halves(term)
                at = c * 64 + (tile * 2 + part) * 16
                high_ref[at : at + 16, :] = high
                low_ref[at : at + 16, :] = low
    row, col = row_col(128, 128)
    first = jnp.right_shift(row * 205, 12) * 20
    sums = ((col == first) & (row < 120)).astype(F32).astype(jnp.bfloat16)
    found = jnp.dot(high_ref[...], sums, preferred_element_type=F32) + jnp.dot(
        low_ref[...], sums, preferred_element_type=F32
    )
    back = found[:64]
    for c in range(1, C):
        back = back + pltpu.roll(found[c * 64 : c * 64 + 64], c, axis=1)
    x_cells([back[:32], back[32:]], 1.0, send_ref)


def weight_grad(odd_ref, share_refs, grad_ref):
    odd = odd_ref[0]
    start = group_start()
    owned = list(slots(odd))
    for tile in range(2):
        spec, dual = [], []
        for share_ref in share_refs:
            at = tile * 32
            spec.append([share_ref[at + p * 16 : at + p * 16 + 16, :] for p in range(2)])
            dual.append([share_ref[at + 64 + p * 16 : at + 80 + p * 16, :] for p in range(2)])
        for c in range(C):
            index = jnp.minimum(start + c, 127)
            real = jnp.zeros((16, 128), F32)
            imag = jnp.zeros((16, 128), F32)
            for (er, ei), (dr, di) in zip(spec, dual):
                sr, si = pick(er, index), pick(ei, index)
                real = real + (sr * dr + si * di)
                imag = imag + (sr * di - si * dr)
            for where, s, pair in owned:
                if where == tile:
                    grad_ref[weight_row(pair, c), :] = real[:KX, 20 * s : 20 * s + C]
                    grad_ref[weight_row(9 + pair, c), :] = imag[:KX, 20 * s : 20 * s + C]


def side(odd_ref, map_ref, signal_ref, value_ref, *refs):
    share_refs, (out_ref, direct_ref, grad_ref, stage_ref) = refs[:-4], refs[-4:]
    stage_ref[...] = value_ref[...].T
    for x, y, at in cell_rows():
        store_cells(out_ref, x, y, stage_ref[at : at + C, :])
    stage_ref[...] = signal_ref[...].T
    mapping = halves(map_ref[...])
    for _, _, at in cell_rows():
        direct_ref[at : at + C, :] = dot(mapping, stage_ref[at : at + C, :])
        direct_ref[at + C : at + 32, :] = jnp.zeros((32 - C, NR), F32)
    weight_grad(odd_ref, share_refs, grad_ref)


def activate(recv_ref, turned_ref, table_ref, direct_ref, cotangent_ref, value_ref, signal_ref, send_ref, modes_ref):
    high, low = halves(gather_depth(recv_ref, modes_ref))
    both = jnp.concatenate([high, high], axis=0)
    value_ref[...] = (
        jnp.dot(turned_ref[...], both, preferred_element_type=F32)
        + jnp.dot(turned_ref[:, :192], low, preferred_element_type=F32)
        + direct_ref[...]
    )
    k = math.sqrt(2.0 / math.pi)
    for at in range(0, NR, 64):
        cut = slice(at, at + 64)
        v = value_ref[cut, :]
        square = v * v
        th = jnp.tanh(k * (v + 0.044715 * (square * v)))
        half = 0.5 * (1.0 + th)
        value_ref[cut, :] = v * half
        slope = half + 0.5 * v * (1.0 - th * th) * (k * (1.0 + 3 * 0.044715 * square))
        signal_ref[cut, :] = slope * cotangent_ref[cut, :]
    emit_depth(dot(pair(table_ref), signal_ref[...]), send_ref)


def finish(recv_ref, table_ref, direct_ref, out_ref, modes_ref):
    modes = halves(gather_depth(recv_ref, modes_ref))
    spectral = dot(modes, pair(table_ref), ((0,), (0,)))
    for x, y, at in cell_rows():
        store_cells(out_ref, x, y, spectral[at : at + C, :] + direct_ref[at : at + C, :])


def as_rows(a):
    return a.reshape(C * NX, NY, 4, 128).transpose(0, 2, 1, 3).reshape(640, 128)


def from_rows(a):
    return a.reshape(C * NX, 4, NY, 128).transpose(0, 2, 1, 3).reshape(1, C, NX, NY, NR)


CELLS = (256, NR)
TURNED = (NR, 256)
ROWS = (640, 128)
SEND_Y = (GY * 16, 128)
SEND_X = (GX * 16, 128)
PACKED = (2 * C * 2 * 16, 128)
SHARE = (128, 128)
BF16 = jnp.bfloat16
DMA = pltpu.SemaphoreType.DMA


def stages():
    base = z_table()
    tz, tz_turned = split_table(base, 0), split_table(base.T.copy(), 1)
    modes = [VMEM((192, 256), F32)]
    return dict(
        depth_forward=lambda f: call(
            depth_forward,
            [SEND_Y],
            *(f, tz),
            scratch=[VMEM(ROWS, F32), VMEM(tz.shape, BF16), VMEM(CELLS, F32), DMA((2,))],
            hbm=(0, 1),
            vmem=66_353_664,
        ),
        prepare=lambda o, w, f, ct, b: call(
            prepare, [PACKED, TURNED, TURNED], o, w, f, ct, b, scratch=[VMEM(CELLS, F32)], smem=(0,)
        ),
        y_spectrum=lambda r: call(y_spectrum, [SEND_X], r),
        y_cells=lambda r: call(y_cells, [SEND_Y], r, scratch=[VMEM((24, 512), F32)]),
        x_mix=lambda r, w: call(x_mix, [SEND_X, (64, 128)], r, w),
        x_unmix=lambda r, s, w: call(x_unmix, [SHARE, SEND_X], *(r, s, w), scratch=[VMEM((64 * C, 128), BF16)] * 2),
        side=lambda o, b, sig, val, *shares: call(
            side, [ROWS, CELLS, (2 * 9 * KX * C, C)], *(o, b, sig, val, *shares), scratch=[VMEM(CELLS, F32)], smem=(0,)
        ),
        activate=lambda r, d, ct: call(activate, [TURNED, TURNED, SEND_Y], r, tz_turned, tz, d, ct, scratch=modes),
        finish=lambda r, d: call(finish, [ROWS], r, tz, d, scratch=modes),
    )


def swap(a, axis, n):
    rows = a.shape[0] // n
    return lax.all_to_all(
        a.reshape(n, rows, 128), axis, split_axis=0, concat_axis=0, tiled=True
    ).reshape(n * rows, 128)


def on_device(fields, cotangent, spectral, bypass):
    samples = lax.axis_size("dp")
    st = stages()
    odd = (lax.axis_index("gx") & 1).astype(jnp.int32).reshape(1)
    rows = as_rows(fields)
    weights = spectral.reshape(2 * 9 * KX * C, C)
    to_y = functools.partial(swap, axis="gy", n=GY)
    to_x = functools.partial(swap, axis="gx", n=GX)
    sent = st["y_spectrum"](to_y(st["depth_forward"](rows)))
    packed, direct, turned = st["prepare"](odd, weights, rows, as_rows(cotangent), bypass.T)
    mixed, spec = st["x_mix"](to_x(sent), packed)
    arrived = to_y(st["y_cells"](to_x(mixed)))
    value, signal, sent = st["activate"](arrived, direct, turned)
    share, sent = st["x_unmix"](to_x(st["y_spectrum"](to_y(sent))), spec, packed)
    arrived = to_x(sent)
    shares = [share]
    for step in range(1, samples):
        shares.append(lax.ppermute(share, "dp", [(i, (i + step) % samples) for i in range(samples)]))
    arrived, *shares = lax.optimization_barrier((arrived, *shares))
    output, direct, grad = st["side"](odd, bypass, signal, value, *shares)
    field_grad = st["finish"](to_y(st["y_cells"](arrived)), direct)
    return (from_rows(output), from_rows(field_grad), grad.reshape(spectral.shape))


def solution(mesh):
    cells = P("dp", None, "gx", "gy", None)
    modes = P(None, "gx", "gy", None, None, None)
    return jax.shard_map(
        on_device,
        mesh=mesh,
        in_specs=(cells, cells, modes, P()),
        out_specs=(cells, cells, modes),
        check_vma=False,
    )
```

time: 134 us -> 125 us (0.933)
  waiting for transfers between devices: 21.3 us -> 6.98 us
  blocking collectives: 61 us -> 67.9 us
  starting transfers between devices: 23.7 us -> 26.9 us
  local copies, waits for them, and re-layouts: 7.43 us -> 4.37 us
    all_to_all x4 -> x3, waiting for transfers between devices: 21.3 us -> 5.06 us  [swap(): lax.all_to_all(a.reshape(n, rows, 128), axis, split_axis=0, concat_axis=0...]
    ppermute x0 -> x3, starting transfers between devices: none -> 10.5 us  [on_device(): lax.ppermute(share, 'dp', [(i, (i + step) % samples) for i in range(sampl...]
    all_to_all x4 -> x3, starting transfers between devices: 23.7 us -> 16.4 us  [swap(): lax.all_to_all(a.reshape(n, rows, 128), axis, split_axis=0, concat_axis=0...]
    all_to_all x5, blocking collectives: 61 us -> 67.9 us  [swap(): lax.all_to_all(a.reshape(n, rows, 128), axis, split_axis=0, concat_axis=0...]
    unnamed x37 -> x13, local copies, waits for them, and re-layouts: 7.43 us -> 4.37 us
    ppermute x0 -> x3, waiting for transfers between devices: none -> 1.92 us  [on_device(): lax.ppermute(share, 'dp', [(i, (i + step) % samples) for i in range(sampl...]
    pallas_call x13 -> x11, Pallas kernels: 18.3 us -> 17.3 us  [call(): pl.pallas_call(body, out_shape=shapes, in_specs=specs, out_specs=[pl.Bloc...]
  transfers between devices with their start and end apart: 4 -> 6, of which waited for: 4 -> 3; matrix products, arithmetic and copies ran while one was open for 0% -> 1% of each run, Pallas kernels for 6% -> 6%
where the time goes in v2:
time: 125 us; the launch traced here: 124 us
  blocking collectives  67.9 us (54%)
  starting transfers between devices  26.9 us (22%)
  Pallas kernels  17.3 us (14%)
  waiting for transfers between devices  6.98 us (6%)
  local copies, waits for them, and re-layouts  4.37 us (3%)
    all_to_all x5, blocking collectives, swap(): lax.all_to_all(a.reshape(n, rows, 128), axis, split_axis=0, concat_axis=0...  67.9 us
    pallas_call x11, Pallas kernels, call(): pl.pallas_call(body, out_shape=shapes, in_specs=specs, out_specs=[pl.Bloc...  17.3 us
    all_to_all x3, starting transfers between devices, swap(): lax.all_to_all(a.reshape(n, rows, 128), axis, split_axis=0, concat_axis=0...  16.4 us
    ppermute x3, starting transfers between devices, on_device(): lax.ppermute(share, 'dp', [(i, (i + step) % samples) for i in range(sampl...  10.5 us
    all_to_all x3, waiting for transfers between devices, swap(): lax.all_to_all(a.reshape(n, rows, 128), axis, split_axis=0, concat_axis=0...  5.06 us
    unnamed x13, local copies, waits for them, and re-layouts  4.37 us
  transfers between devices with their start and end apart: 6, of which 3 were waited for; matrix products, arithmetic and copies ran while one was open for 1% of the time, Pallas kernels for 6%

profile of v2, /device:TPU:1, one launch (start us, length us, event | category | flops | bytes accessed | tf_op | source)
XLA Modules:
  0.0 124.1 jit_solution(14373426522812436192)
XLA Ops:
  0.6 2.5 %shard_map.85 = f32[256,128]{1,0:T(8,128)} custom-call(f32[640,128]{1,0:T(8,128)} %bitcast.41, bf16[384,512]{1,0:T(8,128)(2,1)} %constant.12.clone.table_hbm.table_ref), custom_call_target="tpu_custom_call" | custom-call | flops 10000000 | bytes 851968 | tf_op jit(solution)/shard_map/pallas_call | solution.py:105
  3.1 0.0 copy-start.3
  3.1 20.8 %all_to_all.40 = f32[16,16,128]{2,1,0:T(8,128)S(1)} all-to-all(f32[16,16,128]{2,1,0:T(8,128)} %bitcast.57), channel_id=1, replica_groups=mesh['dp'=4,'gx'=8,'gy'=16] {'gy'}, dimensions={0} | all-to-all | bytes 262144 | tf_op jit(solution)/shard_map/all_to_all | solution.py:469
  24.0 1.0 shard_map.86
  24.9 0.0 copy-start
  24.9 7.0 %all-to-all-start.1 = ((f32[8,16,128]{2,1,0:T(8,128)}), f32[8,16,128]{2,1,0:T(8,128)S(1)}, u32[]{:S(2)}, u32[]{:S(2)}) async-start(f32[8,16,128]{2,1,0:T(8,128)} %bitcast.6), calls=%async_computation.1 | async-start | bytes 131072 | tf_op jit(solution)/shard_map/all_to_all | solution.py:469
  31.9 0.8 copy.17
  32.7 0.0 copy-start.1
  32.7 1.6 %copy-done.1 = f32[2,9,1,12,20,20]{5,2,4,3,1,0:T(1,128)S(1)} copy-done((f32[2,9,1,12,20,20]{5,2,4,3,1,0:T(1,128)S(1)}, f32[2,9,1,12,20,20]{5,2,4,3,1,0:T(1,128)}, u32[]{:S(2)}) %copy-start.1) | copy-done | bytes 345624
  34.3 0.0 copy-start.2
  34.3 1.0 copy-done.2
  35.3 0.0 copy-start.4
  35.3 1.0 copy-done.4
  36.2 1.1 shard_map.87
  37.3 1.7 %all-to-all-done.1 = f32[8,16,128]{2,1,0:T(8,128)S(1)} async-done(((f32[8,16,128]{2,1,0:T(8,128)}), f32[8,16,128]{2,1,0:T(8,128)S(1)}, u32[]{:S(2)}, u32[]{:S(2)}) %all-to-all-start.1) | async-done | bytes 65568 | tf_op jit(solution)/shard_map/all_to_all | solution.py:469
  39.0 0.8 shard_map.88
  39.8 12.0 %all_to_all.41 = f32[8,16,128]{2,1,0:T(8,128)S(1)} all-to-all(f32[8,16,128]{2,1,0:T(8,128)S(1)} %bitcast.55), channel_id=1, replica_groups=mesh['dp'=4,'gx'=8,'gy'=16] {'gx'}, dimensions={0} | all-to-all | bytes 131072 | tf_op jit(solution)/shard_map/all_to_all | solution.py:469
  51.8 0.0 copy-start.5
  51.8 0.3 shard_map.89
  52.1 13.5 %all_to_all.42 = f32[16,16,128]{2,1,0:T(8,128)S(1)} all-to-all(f32[16,16,128]{2,1,0:T(8,128)S(1)} %bitcast.44), channel_id=1, replica_groups=mesh['dp'=4,'gx'=8,'gy'=16] {'gy'}, dimensions={0} | all-to-all | bytes 262144 | tf_op jit(solution)/shard_map/all_to_all | solution.py:469
  65.7 0.0 copy-done.3
  65.7 0.0 copy-done
  65.7 1.6 %shard_map.90 = (f32[512,256]{1,0:T(8,128)S(1)}, f32[512,256]{1,0:T(8,128)S(1)}, f32[256,128]{1,0:T(8,128)S(1)}) custom-call(f32[256,128]{1,0:T(8,128)S(1)} %bitcast.47, bf16[512,384]{1,0:T(8,128)(2,1)S(1)} %copy-done.3, bf16[384,512]{1,0:T(8,128)(2,1)S(1)} %copy-done, f32[512,256]{1,0:T(8,128)S(1)} %get-tuple-element.23.direct_ref, ...), custom_call_target="tpu_custom_call" | custom-call | flops 10000000 | bytes 3145728 | tf_op jit(solution)/shard_map/pallas_call | solution.py:105
  67.3 11.6 %all_to_all.43 = f32[16,16,128]{2,1,0:T(8,128)S(1)} all-to-all(f32[16,16,128]{2,1,0:T(8,128)S(1)} %bitcast.54), channel_id=1, replica_groups=mesh['dp'=4,'gx'=8,'gy'=16] {'gy'}, dimensions={0} | all-to-all | bytes 262144 | tf_op jit(solution)/shard_map/all_to_all | solution.py:469
  78.8 0.3 shard_map.91
  79.2 9.9 %all_to_all.44 = f32[8,16,128]{2,1,0:T(8,128)S(1)} all-to-all(f32[8,16,128]{2,1,0:T(8,128)S(1)} %bitcast.52), channel_id=1, replica_groups=mesh['dp'=4,'gx'=8,'gy'=16] {'gx'}, dimensions={0} | all-to-all | bytes 131072 | tf_op jit(solution)/shard_map/all_to_all | solution.py:469
  89.1 1.4 %shard_map.92 = (f32[128,128]{1,0:T(8,128)S(1)}, f32[128,128]{1,0:T(8,128)}) custom-call(f32[128,128]{1,0:T(8,128)S(1)} %bitcast.50, f32[64,128]{1,0:T(8,128)S(1)} %get-tuple-element.28.spec_ref, f32[1280,128]{1,0:T(8,128)S(1)} %get-tuple-element.21.packed_ref), custom_call_target="tpu_custom_call" | custom-call | flops 10000000 | bytes 884736 | tf_op jit(solution)/shard_map/pallas_call | solution.py:105
  90.5 3.4 %all-to-all-start.6 = ((f32[8,16,128]{2,1,0:T(8,128)}), f32[8,16,128]{2,1,0:T(8,128)S(1)}, u32[]{:S(2)}, u32[]{:S(2)}) async-start(f32[8,16,128]{2,1,0:T(8,128)} %bitcast.23), calls=%async_computation.6 | async-start | bytes 131072 | tf_op jit(solution)/shard_map/all_to_all | solution.py:469
  93.9 3.1 %collective-permute-start = (f32[128,128]{1,0:T(8,128)S(1)}, f32[128,128]{1,0:T(8,128)S(1)}, u32[]{:S(2)}, u32[]{:S(2)}) collective-permute-start(f32[128,128]{1,0:T(8,128)S(1)} %get-tuple-element.31.refs_0_), channel_id=1, source_target_pairs={{0,128},{128,256},{256,384},{384,0},{1,129},{129,257},{257,385},{3... | collective-permute-start | bytes 196616 | tf_op jit(solution)/shard_map/ppermute | solution.py:491
  97.0 4.4 %collective-permute-start.1 = (f32[128,128]{1,0:T(8,128)S(1)}, f32[128,128]{1,0:T(8,128)S(1)}, u32[]{:S(2)}, u32[]{:S(2)}) collective-permute-start(f32[128,128]{1,0:T(8,128)S(1)} %get-tuple-element.31.refs_0_), channel_id=1, source_target_pairs={{0,256},{128,384},{256,0},{384,128},{1,257},{129,385},{257,1},{385... | collective-permute-start | bytes 196616 | tf_op jit(solution)/shard_map/ppermute | solution.py:491
  101.4 3.1 %collective-permute-start.2 = (f32[128,128]{1,0:T(8,128)S(1)}, f32[128,128]{1,0:T(8,128)S(1)}, u32[]{:S(2)}, u32[]{:S(2)}) collective-permute-start(f32[128,128]{1,0:T(8,128)S(1)} %get-tuple-element.31.refs_0_), channel_id=1, source_target_pairs={{0,384},{128,0},{256,128},{384,256},{1,385},{129,1},{257,129},{385... | collective-permute-start | bytes 196616 | tf_op jit(solution)/shard_map/ppermute | solution.py:491
  104.4 0.0 collective-permute-done.refs_1_
  104.4 0.0 collective-permute-done.1.refs_2_
  104.5 1.9 %collective-permute-done.2.refs_3_ = f32[128,128]{1,0:T(8,128)S(1)} collective-permute-done((f32[128,128]{1,0:T(8,128)S(1)}, f32[128,128]{1,0:T(8,128)S(1)}, u32[]{:S(2)}, u32[]{:S(2)}) %collective-permute-start.2) | collective-permute-done | bytes 65568 | tf_op jit(solution)/shard_map/ppermute | solution.py:491
  106.4 0.0 all-to-all-done.6
  106.4 1.0 shard_map.94
  107.3 6.0 %all-to-all-start.7 = ((f32[16,16,128]{2,1,0:T(8,128)}), f32[16,16,128]{2,1,0:T(8,128)S(1)}, u32[]{:S(2)}, u32[]{:S(2)}) async-start(f32[16,16,128]{2,1,0:T(8,128)} %bitcast.28), calls=%async_computation.7 | async-start | bytes 262144 | tf_op jit(solution)/shard_map/all_to_all | solution.py:469
  113.4 0.0 copy-done.5
  113.4 5.8 %shard_map.93 = (f32[640,128]{1,0:T(8,128)}, f32[256,512]{1,0:T(8,128)S(1)}, f32[4320,20]{1,0:T(8,128)}) custom-call(s32[1]{0:T(128)} %bitcast.odd_ref, f32[20,20]{1,0:T(8,128)S(1)} %copy-done.5, f32[512,256]{1,0:T(8,128)S(1)} %get-tuple-element.25.signal_ref, f32[512,256]{1,0:T(8,128)S(1)} %get-tuple-element.26.value_ref, ...), custom_call_target="tpu_custom_call" | custom-call | flops 10000000 | bytes 2509892 | tf_op jit(solution)/shard_map/pallas_call | solution.py:105
  119.2 3.3 %all-to-all-done.7 = f32[16,16,128]{2,1,0:T(8,128)S(1)} async-done(((f32[16,16,128]{2,1,0:T(8,128)}), f32[16,16,128]{2,1,0:T(8,128)S(1)}, u32[]{:S(2)}, u32[]{:S(2)}) %all-to-all-start.7) | async-done | bytes 131104 | tf_op jit(solution)/shard_map/all_to_all | solution.py:469
  122.6 1.5 %shard_map.95 = f32[640,128]{1,0:T(8,128)} custom-call(f32[256,128]{1,0:T(8,128)S(1)} %bitcast.46, bf16[384,512]{1,0:T(8,128)(2,1)S(1)} %copy-done, f32[256,512]{1,0:T(8,128)S(1)} %get-tuple-element.37.direct_ref), custom_call_target="tpu_custom_call" | custom-call | flops 10000000 | bytes 1376256 | tf_op jit(solution)/shard_map/pallas_call | solution.py:105
Async XLA Ops:
  3.1 62.5 %copy-start.3 = (bf16[512,384]{1,0:T(8,128)(2,1)S(1)}, bf16[512,384]{1,0:T(8,128)(2,1)}, u32[]{:S(2)}) copy-start(bf16[512,384]{1,0:T(8,128)(2,1)} %constant.13.clone.turned_ref) | copy-start | bytes 1179652
  24.9 40.7 %copy-start = (bf16[384,512]{1,0:T(8,128)(2,1)S(1)}, bf16[384,512]{1,0:T(8,128)(2,1)}, u32[]{:S(2)}) copy-start(bf16[384,512]{1,0:T(8,128)(2,1)} %constant.12.clone.table_hbm.table_ref) | copy-start | bytes 1179652
  24.9 14.1 %all-to-all-start.1 = ((f32[8,16,128]{2,1,0:T(8,128)}), f32[8,16,128]{2,1,0:T(8,128)S(1)}, u32[]{:S(2)}, u32[]{:S(2)}) async-start(f32[8,16,128]{2,1,0:T(8,128)} %bitcast.6), calls=%async_computation.1 | async-start | bytes 131072 | tf_op jit(solution)/shard_map/all_to_all | solution.py:469
  32.7 1.6 %copy-start.1 = (f32[2,9,1,12,20,20]{5,2,4,3,1,0:T(1,128)S(1)}, f32[2,9,1,12,20,20]{5,2,4,3,1,0:T(1,128)}, u32[]{:S(2)}) copy-start(f32[2,9,1,12,20,20]{5,2,4,3,1,0:T(1,128)} %param.8) | copy-start | bytes 1036804
  34.3 1.0 copy-start.2
  35.3 1.0 copy-start.4
  51.8 61.6 %copy-start.5 = (f32[20,20]{1,0:T(8,128)S(1)}, f32[20,20]{1,0:T(8,128)}, u32[]{:S(2)}) copy-start(f32[20,20]{1,0:T(8,128)} %map_ref.1) | copy-start | bytes 4804
  90.5 15.9 %all-to-all-start.6 = ((f32[8,16,128]{2,1,0:T(8,128)}), f32[8,16,128]{2,1,0:T(8,128)S(1)}, u32[]{:S(2)}, u32[]{:S(2)}) async-start(f32[8,16,128]{2,1,0:T(8,128)} %bitcast.23), calls=%async_computation.6 | async-start | bytes 131072 | tf_op jit(solution)/shard_map/all_to_all | solution.py:469
  93.9 10.6 %collective-permute-start = (f32[128,128]{1,0:T(8,128)S(1)}, f32[128,128]{1,0:T(8,128)S(1)}, u32[]{:S(2)}, u32[]{:S(2)}) collective-permute-start(f32[128,128]{1,0:T(8,128)S(1)} %get-tuple-element.31.refs_0_), channel_id=1, source_target_pairs={{0,128},{128,256},{256,384},{384,0},{1,129},{129,257},{257,385},{3... | collective-permute-start | bytes 196616 | tf_op jit(solution)/shard_map/ppermute | solution.py:491
  97.0 7.5 %collective-permute-start.1 = (f32[128,128]{1,0:T(8,128)S(1)}, f32[128,128]{1,0:T(8,128)S(1)}, u32[]{:S(2)}, u32[]{:S(2)}) collective-permute-start(f32[128,128]{1,0:T(8,128)S(1)} %get-tuple-element.31.refs_0_), channel_id=1, source_target_pairs={{0,256},{128,384},{256,0},{384,128},{1,257},{129,385},{257,1},{385... | collective-permute-start | bytes 196616 | tf_op jit(solution)/shard_map/ppermute | solution.py:491
  101.4 5.0 %collective-permute-start.2 = (f32[128,128]{1,0:T(8,128)S(1)}, f32[128,128]{1,0:T(8,128)S(1)}, u32[]{:S(2)}, u32[]{:S(2)}) collective-permute-start(f32[128,128]{1,0:T(8,128)S(1)} %get-tuple-element.31.refs_0_), channel_id=1, source_target_pairs={{0,384},{128,0},{256,128},{384,256},{1,385},{129,1},{257,129},{385... | collective-permute-start | bytes 196616 | tf_op jit(solution)/shard_map/ppermute | solution.py:491
  107.3 15.2 %all-to-all-start.7 = ((f32[16,16,128]{2,1,0:T(8,128)}), f32[16,16,128]{2,1,0:T(8,128)S(1)}, u32[]{:S(2)}, u32[]{:S(2)}) async-start(f32[16,16,128]{2,1,0:T(8,128)} %bitcast.28), calls=%async_computation.7 | async-start | bytes 262144 | tf_op jit(solution)/shard_map/all_to_all | solution.py:469

commit v3 on v2

--- a/solution.py
+++ b/solution.py
@@ -278,9 +278,10 @@
 
 def prepare(odd_ref, weight_ref, fields_ref, cotangent_ref, map_ref, packed_ref, direct_ref, cotangent_t_ref, stage_ref):
     pack_weights(odd_ref, weight_ref, packed_ref)
+    mapping = halves(map_ref[...])
     stage_ref[...] = jnp.zeros_like(stage_ref)
     for x, y, at in cell_rows():
-        stage_ref[at : at + C, :] = dot(map_ref[...], load_cells(fields_ref, x, y))
+        stage_ref[at : at + C, :] = dot(mapping, load_cells(fields_ref, x, y), ((0,), (0,)))
     direct_ref[...] = stage_ref[...].T
     for x, y, at in cell_rows():
         stage_ref[at : at + C, :] = load_cells(cotangent_ref, x, y)
@@ -447,7 +448,7 @@
             *(f, tz),
             scratch=[VMEM(ROWS, F32), VMEM(tz.shape, BF16), VMEM(CELLS, F32), DMA((2,))],
             hbm=(0, 1),
-            vmem=66_353_664,
+            vmem=66_313_216,
         ),
         prepare=lambda o, w, f, ct, b: call(
             prepare, [PACKED, TURNED, TURNED], o, w, f, ct, b, scratch=[VMEM(CELLS, F32)], smem=(0,)
@@ -479,19 +480,20 @@
     weights = spectral.reshape(2 * 9 * KX * C, C)
     to_y = functools.partial(swap, axis="gy", n=GY)
     to_x = functools.partial(swap, axis="gx", n=GX)
-    sent = st["y_spectrum"](to_y(st["depth_forward"](rows)))
-    packed, direct, turned = st["prepare"](odd, weights, rows, as_rows(cotangent), bypass.T)
+    arrived = to_y(st["depth_forward"](rows))
+    packed, direct, turned = st["prepare"](odd, weights, rows, as_rows(cotangent), bypass)
+    sent = st["y_spectrum"](arrived)
     mixed, spec = st["x_mix"](to_x(sent), packed)
     arrived = to_y(st["y_cells"](to_x(mixed)))
     value, signal, sent = st["activate"](arrived, direct, turned)
     share, sent = st["x_unmix"](to_x(st["y_spectrum"](to_y(sent))), spec, packed)
     arrived = to_x(sent)
+    sent = st["y_cells"](arrived)
     shares = [share]
     for step in range(1, samples):
         shares.append(lax.ppermute(share, "dp", [(i, (i + step) % samples) for i in range(samples)]))
-    arrived, *shares = lax.optimization_barrier((arrived, *shares))
     output, direct, grad = st["side"](odd, bypass, signal, value, *shares)
-    field_grad = st["finish"](to_y(st["y_cells"](arrived)), direct)
+    field_grad = st["finish"](to_y(sent), direct)
     return (from_rows(output), from_rows(field_grad), grad.reshape(spectral.shape))
 
 

time: 125 us -> 127 us (1.016)
  blocking collectives: 67.9 us -> 77.6 us
  starting transfers between devices: 26.9 us -> 22.9 us
  waiting for transfers between devices: 6.98 us -> 3.64 us
    all_to_all x5 -> x6, blocking collectives: 67.9 us -> 77.6 us  [swap(): lax.all_to_all(a.reshape(n, rows, 128), axis, split_axis=0, concat_axis=0...]
    all_to_all x3 -> x2, starting transfers between devices: 16.4 us -> 12.3 us  [swap(): lax.all_to_all(a.reshape(n, rows, 128), axis, split_axis=0, concat_axis=0...]
    all_to_all x3 -> x2, waiting for transfers between devices: 5.06 us -> 1.71 us  [swap(): lax.all_to_all(a.reshape(n, rows, 128), axis, split_axis=0, concat_axis=0...]
    unnamed x13 -> x14, local copies, waits for them, and re-layouts: 4.37 us -> 4.29 us
  transfers between devices with their start and end apart: 6 -> 5, of which waited for: 3 -> 2; matrix products, arithmetic and copies ran while one was open for 1% -> 0% of each run, Pallas kernels for 6% -> 6%
where the time goes in v3:
time: 127 us; the launch traced here: 126 us
  blocking collectives  77.6 us (61%)
  starting transfers between devices  22.9 us (18%)
  Pallas kernels  16.7 us (13%)
  local copies, waits for them, and re-layouts  4.29 us (3%)
  waiting for transfers between devices  3.64 us (3%)
    all_to_all x6, blocking collectives, swap(): lax.all_to_all(a.reshape(n, rows, 128), axis, split_axis=0, concat_axis=0...  77.6 us
    pallas_call x11, Pallas kernels, call(): pl.pallas_call(body, out_shape=shapes, in_specs=specs, out_specs=[pl.Bloc...  16.7 us
    all_to_all x2, starting transfers between devices, swap(): lax.all_to_all(a.reshape(n, rows, 128), axis, split_axis=0, concat_axis=0...  12.3 us
    ppermute x3, starting transfers between devices, on_device(): lax.ppermute(share, 'dp', [(i, (i + step) % samples) for i in range(sampl...  10.5 us
    unnamed x14, local copies, waits for them, and re-layouts  4.29 us
  transfers between devices with their start and end apart: 5, of which 2 were waited for; matrix products, arithmetic and copies ran while one was open for 0% of the time, Pallas kernels for 6%

profile of v3, /device:TPU:1, one launch (start us, length us, event | category | flops | bytes accessed | tf_op | source)
XLA Modules:
  0.0 125.8 jit_solution(5596077226544663455)
XLA Ops:
  0.6 2.5 %shard_map.85 = f32[256,128]{1,0:T(8,128)} custom-call(f32[640,128]{1,0:T(8,128)} %bitcast.40, bf16[384,512]{1,0:T(8,128)(2,1)} %constant.12.clone.table_hbm.table_ref), custom_call_target="tpu_custom_call" | custom-call | flops 10000000 | bytes 851968 | tf_op jit(solution)/shard_map/pallas_call | solution.py:105
  3.1 0.0 copy-start.3
  3.1 20.8 %all_to_all.40 = f32[16,16,128]{2,1,0:T(8,128)S(1)} all-to-all(f32[16,16,128]{2,1,0:T(8,128)} %bitcast.56), channel_id=1, replica_groups=mesh['dp'=4,'gx'=8,'gy'=16] {'gy'}, dimensions={0} | all-to-all | bytes 262144 | tf_op jit(solution)/shard_map/all_to_all | solution.py:470
  24.0 1.0 shard_map.86
  24.9 0.0 copy-start
  24.9 7.0 %all-to-all-start.1 = ((f32[8,16,128]{2,1,0:T(8,128)}), f32[8,16,128]{2,1,0:T(8,128)S(1)}, u32[]{:S(2)}, u32[]{:S(2)}) async-start(f32[8,16,128]{2,1,0:T(8,128)} %bitcast.6), calls=%async_computation.1 | async-start | bytes 131072 | tf_op jit(solution)/shard_map/all_to_all | solution.py:470
  31.9 0.0 copy-start.1
  31.9 1.6 %copy-done.1 = f32[2,9,1,12,20,20]{5,2,4,3,1,0:T(1,128)S(1)} copy-done((f32[2,9,1,12,20,20]{5,2,4,3,1,0:T(1,128)S(1)}, f32[2,9,1,12,20,20]{5,2,4,3,1,0:T(1,128)}, u32[]{:S(2)}) %copy-start.1) | copy-done | bytes 345624
  33.5 0.0 copy-start.2
  33.5 1.0 copy-done.2
  34.5 0.0 copy-start.4
  34.5 1.0 copy-done.4
  35.5 0.0 copy-start.5
  35.5 0.7 copy-done.5
  36.2 1.2 shard_map.87
  37.3 1.7 %all-to-all-done.1 = f32[8,16,128]{2,1,0:T(8,128)S(1)} async-done(((f32[8,16,128]{2,1,0:T(8,128)}), f32[8,16,128]{2,1,0:T(8,128)S(1)}, u32[]{:S(2)}, u32[]{:S(2)}) %all-to-all-start.1) | async-done | bytes 65568 | tf_op jit(solution)/shard_map/all_to_all | solution.py:470
  39.0 0.8 shard_map.88
  39.8 12.0 %all_to_all.41 = f32[8,16,128]{2,1,0:T(8,128)S(1)} all-to-all(f32[8,16,128]{2,1,0:T(8,128)S(1)} %bitcast.55), channel_id=1, replica_groups=mesh['dp'=4,'gx'=8,'gy'=16] {'gx'}, dimensions={0} | all-to-all | bytes 131072 | tf_op jit(solution)/shard_map/all_to_all | solution.py:470
  51.8 0.0 copy-start.6
  51.8 0.3 shard_map.89
  52.1 13.5 %all_to_all.42 = f32[16,16,128]{2,1,0:T(8,128)S(1)} all-to-all(f32[16,16,128]{2,1,0:T(8,128)S(1)} %bitcast.43), channel_id=1, replica_groups=mesh['dp'=4,'gx'=8,'gy'=16] {'gy'}, dimensions={0} | all-to-all | bytes 262144 | tf_op jit(solution)/shard_map/all_to_all | solution.py:470
  65.7 0.0 copy-done.3
  65.7 0.0 copy-done
  65.7 1.6 %shard_map.90 = (f32[512,256]{1,0:T(8,128)S(1)}, f32[512,256]{1,0:T(8,128)S(1)}, f32[256,128]{1,0:T(8,128)S(1)}) custom-call(f32[256,128]{1,0:T(8,128)S(1)} %bitcast.46, bf16[512,384]{1,0:T(8,128)(2,1)S(1)} %copy-done.3, bf16[384,512]{1,0:T(8,128)(2,1)S(1)} %copy-done, f32[512,256]{1,0:T(8,128)S(1)} %get-tuple-element.18.direct_ref, ...), custom_call_target="tpu_custom_call" | custom-call | flops 10000000 | bytes 3145728 | tf_op jit(solution)/shard_map/pallas_call | solution.py:105
  67.3 11.6 %all_to_all.43 = f32[16,16,128]{2,1,0:T(8,128)S(1)} all-to-all(f32[16,16,128]{2,1,0:T(8,128)S(1)} %bitcast.53), channel_id=1, replica_groups=mesh['dp'=4,'gx'=8,'gy'=16] {'gy'}, dimensions={0} | all-to-all | bytes 262144 | tf_op jit(solution)/shard_map/all_to_all | solution.py:470
  78.8 0.3 shard_map.91
  79.2 9.9 %all_to_all.44 = f32[8,16,128]{2,1,0:T(8,128)S(1)} all-to-all(f32[8,16,128]{2,1,0:T(8,128)S(1)} %bitcast.50), channel_id=1, replica_groups=mesh['dp'=4,'gx'=8,'gy'=16] {'gx'}, dimensions={0} | all-to-all | bytes 131072 | tf_op jit(solution)/shard_map/all_to_all | solution.py:470
  89.1 0.8 shard_map.92
  89.9 9.7 %all_to_all.45 = f32[8,16,128]{2,1,0:T(8,128)S(1)} all-to-all(f32[8,16,128]{2,1,0:T(8,128)S(1)} %bitcast.54), channel_id=1, replica_groups=mesh['dp'=4,'gx'=8,'gy'=16] {'gx'}, dimensions={0} | all-to-all | bytes 131072 | tf_op jit(solution)/shard_map/all_to_all | solution.py:470
  99.6 1.0 shard_map.94
  100.5 5.4 %all-to-all-start.7 = ((f32[16,16,128]{2,1,0:T(8,128)}), f32[16,16,128]{2,1,0:T(8,128)S(1)}, u32[]{:S(2)}, u32[]{:S(2)}) async-start(f32[16,16,128]{2,1,0:T(8,128)} %bitcast.27), calls=%async_computation.7 | async-start | bytes 262144 | tf_op jit(solution)/shard_map/all_to_all | solution.py:470
  105.9 3.1 %collective-permute-start = (f32[128,128]{1,0:T(8,128)S(1)}, f32[128,128]{1,0:T(8,128)S(1)}, u32[]{:S(2)}, u32[]{:S(2)}) collective-permute-start(f32[128,128]{1,0:T(8,128)S(1)} %get-tuple-element.24.refs_0_), channel_id=1, source_target_pairs={{0,128},{128,256},{256,384},{384,0},{1,129},{129,257},{257,385},{3... | collective-permute-start | bytes 196616 | tf_op jit(solution)/shard_map/ppermute | solution.py:494
  109.1 4.4 %collective-permute-start.1 = (f32[128,128]{1,0:T(8,128)S(1)}, f32[128,128]{1,0:T(8,128)S(1)}, u32[]{:S(2)}, u32[]{:S(2)}) collective-permute-start(f32[128,128]{1,0:T(8,128)S(1)} %get-tuple-element.24.refs_0_), channel_id=1, source_target_pairs={{0,256},{128,384},{256,0},{384,128},{1,257},{129,385},{257,1},{385... | collective-permute-start | bytes 196616 | tf_op jit(solution)/shard_map/ppermute | solution.py:494
  113.4 3.1 %collective-permute-start.2 = (f32[128,128]{1,0:T(8,128)S(1)}, f32[128,128]{1,0:T(8,128)S(1)}, u32[]{:S(2)}, u32[]{:S(2)}) collective-permute-start(f32[128,128]{1,0:T(8,128)S(1)} %get-tuple-element.24.refs_0_), channel_id=1, source_target_pairs={{0,384},{128,0},{256,128},{384,256},{1,385},{129,1},{257,129},{385... | collective-permute-start | bytes 196616 | tf_op jit(solution)/shard_map/ppermute | solution.py:494
  116.5 0.0 collective-permute-done.refs_1_
  116.5 0.0 collective-permute-done.1.refs_2_
  116.5 1.9 %collective-permute-done.2.refs_3_ = f32[128,128]{1,0:T(8,128)S(1)} collective-permute-done((f32[128,128]{1,0:T(8,128)S(1)}, f32[128,128]{1,0:T(8,128)S(1)}, u32[]{:S(2)}, u32[]{:S(2)}) %collective-permute-start.2) | collective-permute-done | bytes 65568 | tf_op jit(solution)/shard_map/ppermute | solution.py:494
  118.4 0.0 copy-done.6
  118.4 5.8 %shard_map.93 = (f32[640,128]{1,0:T(8,128)}, f32[256,512]{1,0:T(8,128)S(1)}, f32[4320,20]{1,0:T(8,128)}) custom-call(s32[1]{0:T(128)} %bitcast.odd_ref, f32[20,20]{1,0:T(8,128)S(1)} %copy-done.6, f32[512,256]{1,0:T(8,128)S(1)} %get-tuple-element.20.signal_ref, f32[512,256]{1,0:T(8,128)S(1)} %get-tuple-element.21.value_ref, ...), custom_call_target="tpu_custom_call" | custom-call | flops 10000000 | bytes 2509892 | tf_op jit(solution)/shard_map/pallas_call | solution.py:105
  124.3 0.0 all-to-all-done.7
  124.3 1.5 %shard_map.95 = f32[640,128]{1,0:T(8,128)} custom-call(f32[256,128]{1,0:T(8,128)S(1)} %bitcast.45, bf16[384,512]{1,0:T(8,128)(2,1)S(1)} %copy-done, f32[256,512]{1,0:T(8,128)S(1)} %get-tuple-element.27.direct_ref), custom_call_target="tpu_custom_call" | custom-call | flops 10000000 | bytes 1376256 | tf_op jit(solution)/shard_map/pallas_call | solution.py:105
Async XLA Ops:
  3.1 62.5 %copy-start.3 = (bf16[512,384]{1,0:T(8,128)(2,1)S(1)}, bf16[512,384]{1,0:T(8,128)(2,1)}, u32[]{:S(2)}) copy-start(bf16[512,384]{1,0:T(8,128)(2,1)} %constant.13.clone.turned_ref) | copy-start | bytes 1179652
  24.9 40.7 %copy-start = (bf16[384,512]{1,0:T(8,128)(2,1)S(1)}, bf16[384,512]{1,0:T(8,128)(2,1)}, u32[]{:S(2)}) copy-start(bf16[384,512]{1,0:T(8,128)(2,1)} %constant.12.clone.table_hbm.table_ref) | copy-start | bytes 1179652
  24.9 14.1 %all-to-all-start.1 = ((f32[8,16,128]{2,1,0:T(8,128)}), f32[8,16,128]{2,1,0:T(8,128)S(1)}, u32[]{:S(2)}, u32[]{:S(2)}) async-start(f32[8,16,128]{2,1,0:T(8,128)} %bitcast.6), calls=%async_computation.1 | async-start | bytes 131072 | tf_op jit(solution)/shard_map/all_to_all | solution.py:470
  31.9 1.6 %copy-start.1 = (f32[2,9,1,12,20,20]{5,2,4,3,1,0:T(1,128)S(1)}, f32[2,9,1,12,20,20]{5,2,4,3,1,0:T(1,128)}, u32[]{:S(2)}) copy-start(f32[2,9,1,12,20,20]{5,2,4,3,1,0:T(1,128)} %param.8) | copy-start | bytes 1036804
  33.5 1.0 copy-start.2
  34.5 1.0 copy-start.4
  35.5 0.7 copy-start.5
  51.8 66.6 %copy-start.6 = (f32[20,20]{1,0:T(8,128)S(1)}, f32[20,20]{1,0:T(8,128)}, u32[]{:S(2)}) copy-start(f32[20,20]{1,0:T(8,128)} %map_ref.3) | copy-start | bytes 4804
  100.5 23.7 %all-to-all-start.7 = ((f32[16,16,128]{2,1,0:T(8,128)}), f32[16,16,128]{2,1,0:T(8,128)S(1)}, u32[]{:S(2)}, u32[]{:S(2)}) async-start(f32[16,16,128]{2,1,0:T(8,128)} %bitcast.27), calls=%async_computation.7 | async-start | bytes 262144 | tf_op jit(solution)/shard_map/all_to_all | solution.py:470
  105.9 10.6 %collective-permute-start = (f32[128,128]{1,0:T(8,128)S(1)}, f32[128,128]{1,0:T(8,128)S(1)}, u32[]{:S(2)}, u32[]{:S(2)}) collective-permute-start(f32[128,128]{1,0:T(8,128)S(1)} %get-tuple-element.24.refs_0_), channel_id=1, source_target_pairs={{0,128},{128,256},{256,384},{384,0},{1,129},{129,257},{257,385},{3... | collective-permute-start | bytes 196616 | tf_op jit(solution)/shard_map/ppermute | solution.py:494
  109.1 7.4 %collective-permute-start.1 = (f32[128,128]{1,0:T(8,128)S(1)}, f32[128,128]{1,0:T(8,128)S(1)}, u32[]{:S(2)}, u32[]{:S(2)}) collective-permute-start(f32[128,128]{1,0:T(8,128)S(1)} %get-tuple-element.24.refs_0_), channel_id=1, source_target_pairs={{0,256},{128,384},{256,0},{384,128},{1,257},{129,385},{257,1},{385... | collective-permute-start | bytes 196616 | tf_op jit(solution)/shard_map/ppermute | solution.py:494
  113.4 5.0 %collective-permute-start.2 = (f32[128,128]{1,0:T(8,128)S(1)}, f32[128,128]{1,0:T(8,128)S(1)}, u32[]{:S(2)}, u32[]{:S(2)}) collective-permute-start(f32[128,128]{1,0:T(8,128)S(1)} %get-tuple-element.24.refs_0_), channel_id=1, source_target_pairs={{0,384},{128,0},{256,128},{384,256},{1,385},{129,1},{257,129},{385... | collective-permute-start | bytes 196616 | tf_op jit(solution)/shard_map/ppermute | solution.py:494

commit v4 on v3

--- a/solution.py
+++ b/solution.py
@@ -353,16 +353,16 @@
     x_cells([back[:32], back[32:]], 1.0, send_ref)
 
 
-def weight_grad(odd_ref, share_refs, grad_ref):
+def weight_grad(odd_ref, near_ref, far_ref, grad_ref):
     odd = odd_ref[0]
     start = group_start()
     owned = list(slots(odd))
     for tile in range(2):
         spec, dual = [], []
-        for share_ref in share_refs:
-            at = tile * 32
-            spec.append([share_ref[at + p * 16 : at + p * 16 + 16, :] for p in range(2)])
-            dual.append([share_ref[at + 64 + p * 16 : at + 80 + p * 16, :] for p in range(2)])
+        for share_ref in (near_ref, far_ref):
+            for at in (tile * 32, 128 + tile * 32):
+                spec.append([share_ref[at + p * 16 : at + p * 16 + 16, :] for p in range(2)])
+                dual.append([share_ref[at + 64 + p * 16 : at + 80 + p * 16, :] for p in range(2)])
         for c in range(C):
             index = jnp.minimum(start + c, 127)
             real = jnp.zeros((16, 128), F32)
@@ -377,8 +377,12 @@
                     grad_ref[weight_row(9 + pair, c), :] = imag[:KX, 20 * s : 20 * s + C]
 
 
-def side(odd_ref, map_ref, signal_ref, value_ref, *refs):
-    share_refs, (out_ref, direct_ref, grad_ref, stage_ref) = refs[:-4], refs[-4:]
+def join(mine_ref, other_ref, out_ref):
+    out_ref[:128, :] = mine_ref[...]
+    out_ref[128:, :] = other_ref[...]
+
+
+def emit(map_ref, signal_ref, value_ref, out_ref, direct_ref, stage_ref):
     stage_ref[...] = value_ref[...].T
     for x, y, at in cell_rows():
         store_cells(out_ref, x, y, stage_ref[at : at + C, :])
@@ -387,7 +391,6 @@
     for _, _, at in cell_rows():
         direct_ref[at : at + C, :] = dot(mapping, stage_ref[at : at + C, :])
         direct_ref[at + C : at + 32, :] = jnp.zeros((32 - C, NR), F32)
-    weight_grad(odd_ref, share_refs, grad_ref)
 
 
 def activate(recv_ref, turned_ref, table_ref, direct_ref, cotangent_ref, value_ref, signal_ref, send_ref, modes_ref):
@@ -457,9 +460,9 @@
         y_cells=lambda r: call(y_cells, [SEND_Y], r, scratch=[VMEM((24, 512), F32)]),
         x_mix=lambda r, w: call(x_mix, [SEND_X, (64, 128)], r, w),
         x_unmix=lambda r, s, w: call(x_unmix, [SHARE, SEND_X], *(r, s, w), scratch=[VMEM((64 * C, 128), BF16)] * 2),
-        side=lambda o, b, sig, val, *shares: call(
-            side, [ROWS, CELLS, (2 * 9 * KX * C, C)], *(o, b, sig, val, *shares), scratch=[VMEM(CELLS, F32)], smem=(0,)
-        ),
+        join=lambda a, b: call(join, [(256, 128)], a, b),
+        emit=lambda b, sig, val: call(emit, [ROWS, CELLS], b, sig, val, scratch=[VMEM(CELLS, F32)]),
+        weight_grad=lambda o, near, far: call(weight_grad, [(2 * 9 * KX * C, C)], o, near, far, smem=(0,)),
         activate=lambda r, d, ct: call(activate, [TURNED, TURNED, SEND_Y], r, tz_turned, tz, d, ct, scratch=modes),
         finish=lambda r, d: call(finish, [ROWS], r, tz, d, scratch=modes),
     )
@@ -473,7 +476,7 @@
 
 
 def on_device(fields, cotangent, spectral, bypass):
-    samples = lax.axis_size("dp")
+    assert lax.axis_size("dp") == 4
     st = stages()
     odd = (lax.axis_index("gx") & 1).astype(jnp.int32).reshape(1)
     rows = as_rows(fields)
@@ -489,10 +492,11 @@
     share, sent = st["x_unmix"](to_x(st["y_spectrum"](to_y(sent))), spec, packed)
     arrived = to_x(sent)
     sent = st["y_cells"](arrived)
-    shares = [share]
-    for step in range(1, samples):
-        shares.append(lax.ppermute(share, "dp", [(i, (i + step) % samples) for i in range(samples)]))
-    output, direct, grad = st["side"](odd, bypass, signal, value, *shares)
+    other = lax.ppermute(share, "dp", [(i, i ^ 1) for i in range(4)])
+    joined = st["join"](share, other)
+    rest = lax.ppermute(joined, "dp", [(i, 3 - i) for i in range(4)])
+    output, direct = st["emit"](bypass, signal, value)
+    grad = st["weight_grad"](odd, joined, rest)
     field_grad = st["finish"](to_y(sent), direct)
     return (from_rows(output), from_rows(field_grad), grad.reshape(spectral.shape))
 

time: 127 us -> 127 us (level)
  starting transfers between devices: 22.9 us -> 19.8 us
  waiting for transfers between devices: 3.64 us -> 5.28 us
    ppermute x3 -> x2, starting transfers between devices: 10.5 us -> 7.49 us  [the longest x1 4.38 us: on_device(): rest = lax.ppermute(joined, 'dp', [(i, 3 - i) for i in range(4)])]
    ppermute x3 -> x2, waiting for transfers between devices: 1.92 us -> 3.57 us  [the longest x1 2.18 us: on_device(): other = lax.ppermute(share, 'dp', [(i, i ^ 1) for i in range(4)])]
    pallas_call x11 -> x13, Pallas kernels: 16.7 us -> 17.3 us  [call(): pl.pallas_call(body, out_shape=shapes, in_specs=specs, out_specs=[pl.Bloc...]
  transfers between devices with their start and end apart: 5 -> 4, of which waited for: 2 -> 3; matrix products, arithmetic and copies ran while one was open for 0% -> 0% of each run, Pallas kernels for 6% -> 6%
where the time goes in v4:
time: 127 us; the launch traced here: 125 us
  blocking collectives  77.6 us (61%)
  starting transfers between devices  19.8 us (16%)
  Pallas kernels  17.3 us (14%)
  waiting for transfers between devices  5.28 us (4%)
  local copies, waits for them, and re-layouts  4.29 us (3%)
    all_to_all x6, blocking collectives, swap(): lax.all_to_all(a.reshape(n, rows, 128), axis, split_axis=0, concat_axis=0...  77.6 us
    pallas_call x13, Pallas kernels, call(): pl.pallas_call(body, out_shape=shapes, in_specs=specs, out_specs=[pl.Bloc...  17.3 us
    all_to_all x2, starting transfers between devices, swap(): lax.all_to_all(a.reshape(n, rows, 128), axis, split_axis=0, concat_axis=0...  12.3 us
    ppermute x1, starting transfers between devices, on_device(): rest = lax.ppermute(joined, 'dp', [(i, 3 - i) for i in range(4)])  4.38 us
    unnamed x14, local copies, waits for them, and re-layouts  4.29 us
    ppermute x1, starting transfers between devices, on_device(): other = lax.ppermute(share, 'dp', [(i, i ^ 1) for i in range(4)])  3.11 us
  transfers between devices with their start and end apart: 4, of which 3 were waited for; matrix products, arithmetic and copies ran while one was open for 0% of the time, Pallas kernels for 6%

profile of v4, /device:TPU:1, one launch (start us, length us, event | category | flops | bytes accessed | tf_op | source)
XLA Modules:
  0.0 125.0 jit_solution(16002046512401934589)
XLA Ops:
  0.6 2.5 %shard_map.85 = f32[256,128]{1,0:T(8,128)} custom-call(f32[640,128]{1,0:T(8,128)} %bitcast.40, bf16[384,512]{1,0:T(8,128)(2,1)} %constant.12.clone.table_hbm.table_ref), custom_call_target="tpu_custom_call" | custom-call | flops 10000000 | bytes 851968 | tf_op jit(solution)/shard_map/pallas_call | solution.py:105
  3.1 0.0 copy-start.3
  3.1 20.8 %all_to_all.40 = f32[16,16,128]{2,1,0:T(8,128)S(1)} all-to-all(f32[16,16,128]{2,1,0:T(8,128)} %bitcast.57), channel_id=1, replica_groups=mesh['dp'=4,'gx'=8,'gy'=16] {'gy'}, dimensions={0} | all-to-all | bytes 262144 | tf_op jit(solution)/shard_map/all_to_all | solution.py:473
  24.0 1.0 shard_map.86
  24.9 0.0 copy-start
  24.9 7.0 %all-to-all-start.1 = ((f32[8,16,128]{2,1,0:T(8,128)}), f32[8,16,128]{2,1,0:T(8,128)S(1)}, u32[]{:S(2)}, u32[]{:S(2)}) async-start(f32[8,16,128]{2,1,0:T(8,128)} %bitcast.5), calls=%async_computation.1 | async-start | bytes 131072 | tf_op jit(solution)/shard_map/all_to_all | solution.py:473
  31.9 0.0 copy-start.1
  31.9 1.6 %copy-done.1 = f32[2,9,1,12,20,20]{5,2,4,3,1,0:T(1,128)S(1)} copy-done((f32[2,9,1,12,20,20]{5,2,4,3,1,0:T(1,128)S(1)}, f32[2,9,1,12,20,20]{5,2,4,3,1,0:T(1,128)}, u32[]{:S(2)}) %copy-start.1) | copy-done | bytes 345624
  33.5 0.0 copy-start.2
  33.5 1.0 copy-done.2
  34.5 0.0 copy-start.4
  34.5 1.0 copy-done.4
  35.5 0.0 copy-start.5
  35.5 0.7 copy-done.5
  36.2 1.2 shard_map.87
  37.3 1.7 %all-to-all-done.1 = f32[8,16,128]{2,1,0:T(8,128)S(1)} async-done(((f32[8,16,128]{2,1,0:T(8,128)}), f32[8,16,128]{2,1,0:T(8,128)S(1)}, u32[]{:S(2)}, u32[]{:S(2)}) %all-to-all-start.1) | async-done | bytes 65568 | tf_op jit(solution)/shard_map/all_to_all | solution.py:473
  39.0 0.8 shard_map.88
  39.8 12.0 %all_to_all.41 = f32[8,16,128]{2,1,0:T(8,128)S(1)} all-to-all(f32[8,16,128]{2,1,0:T(8,128)S(1)} %bitcast.55), channel_id=1, replica_groups=mesh['dp'=4,'gx'=8,'gy'=16] {'gx'}, dimensions={0} | all-to-all | bytes 131072 | tf_op jit(solution)/shard_map/all_to_all | solution.py:473
  51.8 0.3 shard_map.89
  52.1 0.0 copy-start.6
  52.1 13.5 %all_to_all.42 = f32[16,16,128]{2,1,0:T(8,128)S(1)} all-to-all(f32[16,16,128]{2,1,0:T(8,128)S(1)} %bitcast.43), channel_id=1, replica_groups=mesh['dp'=4,'gx'=8,'gy'=16] {'gy'}, dimensions={0} | all-to-all | bytes 262144 | tf_op jit(solution)/shard_map/all_to_all | solution.py:473
  65.7 0.0 copy-done.3
  65.7 0.0 copy-done
  65.7 1.6 %shard_map.90 = (f32[512,256]{1,0:T(8,128)S(1)}, f32[512,256]{1,0:T(8,128)S(1)}, f32[256,128]{1,0:T(8,128)S(1)}) custom-call(f32[256,128]{1,0:T(8,128)S(1)} %bitcast.46, bf16[512,384]{1,0:T(8,128)(2,1)S(1)} %copy-done.3, bf16[384,512]{1,0:T(8,128)(2,1)S(1)} %copy-done, f32[512,256]{1,0:T(8,128)S(1)} %get-tuple-element.17.direct_ref, ...), custom_call_target="tpu_custom_call" | custom-call | flops 10000000 | bytes 3145728 | tf_op jit(solution)/shard_map/pallas_call | solution.py:105
  67.3 11.6 %all_to_all.43 = f32[16,16,128]{2,1,0:T(8,128)S(1)} all-to-all(f32[16,16,128]{2,1,0:T(8,128)S(1)} %bitcast.53), channel_id=1, replica_groups=mesh['dp'=4,'gx'=8,'gy'=16] {'gy'}, dimensions={0} | all-to-all | bytes 262144 | tf_op jit(solution)/shard_map/all_to_all | solution.py:473
  78.8 0.3 shard_map.92
  79.2 9.9 %all_to_all.44 = f32[8,16,128]{2,1,0:T(8,128)S(1)} all-to-all(f32[8,16,128]{2,1,0:T(8,128)S(1)} %bitcast.50), channel_id=1, replica_groups=mesh['dp'=4,'gx'=8,'gy'=16] {'gx'}, dimensions={0} | all-to-all | bytes 131072 | tf_op jit(solution)/shard_map/all_to_all | solution.py:473
  89.1 0.8 shard_map.93
  89.9 9.7 %all_to_all.45 = f32[8,16,128]{2,1,0:T(8,128)S(1)} all-to-all(f32[8,16,128]{2,1,0:T(8,128)S(1)} %bitcast.54), channel_id=1, replica_groups=mesh['dp'=4,'gx'=8,'gy'=16] {'gx'}, dimensions={0} | all-to-all | bytes 131072 | tf_op jit(solution)/shard_map/all_to_all | solution.py:473
  99.6 1.0 shard_map.94
  100.6 5.4 %all-to-all-start.7 = ((f32[16,16,128]{2,1,0:T(8,128)}), f32[16,16,128]{2,1,0:T(8,128)S(1)}, u32[]{:S(2)}, u32[]{:S(2)}) async-start(f32[16,16,128]{2,1,0:T(8,128)} %bitcast.27), calls=%async_computation.7 | async-start | bytes 262144 | tf_op jit(solution)/shard_map/all_to_all | solution.py:473
  105.9 3.1 %collective-permute-start = (f32[128,128]{1,0:T(8,128)S(1)}, f32[128,128]{1,0:T(8,128)S(1)}, u32[]{:S(2)}, u32[]{:S(2)}) collective-permute-start(f32[128,128]{1,0:T(8,128)S(1)} %get-tuple-element.26.mine_ref), channel_id=1, source_target_pairs={{0,128},{128,0},{256,384},{384,256},{1,129},{129,1},{257,385},{385... | collective-permute-start | bytes 196616 | tf_op jit(solution)/shard_map/ppermute | solution.py:495
  109.1 2.2 %collective-permute-done.other_ref = f32[128,128]{1,0:T(8,128)S(1)} collective-permute-done((f32[128,128]{1,0:T(8,128)S(1)}, f32[128,128]{1,0:T(8,128)S(1)}, u32[]{:S(2)}, u32[]{:S(2)}) %collective-permute-start) | collective-permute-done | bytes 65568 | tf_op jit(solution)/shard_map/ppermute | solution.py:495
  111.3 4.4 %collective-permute-start.1 = (f32[256,128]{1,0:T(8,128)S(1)}, f32[256,128]{1,0:T(8,128)S(1)}, u32[]{:S(2)}, u32[]{:S(2)}) collective-permute-start(f32[256,128]{1,0:T(8,128)S(1)} %shard_map.96.near_ref), channel_id=1, source_target_pairs={{0,384},{128,256},{256,128},{384,0},{1,385},{129,257},{257,129},{3... | collective-permute-start | bytes 393224 | tf_op jit(solution)/shard_map/ppermute | solution.py:497
  115.7 0.0 copy-done.6
  115.7 1.1 shard_map.91
  116.8 1.4 %collective-permute-done.1.far_ref = f32[256,128]{1,0:T(8,128)S(1)} collective-permute-done((f32[256,128]{1,0:T(8,128)S(1)}, f32[256,128]{1,0:T(8,128)S(1)}, u32[]{:S(2)}, u32[]{:S(2)}) %collective-permute-start.1) | collective-permute-done | bytes 131104 | tf_op jit(solution)/shard_map/ppermute | solution.py:497
  118.2 5.3 %shard_map.97 = f32[4320,20]{1,0:T(8,128)} custom-call(s32[1]{0:T(128)} %bitcast.7.odd_ref, f32[256,128]{1,0:T(8,128)S(1)} %shard_map.96.near_ref, f32[256,128]{1,0:T(8,128)S(1)} %collective-permute-done.1.far_ref), custom_call_target="tpu_custom_call" | custom-call | flops 10000000 | bytes 607748 | tf_op jit(solution)/shard_map/pallas_call | solution.py:105
  123.5 0.0 all-to-all-done.7
  123.5 1.5 %shard_map.95 = f32[640,128]{1,0:T(8,128)} custom-call(f32[256,128]{1,0:T(8,128)S(1)} %bitcast.45, bf16[384,512]{1,0:T(8,128)(2,1)S(1)} %copy-done, f32[256,512]{1,0:T(8,128)S(1)} %get-tuple-element.25.direct_ref), custom_call_target="tpu_custom_call" | custom-call | flops 10000000 | bytes 1376256 | tf_op jit(solution)/shard_map/pallas_call | solution.py:105
  (1 shorter events, 0.0 us)
Async XLA Ops:
  3.1 62.6 %copy-start.3 = (bf16[512,384]{1,0:T(8,128)(2,1)S(1)}, bf16[512,384]{1,0:T(8,128)(2,1)}, u32[]{:S(2)}) copy-start(bf16[512,384]{1,0:T(8,128)(2,1)} %constant.13.clone.turned_ref) | copy-start | bytes 1179652
  24.9 40.8 %copy-start = (bf16[384,512]{1,0:T(8,128)(2,1)S(1)}, bf16[384,512]{1,0:T(8,128)(2,1)}, u32[]{:S(2)}) copy-start(bf16[384,512]{1,0:T(8,128)(2,1)} %constant.12.clone.table_hbm.table_ref) | copy-start | bytes 1179652
  24.9 14.1 %all-to-all-start.1 = ((f32[8,16,128]{2,1,0:T(8,128)}), f32[8,16,128]{2,1,0:T(8,128)S(1)}, u32[]{:S(2)}, u32[]{:S(2)}) async-start(f32[8,16,128]{2,1,0:T(8,128)} %bitcast.5), calls=%async_computation.1 | async-start | bytes 131072 | tf_op jit(solution)/shard_map/all_to_all | solution.py:473
  31.9 1.6 %copy-start.1 = (f32[2,9,1,12,20,20]{5,2,4,3,1,0:T(1,128)S(1)}, f32[2,9,1,12,20,20]{5,2,4,3,1,0:T(1,128)}, u32[]{:S(2)}) copy-start(f32[2,9,1,12,20,20]{5,2,4,3,1,0:T(1,128)} %param.8) | copy-start | bytes 1036804
  33.5 1.0 copy-start.2
  34.5 1.0 copy-start.4
  35.5 0.7 copy-start.5
  52.1 63.5 %copy-start.6 = (f32[20,20]{1,0:T(8,128)S(1)}, f32[20,20]{1,0:T(8,128)}, u32[]{:S(2)}) copy-start(f32[20,20]{1,0:T(8,128)} %map_ref.3) | copy-start | bytes 4804
  100.6 22.9 %all-to-all-start.7 = ((f32[16,16,128]{2,1,0:T(8,128)}), f32[16,16,128]{2,1,0:T(8,128)S(1)}, u32[]{:S(2)}, u32[]{:S(2)}) async-start(f32[16,16,128]{2,1,0:T(8,128)} %bitcast.27), calls=%async_computation.7 | async-start | bytes 262144 | tf_op jit(solution)/shard_map/all_to_all | solution.py:473
  105.9 5.3 %collective-permute-start = (f32[128,128]{1,0:T(8,128)S(1)}, f32[128,128]{1,0:T(8,128)S(1)}, u32[]{:S(2)}, u32[]{:S(2)}) collective-permute-start(f32[128,128]{1,0:T(8,128)S(1)} %get-tuple-element.26.mine_ref), channel_id=1, source_target_pairs={{0,128},{128,0},{256,384},{384,256},{1,129},{129,1},{257,385},{385... | collective-permute-start | bytes 196616 | tf_op jit(solution)/shard_map/ppermute | solution.py:495
  111.3 6.9 %collective-permute-start.1 = (f32[256,128]{1,0:T(8,128)S(1)}, f32[256,128]{1,0:T(8,128)S(1)}, u32[]{:S(2)}, u32[]{:S(2)}) collective-permute-start(f32[256,128]{1,0:T(8,128)S(1)} %shard_map.96.near_ref), channel_id=1, source_target_pairs={{0,384},{128,256},{256,128},{384,0},{1,385},{129,257},{257,129},{3... | collective-permute-start | bytes 393224 | tf_op jit(solution)/shard_map/ppermute | solution.py:497

commit v5 on v4

--- a/solution.py
+++ b/solution.py
@@ -15,6 +15,7 @@
 GX, GY = 8, 16
 S6 = 6
 KX = 12
+SHARE_ROWS = 6 * KX
 F32 = jnp.float32
 VMEM = pltpu.VMEM
 INV_CELLS = 1.0 / (32 * 32 * 512)
@@ -95,7 +96,7 @@
     return rotation(col & 15, row >> 1, row & 1, col >> 4, 1.0, scale)
 
 
-def call(body, outs, *args, scratch=(), smem=(), hbm=(), vmem=16 << 20, flops=10**7):
+def call(body, outs, *args, scratch=(), smem=(), hbm=(), hbm_out=False, vmem=16 << 20, flops=10**7):
     specs = [
         pl.BlockSpec(memory_space=pltpu.SMEM if i in smem else pltpu.HBM if i in hbm else VMEM)
         for i in range(len(args))
@@ -106,7 +107,7 @@
         body,
         out_shape=shapes,
         in_specs=specs,
-        out_specs=[pl.BlockSpec(memory_space=VMEM)] * len(outs),
+        out_specs=[pl.BlockSpec(memory_space=pl.ANY if hbm_out else VMEM)] * len(outs),
         scratch_shapes=list(scratch),
         compiler_params=pltpu.CompilerParams(vmem_limit_bytes=vmem),
         cost_estimate=pl.CostEstimate(flops=flops, bytes_accessed=nbytes, transcendentals=0),
@@ -328,10 +329,15 @@
 
 
 def x_unmix(recv_ref, spec_ref, packed_ref, share_ref, send_ref, high_ref, low_ref):
-    share_ref[:64, :] = spec_ref[...]
     spectrum = x_spectrum(recv_ref, INV_CELLS)
+    lane = lanes(KX)
+    for part in range(2):
+        low, high = part * 16, part * KX
+        share_ref[high : high + KX, :] = spec_ref[low : low + KX, :]
+        share_ref[24 + high : 24 + high + KX, :] = spectrum[0][low : low + KX]
+        dual = pltpu.roll(spectrum[1][low : low + 16], 60, axis=1)[:KX]
+        share_ref[48 + high : 48 + high + KX, :] = jnp.where(lane < 60, spec_ref[32 + low : 32 + low + KX, :], dual)
     for tile in range(2):
-        share_ref[64 + tile * 32 : 96 + tile * 32, :] = spectrum[tile]
         dr, di = spectrum[tile][:16], spectrum[tile][16:]
         for c in range(C):
             wr = packed_ref[packed_row(0, c, tile), :]
@@ -353,33 +359,49 @@
     x_cells([back[:32], back[32:]], 1.0, send_ref)
 
 
-def weight_grad(odd_ref, near_ref, far_ref, grad_ref):
+def weight_grad(odd_ref, near_ref, far_ref, grad_hbm, *scratch):
     odd = odd_ref[0]
-    start = group_start()
-    owned = list(slots(odd))
+    buffers, sems = scratch[:2], scratch[2]
+    start = group_start()[:KX]
+    copies = []
     for tile in range(2):
-        spec, dual = [], []
+        buffer, pairs = buffers[tile], (6, 3)[tile]
+        samples = []
         for share_ref in (near_ref, far_ref):
-            for at in (tile * 32, 128 + tile * 32):
-                spec.append([share_ref[at + p * 16 : at + p * 16 + 16, :] for p in range(2)])
-                dual.append([share_ref[at + 64 + p * 16 : at + 80 + p * 16, :] for p in range(2)])
+            for at in (0, SHARE_ROWS):
+                parts = [share_ref[at + k * KX : at + k * KX + KX, :] for k in range(6)]
+                if tile == 0:
+                    samples.append(parts[:4])
+                else:
+                    samples.append(parts[4:] + [pltpu.roll(a, 68, axis=1) for a in parts[4:]])
+        rows = pairs * KX * C
         for c in range(C):
             index = jnp.minimum(start + c, 127)
-            real = jnp.zeros((16, 128), F32)
-            imag = jnp.zeros((16, 128), F32)
-            for (er, ei), (dr, di) in zip(spec, dual):
+            real = jnp.zeros((KX, 128), F32)
+            imag = jnp.zeros((KX, 128), F32)
+            for er, ei, dr, di in samples:
                 sr, si = pick(er, index), pick(ei, index)
                 real = real + (sr * dr + si * di)
                 imag = imag + (sr * di - si * dr)
-            for where, s, pair in owned:
-                if where == tile:
-                    grad_ref[weight_row(pair, c), :] = real[:KX, 20 * s : 20 * s + C]
-                    grad_ref[weight_row(9 + pair, c), :] = imag[:KX, 20 * s : 20 * s + C]
+            for s in range(pairs):
+                buffer[weight_row(s, c), :] = real[:, 20 * s : 20 * s + C]
+                buffer[pl.ds(rows + s * (KX * C) + c, KX, stride=C), :] = imag[:, 20 * s : 20 * s + C]
+        first = (3 * odd if tile == 0 else 6 * (1 - odd)) * (KX * C)
+        for part in range(2):
+            copy = pltpu.make_async_copy(
+                buffer.at[pl.ds(part * rows, rows), :],
+                grad_hbm.at[pl.ds(pl.multiple_of(part * (9 * KX * C) + first, 8), rows), :],
+                sems.at[tile * 2 + part],
+            )
+            copy.start()
+            copies.append(copy)
+    for copy in copies:
+        copy.wait()
 
 
 def join(mine_ref, other_ref, out_ref):
-    out_ref[:128, :] = mine_ref[...]
-    out_ref[128:, :] = other_ref[...]
+    out_ref[:SHARE_ROWS, :] = mine_ref[...]
+    out_ref[SHARE_ROWS:, :] = other_ref[...]
 
 
 def emit(map_ref, signal_ref, value_ref, out_ref, direct_ref, stage_ref):
@@ -435,7 +457,7 @@
 SEND_Y = (GY * 16, 128)
 SEND_X = (GX * 16, 128)
 PACKED = (2 * C * 2 * 16, 128)
-SHARE = (128, 128)
+SHARE = (SHARE_ROWS, 128)
 BF16 = jnp.bfloat16
 DMA = pltpu.SemaphoreType.DMA
 
@@ -460,9 +482,16 @@
         y_cells=lambda r: call(y_cells, [SEND_Y], r, scratch=[VMEM((24, 512), F32)]),
         x_mix=lambda r, w: call(x_mix, [SEND_X, (64, 128)], r, w),
         x_unmix=lambda r, s, w: call(x_unmix, [SHARE, SEND_X], *(r, s, w), scratch=[VMEM((64 * C, 128), BF16)] * 2),
-        join=lambda a, b: call(join, [(256, 128)], a, b),
+        join=lambda a, b: call(join, [(2 * SHARE_ROWS, 128)], a, b),
         emit=lambda b, sig, val: call(emit, [ROWS, CELLS], b, sig, val, scratch=[VMEM(CELLS, F32)]),
-        weight_grad=lambda o, near, far: call(weight_grad, [(2 * 9 * KX * C, C)], o, near, far, smem=(0,)),
+        weight_grad=lambda o, near, far: call(
+            weight_grad,
+            [(2 * 9 * KX * C, C)],
+            *(o, near, far),
+            scratch=[VMEM((2 * 6 * KX * C, C), F32), VMEM((2 * 3 * KX * C, C), F32), DMA((4,))],
+            smem=(0,),
+            hbm_out=True,
+        ),
         activate=lambda r, d, ct: call(activate, [TURNED, TURNED, SEND_Y], r, tz_turned, tz, d, ct, scratch=modes),
         finish=lambda r, d: call(finish, [ROWS], r, tz, d, scratch=modes),
     )
@@ -492,12 +521,13 @@
     share, sent = st["x_unmix"](to_x(st["y_spectrum"](to_y(sent))), spec, packed)
     arrived = to_x(sent)
     sent = st["y_cells"](arrived)
+    arrived = to_y(sent)
     other = lax.ppermute(share, "dp", [(i, i ^ 1) for i in range(4)])
     joined = st["join"](share, other)
     rest = lax.ppermute(joined, "dp", [(i, 3 - i) for i in range(4)])
     output, direct = st["emit"](bypass, signal, value)
     grad = st["weight_grad"](odd, joined, rest)
-    field_grad = st["finish"](to_y(sent), direct)
+    field_grad = st["finish"](arrived, direct)
     return (from_rows(output), from_rows(field_grad), grad.reshape(spectral.shape))
 
 

time: 127 us -> 125 us (0.984)
  no operation moved by 1% of the time
where the time goes in v5:
time: 125 us; the launch traced here: 124 us
  blocking collectives  77.6 us (62%)
  starting transfers between devices  19.8 us (16%)
  Pallas kernels  17 us (14%)
  waiting for transfers between devices  4.36 us (3%)
  local copies, waits for them, and re-layouts  4.29 us (3%)
    all_to_all x6, blocking collectives, swap(): lax.all_to_all(a.reshape(n, rows, 128), axis, split_axis=0, concat_axis=0...  77.6 us
    pallas_call x13, Pallas kernels, call(): pl.pallas_call(body, out_shape=shapes, in_specs=specs, out_specs=[pl.Bloc...  17 us
    all_to_all x2, starting transfers between devices, swap(): lax.all_to_all(a.reshape(n, rows, 128), axis, split_axis=0, concat_axis=0...  12.3 us
    ppermute x1, starting transfers between devices, on_device(): rest = lax.ppermute(joined, 'dp', [(i, 3 - i) for i in range(4)])  4.37 us
    unnamed x14, local copies, waits for them, and re-layouts  4.29 us
    ppermute x1, starting transfers between devices, on_device(): other = lax.ppermute(share, 'dp', [(i, i ^ 1) for i in range(4)])  3.11 us
  transfers between devices with their start and end apart: 4, of which 3 were waited for; matrix products, arithmetic and copies ran while one was open for 0% of the time, Pallas kernels for 6%

profile of v5, /device:TPU:1, one launch (start us, length us, event | category | flops | bytes accessed | tf_op | source)
XLA Modules:
  0.0 123.8 jit_solution(16186866091179444785)
XLA Ops:
  0.6 2.5 %shard_map.85 = f32[256,128]{1,0:T(8,128)} custom-call(f32[640,128]{1,0:T(8,128)} %bitcast.40, bf16[384,512]{1,0:T(8,128)(2,1)} %constant.12.clone.table_hbm.table_ref), custom_call_target="tpu_custom_call" | custom-call | flops 10000000 | bytes 851968 | tf_op jit(solution)/shard_map/pallas_call | solution.py:106
  3.1 0.0 copy-start.3
  3.1 20.8 %all_to_all.40 = f32[16,16,128]{2,1,0:T(8,128)S(1)} all-to-all(f32[16,16,128]{2,1,0:T(8,128)} %bitcast.57), channel_id=1, replica_groups=mesh['dp'=4,'gx'=8,'gy'=16] {'gy'}, dimensions={0} | all-to-all | bytes 262144 | tf_op jit(solution)/shard_map/all_to_all | solution.py:502
  24.0 1.0 shard_map.86
  24.9 0.0 copy-start
  24.9 7.0 %all-to-all-start.1 = ((f32[8,16,128]{2,1,0:T(8,128)}), f32[8,16,128]{2,1,0:T(8,128)S(1)}, u32[]{:S(2)}, u32[]{:S(2)}) async-start(f32[8,16,128]{2,1,0:T(8,128)} %bitcast.5), calls=%async_computation.1 | async-start | bytes 131072 | tf_op jit(solution)/shard_map/all_to_all | solution.py:502
  31.9 0.0 copy-start.1
  31.9 1.6 %copy-done.1 = f32[2,9,1,12,20,20]{5,2,4,3,1,0:T(1,128)S(1)} copy-done((f32[2,9,1,12,20,20]{5,2,4,3,1,0:T(1,128)S(1)}, f32[2,9,1,12,20,20]{5,2,4,3,1,0:T(1,128)}, u32[]{:S(2)}) %copy-start.1) | copy-done | bytes 345624
  33.5 0.0 copy-start.2
  33.5 1.0 copy-done.2
  34.5 0.0 copy-start.4
  34.5 1.0 copy-done.4
  35.5 0.0 copy-start.5
  35.5 0.7 copy-done.5
  36.2 1.2 shard_map.87
  37.3 1.7 %all-to-all-done.1 = f32[8,16,128]{2,1,0:T(8,128)S(1)} async-done(((f32[8,16,128]{2,1,0:T(8,128)}), f32[8,16,128]{2,1,0:T(8,128)S(1)}, u32[]{:S(2)}, u32[]{:S(2)}) %all-to-all-start.1) | async-done | bytes 65568 | tf_op jit(solution)/shard_map/all_to_all | solution.py:502
  39.0 0.8 shard_map.88
  39.8 12.0 %all_to_all.41 = f32[8,16,128]{2,1,0:T(8,128)S(1)} all-to-all(f32[8,16,128]{2,1,0:T(8,128)S(1)} %bitcast.55), channel_id=1, replica_groups=mesh['dp'=4,'gx'=8,'gy'=16] {'gx'}, dimensions={0} | all-to-all | bytes 131072 | tf_op jit(solution)/shard_map/all_to_all | solution.py:502
  51.8 0.3 shard_map.89
  52.1 0.0 copy-start.6
  52.1 13.5 %all_to_all.42 = f32[16,16,128]{2,1,0:T(8,128)S(1)} all-to-all(f32[16,16,128]{2,1,0:T(8,128)S(1)} %bitcast.43), channel_id=1, replica_groups=mesh['dp'=4,'gx'=8,'gy'=16] {'gy'}, dimensions={0} | all-to-all | bytes 262144 | tf_op jit(solution)/shard_map/all_to_all | solution.py:502
  65.7 0.0 copy-done.3
  65.7 0.0 copy-done
  65.7 1.6 %shard_map.90 = (f32[512,256]{1,0:T(8,128)S(1)}, f32[512,256]{1,0:T(8,128)S(1)}, f32[256,128]{1,0:T(8,128)S(1)}) custom-call(f32[256,128]{1,0:T(8,128)S(1)} %bitcast.46, bf16[512,384]{1,0:T(8,128)(2,1)S(1)} %copy-done.3, bf16[384,512]{1,0:T(8,128)(2,1)S(1)} %copy-done, f32[512,256]{1,0:T(8,128)S(1)} %get-tuple-element.17.direct_ref, ...), custom_call_target="tpu_custom_call" | custom-call | flops 10000000 | bytes 3145728 | tf_op jit(solution)/shard_map/pallas_call | solution.py:106
  67.3 11.6 %all_to_all.43 = f32[16,16,128]{2,1,0:T(8,128)S(1)} all-to-all(f32[16,16,128]{2,1,0:T(8,128)S(1)} %bitcast.53), channel_id=1, replica_groups=mesh['dp'=4,'gx'=8,'gy'=16] {'gy'}, dimensions={0} | all-to-all | bytes 262144 | tf_op jit(solution)/shard_map/all_to_all | solution.py:502
  78.8 0.3 shard_map.92
  79.2 9.9 %all_to_all.44 = f32[8,16,128]{2,1,0:T(8,128)S(1)} all-to-all(f32[8,16,128]{2,1,0:T(8,128)S(1)} %bitcast.50), channel_id=1, replica_groups=mesh['dp'=4,'gx'=8,'gy'=16] {'gx'}, dimensions={0} | all-to-all | bytes 131072 | tf_op jit(solution)/shard_map/all_to_all | solution.py:502
  89.1 0.8 shard_map.93
  89.9 9.7 %all_to_all.45 = f32[8,16,128]{2,1,0:T(8,128)S(1)} all-to-all(f32[8,16,128]{2,1,0:T(8,128)S(1)} %bitcast.54), channel_id=1, replica_groups=mesh['dp'=4,'gx'=8,'gy'=16] {'gx'}, dimensions={0} | all-to-all | bytes 131072 | tf_op jit(solution)/shard_map/all_to_all | solution.py:502
  99.6 1.0 shard_map.94
  100.6 5.4 %all-to-all-start.7 = ((f32[16,16,128]{2,1,0:T(8,128)}), f32[16,16,128]{2,1,0:T(8,128)S(1)}, u32[]{:S(2)}, u32[]{:S(2)}) async-start(f32[16,16,128]{2,1,0:T(8,128)} %bitcast.27), calls=%async_computation.7 | async-start | bytes 262144 | tf_op jit(solution)/shard_map/all_to_all | solution.py:502
  105.9 3.1 %collective-permute-start = (f32[72,128]{1,0:T(8,128)S(1)}, f32[72,128]{1,0:T(8,128)S(1)}, u32[]{:S(2)}, u32[]{:S(2)}) collective-permute-start(f32[72,128]{1,0:T(8,128)S(1)} %get-tuple-element.26.mine_ref), channel_id=1, source_target_pairs={{0,128},{128,0},{256,384},{384,256},{1,129},{129,1},{257,385},{385... | collective-permute-start | bytes 110600 | tf_op jit(solution)/shard_map/ppermute | solution.py:525
  109.1 1.9 %collective-permute-done.other_ref = f32[72,128]{1,0:T(8,128)S(1)} collective-permute-done((f32[72,128]{1,0:T(8,128)S(1)}, f32[72,128]{1,0:T(8,128)S(1)}, u32[]{:S(2)}, u32[]{:S(2)}) %collective-permute-start) | collective-permute-done | bytes 36896 | tf_op jit(solution)/shard_map/ppermute | solution.py:525
  110.9 4.4 %collective-permute-start.1 = (f32[144,128]{1,0:T(8,128)S(1)}, f32[144,128]{1,0:T(8,128)S(1)}, u32[]{:S(2)}, u32[]{:S(2)}) collective-permute-start(f32[144,128]{1,0:T(8,128)S(1)} %shard_map.96.near_ref), channel_id=1, source_target_pairs={{0,384},{128,256},{256,128},{384,0},{1,385},{129,257},{257,129},{3... | collective-permute-start | bytes 221192 | tf_op jit(solution)/shard_map/ppermute | solution.py:527
  115.3 0.0 copy-done.6
  115.3 1.1 shard_map.91
  116.5 0.8 collective-permute-done.1.far_ref
  117.2 5.0 %shard_map.97 = f32[4320,20]{1,0:T(8,128)} custom-call(s32[1]{0:T(128)} %bitcast.7.odd_ref, f32[144,128]{1,0:T(8,128)S(1)} %shard_map.96.near_ref, f32[144,128]{1,0:T(8,128)S(1)} %collective-permute-done.1.far_ref), custom_call_target="tpu_custom_call" | custom-call | flops 10000000 | bytes 493060 | tf_op jit(solution)/shard_map/pallas_call | solution.py:106
  122.3 0.0 all-to-all-done.7
  122.3 1.5 %shard_map.95 = f32[640,128]{1,0:T(8,128)} custom-call(f32[256,128]{1,0:T(8,128)S(1)} %bitcast.45, bf16[384,512]{1,0:T(8,128)(2,1)S(1)} %copy-done, f32[256,512]{1,0:T(8,128)S(1)} %get-tuple-element.25.direct_ref), custom_call_target="tpu_custom_call" | custom-call | flops 10000000 | bytes 1376256 | tf_op jit(solution)/shard_map/pallas_call | solution.py:106
  (1 shorter events, 0.0 us)
Async XLA Ops:
  3.1 62.6 %copy-start.3 = (bf16[512,384]{1,0:T(8,128)(2,1)S(1)}, bf16[512,384]{1,0:T(8,128)(2,1)}, u32[]{:S(2)}) copy-start(bf16[512,384]{1,0:T(8,128)(2,1)} %constant.13.clone.turned_ref) | copy-start | bytes 1179652
  24.9 40.8 %copy-start = (bf16[384,512]{1,0:T(8,128)(2,1)S(1)}, bf16[384,512]{1,0:T(8,128)(2,1)}, u32[]{:S(2)}) copy-start(bf16[384,512]{1,0:T(8,128)(2,1)} %constant.12.clone.table_hbm.table_ref) | copy-start | bytes 1179652
  24.9 14.1 %all-to-all-start.1 = ((f32[8,16,128]{2,1,0:T(8,128)}), f32[8,16,128]{2,1,0:T(8,128)S(1)}, u32[]{:S(2)}, u32[]{:S(2)}) async-start(f32[8,16,128]{2,1,0:T(8,128)} %bitcast.5), calls=%async_computation.1 | async-start | bytes 131072 | tf_op jit(solution)/shard_map/all_to_all | solution.py:502
  31.9 1.6 %copy-start.1 = (f32[2,9,1,12,20,20]{5,2,4,3,1,0:T(1,128)S(1)}, f32[2,9,1,12,20,20]{5,2,4,3,1,0:T(1,128)}, u32[]{:S(2)}) copy-start(f32[2,9,1,12,20,20]{5,2,4,3,1,0:T(1,128)} %param.8) | copy-start | bytes 1036804
  33.5 1.0 copy-start.2
  34.5 1.0 copy-start.4
  35.5 0.7 copy-start.5
  52.1 63.2 %copy-start.6 = (f32[20,20]{1,0:T(8,128)S(1)}, f32[20,20]{1,0:T(8,128)}, u32[]{:S(2)}) copy-start(f32[20,20]{1,0:T(8,128)} %map_ref.3) | copy-start | bytes 4804
  100.6 21.7 %all-to-all-start.7 = ((f32[16,16,128]{2,1,0:T(8,128)}), f32[16,16,128]{2,1,0:T(8,128)S(1)}, u32[]{:S(2)}, u32[]{:S(2)}) async-start(f32[16,16,128]{2,1,0:T(8,128)} %bitcast.27), calls=%async_computation.7 | async-start | bytes 262144 | tf_op jit(solution)/shard_map/all_to_all | solution.py:502
  105.9 5.0 %collective-permute-start = (f32[72,128]{1,0:T(8,128)S(1)}, f32[72,128]{1,0:T(8,128)S(1)}, u32[]{:S(2)}, u32[]{:S(2)}) collective-permute-start(f32[72,128]{1,0:T(8,128)S(1)} %get-tuple-element.26.mine_ref), channel_id=1, source_target_pairs={{0,128},{128,0},{256,384},{384,256},{1,129},{129,1},{257,385},{385... | collective-permute-start | bytes 110600 | tf_op jit(solution)/shard_map/ppermute | solution.py:525
  110.9 6.3 %collective-permute-start.1 = (f32[144,128]{1,0:T(8,128)S(1)}, f32[144,128]{1,0:T(8,128)S(1)}, u32[]{:S(2)}, u32[]{:S(2)}) collective-permute-start(f32[144,128]{1,0:T(8,128)S(1)} %shard_map.96.near_ref), channel_id=1, source_target_pairs={{0,384},{128,256},{256,128},{384,0},{1,385},{129,257},{257,129},{3... | collective-permute-start | bytes 221192 | tf_op jit(solution)/shard_map/ppermute | solution.py:527

commit v6 on v5

--- a/solution.py
+++ b/solution.py
@@ -359,30 +359,47 @@
     x_cells([back[:32], back[32:]], 1.0, send_ref)
 
 
-def weight_grad(odd_ref, near_ref, far_ref, grad_hbm, *scratch):
+def share_parts(share_ref, tile):
+    for at in (0, SHARE_ROWS):
+        parts = [share_ref[at + k * KX : at + k * KX + KX, :] for k in range(6)]
+        if tile == 0:
+            yield parts[:4]
+        else:
+            yield parts[4:] + [pltpu.roll(a, 68, axis=1) for a in parts[4:]]
+
+
+def add_outer(samples, index, real, imag):
+    for er, ei, dr, di in samples:
+        sr, si = pick(er, index), pick(ei, index)
+        real = real + (sr * dr + si * di)
+        imag = imag + (sr * di - si * dr)
+    return real, imag
+
+
+def near_sum(near_ref, sum_ref):
+    start = group_start()[:KX]
+    zero = jnp.zeros((KX, 128), F32)
+    for tile in range(2):
+        samples = list(share_parts(near_ref, tile))
+        for c in range(C):
+            found = add_outer(samples, jnp.minimum(start + c, 127), zero, zero)
+            for part in range(2):
+                at = packed_row(part, c, tile).start
+                sum_ref[at : at + KX, :] = found[part]
+
+
+def weight_grad(odd_ref, sum_ref, far_ref, grad_hbm, *scratch):
     odd = odd_ref[0]
     buffers, sems = scratch[:2], scratch[2]
     start = group_start()[:KX]
     copies = []
     for tile in range(2):
         buffer, pairs = buffers[tile], (6, 3)[tile]
-        samples = []
-        for share_ref in (near_ref, far_ref):
-            for at in (0, SHARE_ROWS):
-                parts = [share_ref[at + k * KX : at + k * KX + KX, :] for k in range(6)]
-                if tile == 0:
-                    samples.append(parts[:4])
-                else:
-                    samples.append(parts[4:] + [pltpu.roll(a, 68, axis=1) for a in parts[4:]])
+        samples = list(share_parts(far_ref, tile))
         rows = pairs * KX * C
         for c in range(C):
-            index = jnp.minimum(start + c, 127)
-            real = jnp.zeros((KX, 128), F32)
-            imag = jnp.zeros((KX, 128), F32)
-            for er, ei, dr, di in samples:
-                sr, si = pick(er, index), pick(ei, index)
-                real = real + (sr * dr + si * di)
-                imag = imag + (sr * di - si * dr)
+            near = [sum_ref[packed_row(p, c, tile).start : packed_row(p, c, tile).start + KX, :] for p in range(2)]
+            real, imag = add_outer(samples, jnp.minimum(start + c, 127), *near)
             for s in range(pairs):
                 buffer[weight_row(s, c), :] = real[:, 20 * s : 20 * s + C]
                 buffer[pl.ds(rows + s * (KX * C) + c, KX, stride=C), :] = imag[:, 20 * s : 20 * s + C]
@@ -484,6 +501,7 @@
         x_unmix=lambda r, s, w: call(x_unmix, [SHARE, SEND_X], *(r, s, w), scratch=[VMEM((64 * C, 128), BF16)] * 2),
         join=lambda a, b: call(join, [(2 * SHARE_ROWS, 128)], a, b),
         emit=lambda b, sig, val: call(emit, [ROWS, CELLS], b, sig, val, scratch=[VMEM(CELLS, F32)]),
+        near_sum=lambda near: call(near_sum, [PACKED], near),
         weight_grad=lambda o, near, far: call(
             weight_grad,
             [(2 * 9 * KX * C, C)],
@@ -525,8 +543,9 @@
     other = lax.ppermute(share, "dp", [(i, i ^ 1) for i in range(4)])
     joined = st["join"](share, other)
     rest = lax.ppermute(joined, "dp", [(i, 3 - i) for i in range(4)])
+    half = st["near_sum"](joined)
     output, direct = st["emit"](bypass, signal, value)
-    grad = st["weight_grad"](odd, joined, rest)
+    grad = st["weight_grad"](odd, half, rest)
     field_grad = st["finish"](arrived, direct)
     return (from_rows(output), from_rows(field_grad), grad.reshape(spectral.shape))
 

time: 125 us -> 125 us (level)
    pallas_call x13 -> x14, Pallas kernels: 17 us -> 17.1 us  [call(): pl.pallas_call(body, out_shape=shapes, in_specs=specs, out_specs=[pl.Bloc...]
where the time goes in v6:
time: 125 us; the launch traced here: 123 us
  blocking collectives  77.6 us (62%)
  starting transfers between devices  19.8 us (16%)
  Pallas kernels  17.1 us (14%)
  local copies, waits for them, and re-layouts  4.29 us (3%)
  waiting for transfers between devices  3.81 us (3%)
    all_to_all x6, blocking collectives, swap(): lax.all_to_all(a.reshape(n, rows, 128), axis, split_axis=0, concat_axis=0...  77.6 us
    pallas_call x14, Pallas kernels, call(): pl.pallas_call(body, out_shape=shapes, in_specs=specs, out_specs=[pl.Bloc...  17.1 us
    all_to_all x2, starting transfers between devices, swap(): lax.all_to_all(a.reshape(n, rows, 128), axis, split_axis=0, concat_axis=0...  12.3 us
    ppermute x1, starting transfers between devices, on_device(): rest = lax.ppermute(joined, 'dp', [(i, 3 - i) for i in range(4)])  4.37 us
    unnamed x14, local copies, waits for them, and re-layouts  4.29 us
    ppermute x1, starting transfers between devices, on_device(): other = lax.ppermute(share, 'dp', [(i, i ^ 1) for i in range(4)])  3.11 us
  transfers between devices with their start and end apart: 4, of which 3 were waited for; matrix products, arithmetic and copies ran while one was open for 0% of the time, Pallas kernels for 6%

profile of v6, /device:TPU:1, one launch (start us, length us, event | category | flops | bytes accessed | tf_op | source)
XLA Modules:
  0.0 123.3 jit_solution(7413834597767155202)
XLA Ops:
  0.6 2.5 %shard_map.85 = f32[256,128]{1,0:T(8,128)} custom-call(f32[640,128]{1,0:T(8,128)} %bitcast.40, bf16[384,512]{1,0:T(8,128)(2,1)} %constant.12.clone.table_hbm.table_ref), custom_call_target="tpu_custom_call" | custom-call | flops 10000000 | bytes 851968 | tf_op jit(solution)/shard_map/pallas_call | solution.py:106
  3.1 0.0 copy-start.3
  3.1 20.8 %all_to_all.40 = f32[16,16,128]{2,1,0:T(8,128)S(1)} all-to-all(f32[16,16,128]{2,1,0:T(8,128)} %bitcast.57), channel_id=1, replica_groups=mesh['dp'=4,'gx'=8,'gy'=16] {'gy'}, dimensions={0} | all-to-all | bytes 262144 | tf_op jit(solution)/shard_map/all_to_all | solution.py:520
  24.0 1.0 shard_map.86
  24.9 0.0 copy-start
  24.9 7.0 %all-to-all-start.1 = ((f32[8,16,128]{2,1,0:T(8,128)}), f32[8,16,128]{2,1,0:T(8,128)S(1)}, u32[]{:S(2)}, u32[]{:S(2)}) async-start(f32[8,16,128]{2,1,0:T(8,128)} %bitcast.5), calls=%async_computation.1 | async-start | bytes 131072 | tf_op jit(solution)/shard_map/all_to_all | solution.py:520
  31.9 0.0 copy-start.1
  31.9 1.6 %copy-done.1 = f32[2,9,1,12,20,20]{5,2,4,3,1,0:T(1,128)S(1)} copy-done((f32[2,9,1,12,20,20]{5,2,4,3,1,0:T(1,128)S(1)}, f32[2,9,1,12,20,20]{5,2,4,3,1,0:T(1,128)}, u32[]{:S(2)}) %copy-start.1) | copy-done | bytes 345624
  33.5 0.0 copy-start.2
  33.5 1.0 copy-done.2
  34.5 0.0 copy-start.4
  34.5 1.0 copy-done.4
  35.5 0.0 copy-start.5
  35.5 0.7 copy-done.5
  36.2 1.2 shard_map.87
  37.3 1.7 %all-to-all-done.1 = f32[8,16,128]{2,1,0:T(8,128)S(1)} async-done(((f32[8,16,128]{2,1,0:T(8,128)}), f32[8,16,128]{2,1,0:T(8,128)S(1)}, u32[]{:S(2)}, u32[]{:S(2)}) %all-to-all-start.1) | async-done | bytes 65568 | tf_op jit(solution)/shard_map/all_to_all | solution.py:520
  39.0 0.8 shard_map.88
  39.8 12.0 %all_to_all.41 = f32[8,16,128]{2,1,0:T(8,128)S(1)} all-to-all(f32[8,16,128]{2,1,0:T(8,128)S(1)} %bitcast.55), channel_id=1, replica_groups=mesh['dp'=4,'gx'=8,'gy'=16] {'gx'}, dimensions={0} | all-to-all | bytes 131072 | tf_op jit(solution)/shard_map/all_to_all | solution.py:520
  51.8 0.3 shard_map.89
  52.1 0.0 copy-start.6
  52.1 13.5 %all_to_all.42 = f32[16,16,128]{2,1,0:T(8,128)S(1)} all-to-all(f32[16,16,128]{2,1,0:T(8,128)S(1)} %bitcast.43), channel_id=1, replica_groups=mesh['dp'=4,'gx'=8,'gy'=16] {'gy'}, dimensions={0} | all-to-all | bytes 262144 | tf_op jit(solution)/shard_map/all_to_all | solution.py:520
  65.7 0.0 copy-done.3
  65.7 0.0 copy-done
  65.7 1.6 %shard_map.90 = (f32[512,256]{1,0:T(8,128)S(1)}, f32[512,256]{1,0:T(8,128)S(1)}, f32[256,128]{1,0:T(8,128)S(1)}) custom-call(f32[256,128]{1,0:T(8,128)S(1)} %bitcast.46, bf16[512,384]{1,0:T(8,128)(2,1)S(1)} %copy-done.3, bf16[384,512]{1,0:T(8,128)(2,1)S(1)} %copy-done, f32[512,256]{1,0:T(8,128)S(1)} %get-tuple-element.17.direct_ref, ...), custom_call_target="tpu_custom_call" | custom-call | flops 10000000 | bytes 3145728 | tf_op jit(solution)/shard_map/pallas_call | solution.py:106
  67.3 11.6 %all_to_all.43 = f32[16,16,128]{2,1,0:T(8,128)S(1)} all-to-all(f32[16,16,128]{2,1,0:T(8,128)S(1)} %bitcast.53), channel_id=1, replica_groups=mesh['dp'=4,'gx'=8,'gy'=16] {'gy'}, dimensions={0} | all-to-all | bytes 262144 | tf_op jit(solution)/shard_map/all_to_all | solution.py:520
  78.8 0.3 shard_map.92
  79.2 9.9 %all_to_all.44 = f32[8,16,128]{2,1,0:T(8,128)S(1)} all-to-all(f32[8,16,128]{2,1,0:T(8,128)S(1)} %bitcast.50), channel_id=1, replica_groups=mesh['dp'=4,'gx'=8,'gy'=16] {'gx'}, dimensions={0} | all-to-all | bytes 131072 | tf_op jit(solution)/shard_map/all_to_all | solution.py:520
  89.1 0.8 shard_map.93
  89.9 9.7 %all_to_all.45 = f32[8,16,128]{2,1,0:T(8,128)S(1)} all-to-all(f32[8,16,128]{2,1,0:T(8,128)S(1)} %bitcast.54), channel_id=1, replica_groups=mesh['dp'=4,'gx'=8,'gy'=16] {'gx'}, dimensions={0} | all-to-all | bytes 131072 | tf_op jit(solution)/shard_map/all_to_all | solution.py:520
  99.6 1.0 shard_map.94
  100.6 5.4 %all-to-all-start.7 = ((f32[16,16,128]{2,1,0:T(8,128)}), f32[16,16,128]{2,1,0:T(8,128)S(1)}, u32[]{:S(2)}, u32[]{:S(2)}) async-start(f32[16,16,128]{2,1,0:T(8,128)} %bitcast.27), calls=%async_computation.7 | async-start | bytes 262144 | tf_op jit(solution)/shard_map/all_to_all | solution.py:520
  105.9 3.1 %collective-permute-start = (f32[72,128]{1,0:T(8,128)S(1)}, f32[72,128]{1,0:T(8,128)S(1)}, u32[]{:S(2)}, u32[]{:S(2)}) collective-permute-start(f32[72,128]{1,0:T(8,128)S(1)} %get-tuple-element.26.mine_ref), channel_id=1, source_target_pairs={{0,128},{128,0},{256,384},{384,256},{1,129},{129,1},{257,385},{385... | collective-permute-start | bytes 110600 | tf_op jit(solution)/shard_map/ppermute | solution.py:543
  109.1 1.9 %collective-permute-done.other_ref = f32[72,128]{1,0:T(8,128)S(1)} collective-permute-done((f32[72,128]{1,0:T(8,128)S(1)}, f32[72,128]{1,0:T(8,128)S(1)}, u32[]{:S(2)}, u32[]{:S(2)}) %collective-permute-start) | collective-permute-done | bytes 36896 | tf_op jit(solution)/shard_map/ppermute | solution.py:543
  110.9 4.4 %collective-permute-start.1 = (f32[144,128]{1,0:T(8,128)S(1)}, f32[144,128]{1,0:T(8,128)S(1)}, u32[]{:S(2)}, u32[]{:S(2)}) collective-permute-start(f32[144,128]{1,0:T(8,128)S(1)} %shard_map.96.near_ref), channel_id=1, source_target_pairs={{0,384},{128,256},{256,128},{384,0},{1,385},{129,257},{257,129},{3... | collective-permute-start | bytes 221192 | tf_op jit(solution)/shard_map/ppermute | solution.py:545
  115.3 0.0 copy-done.6
  115.3 1.1 shard_map.91
  116.5 0.5 shard_map.97.sum_ref
  117.0 0.2 collective-permute-done.1.far_ref
  117.2 4.6 %shard_map.98 = f32[4320,20]{1,0:T(8,128)} custom-call(s32[1]{0:T(128)} %bitcast.7.odd_ref, f32[1280,128]{1,0:T(8,128)S(1)} %shard_map.97.sum_ref, f32[144,128]{1,0:T(8,128)S(1)} %collective-permute-done.1.far_ref), custom_call_target="tpu_custom_call" | custom-call | flops 10000000 | bytes 1074692 | tf_op jit(solution)/shard_map/pallas_call | solution.py:106
  121.8 0.0 all-to-all-done.7
  121.8 1.5 %shard_map.95 = f32[640,128]{1,0:T(8,128)} custom-call(f32[256,128]{1,0:T(8,128)S(1)} %bitcast.45, bf16[384,512]{1,0:T(8,128)(2,1)S(1)} %copy-done, f32[256,512]{1,0:T(8,128)S(1)} %get-tuple-element.25.direct_ref), custom_call_target="tpu_custom_call" | custom-call | flops 10000000 | bytes 1376256 | tf_op jit(solution)/shard_map/pallas_call | solution.py:106
  (1 shorter events, 0.0 us)
Async XLA Ops:
  3.1 62.6 %copy-start.3 = (bf16[512,384]{1,0:T(8,128)(2,1)S(1)}, bf16[512,384]{1,0:T(8,128)(2,1)}, u32[]{:S(2)}) copy-start(bf16[512,384]{1,0:T(8,128)(2,1)} %constant.13.clone.turned_ref) | copy-start | bytes 1179652
  24.9 40.8 %copy-start = (bf16[384,512]{1,0:T(8,128)(2,1)S(1)}, bf16[384,512]{1,0:T(8,128)(2,1)}, u32[]{:S(2)}) copy-start(bf16[384,512]{1,0:T(8,128)(2,1)} %constant.12.clone.table_hbm.table_ref) | copy-start | bytes 1179652
  24.9 14.1 %all-to-all-start.1 = ((f32[8,16,128]{2,1,0:T(8,128)}), f32[8,16,128]{2,1,0:T(8,128)S(1)}, u32[]{:S(2)}, u32[]{:S(2)}) async-start(f32[8,16,128]{2,1,0:T(8,128)} %bitcast.5), calls=%async_computation.1 | async-start | bytes 131072 | tf_op jit(solution)/shard_map/all_to_all | solution.py:520
  31.9 1.6 %copy-start.1 = (f32[2,9,1,12,20,20]{5,2,4,3,1,0:T(1,128)S(1)}, f32[2,9,1,12,20,20]{5,2,4,3,1,0:T(1,128)}, u32[]{:S(2)}) copy-start(f32[2,9,1,12,20,20]{5,2,4,3,1,0:T(1,128)} %param.8) | copy-start | bytes 1036804
  33.5 1.0 copy-start.2
  34.5 1.0 copy-start.4
  35.5 0.7 copy-start.5
  52.1 63.2 %copy-start.6 = (f32[20,20]{1,0:T(8,128)S(1)}, f32[20,20]{1,0:T(8,128)}, u32[]{:S(2)}) copy-start(f32[20,20]{1,0:T(8,128)} %map_ref.3) | copy-start | bytes 4804
  100.6 21.2 %all-to-all-start.7 = ((f32[16,16,128]{2,1,0:T(8,128)}), f32[16,16,128]{2,1,0:T(8,128)S(1)}, u32[]{:S(2)}, u32[]{:S(2)}) async-start(f32[16,16,128]{2,1,0:T(8,128)} %bitcast.27), calls=%async_computation.7 | async-start | bytes 262144 | tf_op jit(solution)/shard_map/all_to_all | solution.py:520
  105.9 5.0 %collective-permute-start = (f32[72,128]{1,0:T(8,128)S(1)}, f32[72,128]{1,0:T(8,128)S(1)}, u32[]{:S(2)}, u32[]{:S(2)}) collective-permute-start(f32[72,128]{1,0:T(8,128)S(1)} %get-tuple-element.26.mine_ref), channel_id=1, source_target_pairs={{0,128},{128,0},{256,384},{384,256},{1,129},{129,1},{257,385},{385... | collective-permute-start | bytes 110600 | tf_op jit(solution)/shard_map/ppermute | solution.py:543
  110.9 6.3 %collective-permute-start.1 = (f32[144,128]{1,0:T(8,128)S(1)}, f32[144,128]{1,0:T(8,128)S(1)}, u32[]{:S(2)}, u32[]{:S(2)}) collective-permute-start(f32[144,128]{1,0:T(8,128)S(1)} %shard_map.96.near_ref), channel_id=1, source_target_pairs={{0,384},{128,256},{256,128},{384,0},{1,385},{129,257},{257,129},{3... | collective-permute-start | bytes 221192 | tf_op jit(solution)/shard_map/ppermute | solution.py:545

commit v7 on v6

--- a/solution.py
+++ b/solution.py
@@ -388,30 +388,33 @@
                 sum_ref[at : at + KX, :] = found[part]
 
 
-def weight_grad(odd_ref, sum_ref, far_ref, grad_hbm, *scratch):
+def weight_grad(odd_ref, sum_ref, far_ref, grad_hbm, whole_ref, buffer_ref, sems):
     odd = odd_ref[0]
-    buffers, sems = scratch[:2], scratch[2]
     start = group_start()[:KX]
+    size = KX * C
     copies = []
     for tile in range(2):
-        buffer, pairs = buffers[tile], (6, 3)[tile]
         samples = list(share_parts(far_ref, tile))
-        rows = pairs * KX * C
         for c in range(C):
-            near = [sum_ref[packed_row(p, c, tile).start : packed_row(p, c, tile).start + KX, :] for p in range(2)]
-            real, imag = add_outer(samples, jnp.minimum(start + c, 127), *near)
-            for s in range(pairs):
-                buffer[weight_row(s, c), :] = real[:, 20 * s : 20 * s + C]
-                buffer[pl.ds(rows + s * (KX * C) + c, KX, stride=C), :] = imag[:, 20 * s : 20 * s + C]
-        first = (3 * odd if tile == 0 else 6 * (1 - odd)) * (KX * C)
-        for part in range(2):
-            copy = pltpu.make_async_copy(
-                buffer.at[pl.ds(part * rows, rows), :],
-                grad_hbm.at[pl.ds(pl.multiple_of(part * (9 * KX * C) + first, 8), rows), :],
-                sems.at[tile * 2 + part],
-            )
-            copy.start()
-            copies.append(copy)
+            at = [packed_row(part, c, tile).start for part in range(2)]
+            near = [sum_ref[k : k + KX, :] for k in at]
+            found = add_outer(samples, jnp.minimum(start + c, 127), *near)
+            for part in range(2):
+                whole_ref[at[part] : at[part] + KX, :] = found[part]
+        first = 3 * odd if tile == 0 else 6 * (1 - odd)
+        for s in range((6, 3)[tile]):
+            for part in range(2):
+                slot = (tile * 6 + s) * 2 + part
+                for c in range(C):
+                    k = packed_row(part, c, tile).start
+                    buffer_ref[pl.ds(slot * size + c, KX, stride=C), :] = whole_ref[k : k + KX, 20 * s : 20 * s + C]
+                copy = pltpu.make_async_copy(
+                    buffer_ref.at[pl.ds(slot * size, size), :],
+                    grad_hbm.at[pl.ds(pl.multiple_of((9 * part + first + s) * size, 8), size), :],
+                    sems.at[slot],
+                )
+                copy.start()
+                copies.append(copy)
     for copy in copies:
         copy.wait()
 
@@ -506,7 +509,7 @@
             weight_grad,
             [(2 * 9 * KX * C, C)],
             *(o, near, far),
-            scratch=[VMEM((2 * 6 * KX * C, C), F32), VMEM((2 * 3 * KX * C, C), F32), DMA((4,))],
+            scratch=[VMEM(PACKED, F32), VMEM((2 * 9 * KX * C, C), F32), DMA((18,))],
             smem=(0,),
             hbm_out=True,
         ),
@@ -540,9 +543,9 @@
     arrived = to_x(sent)
     sent = st["y_cells"](arrived)
     arrived = to_y(sent)
-    other = lax.ppermute(share, "dp", [(i, i ^ 1) for i in range(4)])
+    other = lax.ppermute(share, "dp", [(i, 3 - i) for i in range(4)])
     joined = st["join"](share, other)
-    rest = lax.ppermute(joined, "dp", [(i, 3 - i) for i in range(4)])
+    rest = lax.ppermute(joined, "dp", [(i, i ^ 1) for i in range(4)])
     half = st["near_sum"](joined)
     output, direct = st["emit"](bypass, signal, value)
     grad = st["weight_grad"](odd, half, rest)

time: 125 us -> 122 us (0.976)
  Pallas kernels: 17.1 us -> 14.6 us
    pallas_call x14, Pallas kernels: 17.1 us -> 14.6 us  [call(): pl.pallas_call(body, out_shape=shapes, in_specs=specs, out_specs=[pl.Bloc...]
  transfers between devices with their start and end apart: 4 -> 4, of which waited for: 3 -> 3; matrix products, arithmetic and copies ran while one was open for 0% -> 0% of each run, Pallas kernels for 6% -> 4%
where the time goes in v7:
time: 122 us; the launch traced here: 121 us
  blocking collectives  77.6 us (64%)
  starting transfers between devices  18.6 us (15%)
  Pallas kernels  14.6 us (12%)
  waiting for transfers between devices  5.01 us (4%)
  local copies, waits for them, and re-layouts  4.29 us (4%)
    all_to_all x6, blocking collectives, swap(): lax.all_to_all(a.reshape(n, rows, 128), axis, split_axis=0, concat_axis=0...  77.6 us
    pallas_call x14, Pallas kernels, call(): pl.pallas_call(body, out_shape=shapes, in_specs=specs, out_specs=[pl.Bloc...  14.6 us
    all_to_all x2, starting transfers between devices, swap(): lax.all_to_all(a.reshape(n, rows, 128), axis, split_axis=0, concat_axis=0...  12.3 us
    ppermute x1, starting transfers between devices, on_device(): other = lax.ppermute(share, 'dp', [(i, 3 - i) for i in range(4)])  4.37 us
    unnamed x14, local copies, waits for them, and re-layouts  4.29 us
  transfers between devices with their start and end apart: 4, of which 3 were waited for; matrix products, arithmetic and copies ran while one was open for 0% of the time, Pallas kernels for 4%

profile of v7, /device:TPU:1, one launch (start us, length us, event | category | flops | bytes accessed | tf_op | source)
XLA Modules:
  0.0 120.8 jit_solution(9536981380670391719)
XLA Ops:
  0.6 2.5 %shard_map.85 = f32[256,128]{1,0:T(8,128)} custom-call(f32[640,128]{1,0:T(8,128)} %bitcast.40, bf16[384,512]{1,0:T(8,128)(2,1)} %constant.12.clone.table_hbm.table_ref), custom_call_target="tpu_custom_call" | custom-call | flops 10000000 | bytes 851968 | tf_op jit(solution)/shard_map/pallas_call | solution.py:106
  3.1 0.0 copy-start.3
  3.1 20.8 %all_to_all.40 = f32[16,16,128]{2,1,0:T(8,128)S(1)} all-to-all(f32[16,16,128]{2,1,0:T(8,128)} %bitcast.57), channel_id=1, replica_groups=mesh['dp'=4,'gx'=8,'gy'=16] {'gy'}, dimensions={0} | all-to-all | bytes 262144 | tf_op jit(solution)/shard_map/all_to_all | solution.py:523
  24.0 1.0 shard_map.86
  24.9 0.0 copy-start
  24.9 7.0 %all-to-all-start.1 = ((f32[8,16,128]{2,1,0:T(8,128)}), f32[8,16,128]{2,1,0:T(8,128)S(1)}, u32[]{:S(2)}, u32[]{:S(2)}) async-start(f32[8,16,128]{2,1,0:T(8,128)} %bitcast.5), calls=%async_computation.1 | async-start | bytes 131072 | tf_op jit(solution)/shard_map/all_to_all | solution.py:523
  31.9 0.0 copy-start.1
  31.9 1.6 %copy-done.1 = f32[2,9,1,12,20,20]{5,2,4,3,1,0:T(1,128)S(1)} copy-done((f32[2,9,1,12,20,20]{5,2,4,3,1,0:T(1,128)S(1)}, f32[2,9,1,12,20,20]{5,2,4,3,1,0:T(1,128)}, u32[]{:S(2)}) %copy-start.1) | copy-done | bytes 345624
  33.5 0.0 copy-start.2
  33.5 1.0 copy-done.2
  34.5 0.0 copy-start.4
  34.5 1.0 copy-done.4
  35.5 0.0 copy-start.5
  35.5 0.7 copy-done.5
  36.2 1.2 shard_map.87
  37.3 1.7 %all-to-all-done.1 = f32[8,16,128]{2,1,0:T(8,128)S(1)} async-done(((f32[8,16,128]{2,1,0:T(8,128)}), f32[8,16,128]{2,1,0:T(8,128)S(1)}, u32[]{:S(2)}, u32[]{:S(2)}) %all-to-all-start.1) | async-done | bytes 65568 | tf_op jit(solution)/shard_map/all_to_all | solution.py:523
  39.0 0.8 shard_map.88
  39.8 12.0 %all_to_all.41 = f32[8,16,128]{2,1,0:T(8,128)S(1)} all-to-all(f32[8,16,128]{2,1,0:T(8,128)S(1)} %bitcast.55), channel_id=1, replica_groups=mesh['dp'=4,'gx'=8,'gy'=16] {'gx'}, dimensions={0} | all-to-all | bytes 131072 | tf_op jit(solution)/shard_map/all_to_all | solution.py:523
  51.8 0.3 shard_map.89
  52.1 0.0 copy-start.6
  52.1 13.5 %all_to_all.42 = f32[16,16,128]{2,1,0:T(8,128)S(1)} all-to-all(f32[16,16,128]{2,1,0:T(8,128)S(1)} %bitcast.43), channel_id=1, replica_groups=mesh['dp'=4,'gx'=8,'gy'=16] {'gy'}, dimensions={0} | all-to-all | bytes 262144 | tf_op jit(solution)/shard_map/all_to_all | solution.py:523
  65.7 0.0 copy-done.3
  65.7 0.0 copy-done
  65.7 1.6 %shard_map.90 = (f32[512,256]{1,0:T(8,128)S(1)}, f32[512,256]{1,0:T(8,128)S(1)}, f32[256,128]{1,0:T(8,128)S(1)}) custom-call(f32[256,128]{1,0:T(8,128)S(1)} %bitcast.46, bf16[512,384]{1,0:T(8,128)(2,1)S(1)} %copy-done.3, bf16[384,512]{1,0:T(8,128)(2,1)S(1)} %copy-done, f32[512,256]{1,0:T(8,128)S(1)} %get-tuple-element.17.direct_ref, ...), custom_call_target="tpu_custom_call" | custom-call | flops 10000000 | bytes 3145728 | tf_op jit(solution)/shard_map/pallas_call | solution.py:106
  67.3 11.6 %all_to_all.43 = f32[16,16,128]{2,1,0:T(8,128)S(1)} all-to-all(f32[16,16,128]{2,1,0:T(8,128)S(1)} %bitcast.53), channel_id=1, replica_groups=mesh['dp'=4,'gx'=8,'gy'=16] {'gy'}, dimensions={0} | all-to-all | bytes 262144 | tf_op jit(solution)/shard_map/all_to_all | solution.py:523
  78.8 0.3 shard_map.92
  79.2 9.9 %all_to_all.44 = f32[8,16,128]{2,1,0:T(8,128)S(1)} all-to-all(f32[8,16,128]{2,1,0:T(8,128)S(1)} %bitcast.50), channel_id=1, replica_groups=mesh['dp'=4,'gx'=8,'gy'=16] {'gx'}, dimensions={0} | all-to-all | bytes 131072 | tf_op jit(solution)/shard_map/all_to_all | solution.py:523
  89.1 0.8 shard_map.93
  89.9 9.7 %all_to_all.45 = f32[8,16,128]{2,1,0:T(8,128)S(1)} all-to-all(f32[8,16,128]{2,1,0:T(8,128)S(1)} %bitcast.54), channel_id=1, replica_groups=mesh['dp'=4,'gx'=8,'gy'=16] {'gx'}, dimensions={0} | all-to-all | bytes 131072 | tf_op jit(solution)/shard_map/all_to_all | solution.py:523
  99.6 1.0 shard_map.94
  100.6 5.4 %all-to-all-start.7 = ((f32[16,16,128]{2,1,0:T(8,128)}), f32[16,16,128]{2,1,0:T(8,128)S(1)}, u32[]{:S(2)}, u32[]{:S(2)}) async-start(f32[16,16,128]{2,1,0:T(8,128)} %bitcast.27), calls=%async_computation.7 | async-start | bytes 262144 | tf_op jit(solution)/shard_map/all_to_all | solution.py:523
  105.9 4.4 %collective-permute-start = (f32[72,128]{1,0:T(8,128)S(1)}, f32[72,128]{1,0:T(8,128)S(1)}, u32[]{:S(2)}, u32[]{:S(2)}) collective-permute-start(f32[72,128]{1,0:T(8,128)S(1)} %get-tuple-element.26.mine_ref), channel_id=1, source_target_pairs={{0,384},{128,256},{256,128},{384,0},{1,385},{129,257},{257,129},{3... | collective-permute-start | bytes 110600 | tf_op jit(solution)/shard_map/ppermute | solution.py:546
  110.3 1.8 %collective-permute-done.other_ref = f32[72,128]{1,0:T(8,128)S(1)} collective-permute-done((f32[72,128]{1,0:T(8,128)S(1)}, f32[72,128]{1,0:T(8,128)S(1)}, u32[]{:S(2)}, u32[]{:S(2)}) %collective-permute-start) | collective-permute-done | bytes 36896 | tf_op jit(solution)/shard_map/ppermute | solution.py:546
  112.2 1.9 %collective-permute-start.1 = (f32[144,128]{1,0:T(8,128)S(1)}, f32[144,128]{1,0:T(8,128)S(1)}, u32[]{:S(2)}, u32[]{:S(2)}) collective-permute-start(f32[144,128]{1,0:T(8,128)S(1)} %shard_map.96.near_ref), channel_id=1, source_target_pairs={{0,128},{128,0},{256,384},{384,256},{1,129},{129,1},{257,385},{385... | collective-permute-start | bytes 221192 | tf_op jit(solution)/shard_map/ppermute | solution.py:548
  114.1 0.0 copy-done.6
  114.1 1.1 shard_map.91
  115.2 0.5 shard_map.97.sum_ref
  115.8 1.5 %collective-permute-done.1.far_ref = f32[144,128]{1,0:T(8,128)S(1)} collective-permute-done((f32[144,128]{1,0:T(8,128)S(1)}, f32[144,128]{1,0:T(8,128)S(1)}, u32[]{:S(2)}, u32[]{:S(2)}) %collective-permute-start.1) | collective-permute-done | bytes 73760 | tf_op jit(solution)/shard_map/ppermute | solution.py:548
  117.2 2.1 %shard_map.98 = f32[4320,20]{1,0:T(8,128)} custom-call(s32[1]{0:T(128)} %bitcast.7.odd_ref, f32[1280,128]{1,0:T(8,128)S(1)} %shard_map.97.sum_ref, f32[144,128]{1,0:T(8,128)S(1)} %collective-permute-done.1.far_ref), custom_call_target="tpu_custom_call" | custom-call | flops 10000000 | bytes 1074692 | tf_op jit(solution)/shard_map/pallas_call | solution.py:106
  119.3 0.0 all-to-all-done.7
  119.3 1.5 %shard_map.95 = f32[640,128]{1,0:T(8,128)} custom-call(f32[256,128]{1,0:T(8,128)S(1)} %bitcast.45, bf16[384,512]{1,0:T(8,128)(2,1)S(1)} %copy-done, f32[256,512]{1,0:T(8,128)S(1)} %get-tuple-element.25.direct_ref), custom_call_target="tpu_custom_call" | custom-call | flops 10000000 | bytes 1376256 | tf_op jit(solution)/shard_map/pallas_call | solution.py:106
  (1 shorter events, 0.0 us)
Async XLA Ops:
  3.1 62.6 %copy-start.3 = (bf16[512,384]{1,0:T(8,128)(2,1)S(1)}, bf16[512,384]{1,0:T(8,128)(2,1)}, u32[]{:S(2)}) copy-start(bf16[512,384]{1,0:T(8,128)(2,1)} %constant.13.clone.turned_ref) | copy-start | bytes 1179652
  24.9 40.8 %copy-start = (bf16[384,512]{1,0:T(8,128)(2,1)S(1)}, bf16[384,512]{1,0:T(8,128)(2,1)}, u32[]{:S(2)}) copy-start(bf16[384,512]{1,0:T(8,128)(2,1)} %constant.12.clone.table_hbm.table_ref) | copy-start | bytes 1179652
  24.9 14.1 %all-to-all-start.1 = ((f32[8,16,128]{2,1,0:T(8,128)}), f32[8,16,128]{2,1,0:T(8,128)S(1)}, u32[]{:S(2)}, u32[]{:S(2)}) async-start(f32[8,16,128]{2,1,0:T(8,128)} %bitcast.5), calls=%async_computation.1 | async-start | bytes 131072 | tf_op jit(solution)/shard_map/all_to_all | solution.py:523
  31.9 1.6 %copy-start.1 = (f32[2,9,1,12,20,20]{5,2,4,3,1,0:T(1,128)S(1)}, f32[2,9,1,12,20,20]{5,2,4,3,1,0:T(1,128)}, u32[]{:S(2)}) copy-start(f32[2,9,1,12,20,20]{5,2,4,3,1,0:T(1,128)} %param.8) | copy-start | bytes 1036804
  33.5 1.0 copy-start.2
  34.5 1.0 copy-start.4
  35.5 0.7 copy-start.5
  52.1 62.0 %copy-start.6 = (f32[20,20]{1,0:T(8,128)S(1)}, f32[20,20]{1,0:T(8,128)}, u32[]{:S(2)}) copy-start(f32[20,20]{1,0:T(8,128)} %map_ref.3) | copy-start | bytes 4804
  100.6 18.8 %all-to-all-start.7 = ((f32[16,16,128]{2,1,0:T(8,128)}), f32[16,16,128]{2,1,0:T(8,128)S(1)}, u32[]{:S(2)}, u32[]{:S(2)}) async-start(f32[16,16,128]{2,1,0:T(8,128)} %bitcast.27), calls=%async_computation.7 | async-start | bytes 262144 | tf_op jit(solution)/shard_map/all_to_all | solution.py:523
  105.9 6.2 %collective-permute-start = (f32[72,128]{1,0:T(8,128)S(1)}, f32[72,128]{1,0:T(8,128)S(1)}, u32[]{:S(2)}, u32[]{:S(2)}) collective-permute-start(f32[72,128]{1,0:T(8,128)S(1)} %get-tuple-element.26.mine_ref), channel_id=1, source_target_pairs={{0,384},{128,256},{256,128},{384,0},{1,385},{129,257},{257,129},{3... | collective-permute-start | bytes 110600 | tf_op jit(solution)/shard_map/ppermute | solution.py:546
  112.2 5.1 %collective-permute-start.1 = (f32[144,128]{1,0:T(8,128)S(1)}, f32[144,128]{1,0:T(8,128)S(1)}, u32[]{:S(2)}, u32[]{:S(2)}) collective-permute-start(f32[144,128]{1,0:T(8,128)S(1)} %shard_map.96.near_ref), channel_id=1, source_target_pairs={{0,128},{128,0},{256,384},{384,256},{1,129},{129,1},{257,385},{385... | collective-permute-start | bytes 221192 | tf_op jit(solution)/shard_map/ppermute | solution.py:548
